TPU v7x, 32 devices: a whole 2x2x4 slice. The times are simulated.
32 devices in a mesh: expert: 8 (over z, y), batch: 4 (over x, core).
Axes of the slice: x: 2, y: 2, z: 4, core: 2. Of those that a mesh axis runs over, the one named last changes fastest.
Arguments:
- tokens: bfloat16 [8192, 1024], P(('expert', 'batch')), may hold values from -6 to 6
- routes: int32 [8192, 1], P(('expert', 'batch')), may hold values from 0 to 7; in each aligned block of 256 rows (0 to 255, 256 to 511, ...) at most 64 rows name the same one
- centroid: bfloat16 [8, 1024], P('expert'), may hold values from -0.1875 to 0.1875
- ln_gain: bfloat16 [8, 1024], P('expert'), may hold values from 0.099609375 to 1.8984375
- ln_bias: bfloat16 [8, 1024], P('expert'), may hold values from -3 to 3
- w_in: bfloat16 [8, 1024, 4096], P('expert', None, 'batch'), may hold values from -0.1875 to 0.1875
- b_in: bfloat16 [8, 4096], P('expert', 'batch'), may hold values from -3 to 3
- w_out: bfloat16 [8, 4096, 1024], P('expert', 'batch'), may hold values from -0.09375 to 0.09375
- b_out: bfloat16 [8, 1024], P('expert'), may hold values from -3 to 3
- cotangent: bfloat16 [8192, 1024], P(('expert', 'batch')), may hold values from -6 to 6
Outputs:
- mixed: bfloat16 [8192, 1024], P(('expert', 'batch'))
- tokens_grad: float32 [8192, 1024], P(('expert', 'batch'))
- centroid_grad: float32 [8, 1024], P('expert')
- gain_grad: float32 [8, 1024], P('expert')
- bias_grad: float32 [8, 1024], P('expert')
- w_in_grad: float32 [8, 1024, 4096], P('expert', None, 'batch')
- b_in_grad: float32 [8, 4096], P('expert', 'batch')
- w_out_grad: float32 [8, 4096, 1024], P('expert', 'batch')
- b_out_grad: float32 [8, 1024], P('expert')
Inputs may be any that keep to these rules, and one draw needn't show every extreme that they name: `routes`: in each aligned block of 256 rows (one device's tokens) no expert is named more than 64 times, a bound that some block reaches.
All inputs are finite; a program needn't handle non-finite values.
Results may differ from a plain program's by a relative error of at most 0.0062.
Values may be sent and summed in bfloat16 or wider, within the bound.
No kernel may reach another device: no remote copies, remote signals or barrier semaphores. Data moves between devices by JAX's collectives and lax.ppermute only.
A program may use at most 128 MiB of HBM per device.

v0:
```python
import jax
import jax.numpy as jnp
from jax import lax
from jax.sharding import PartitionSpec as P

epsilon = 1e-05
root_half = 0.7071067811865476
gauss_norm = 0.3989422804014327


def gelu_parts(pre_act):
    gelu_value = jax.nn.gelu(pre_act, approximate=False)
    gelu_slope = (
        0.5 * (1.0 + lax.erf(pre_act * root_half))
        + pre_act * jnp.exp(-0.5 * pre_act * pre_act) * gauss_norm
    )
    return (gelu_value.astype(jnp.bfloat16), gelu_slope)


def contract_first(left, right):
    return lax.dot_general(
        left, right, (((0,), (0,)), ((), ())), preferred_element_type=jnp.float32
    )


def contract_last(left, right):
    return lax.dot_general(
        left, right, (((1,), (1,)), ((), ())), preferred_element_type=jnp.float32
    )


def local(tokens, routes, centroid, ln_gain, ln_bias, w_in, b_in, w_out, b_out, cotangent):
    experts = lax.axis_size("expert")
    tok_count = tokens.shape[0]
    model_width = tokens.shape[1]
    capacity = max(2, 2 * tok_count // experts)
    row_count = experts * capacity
    route_ids = routes[:, 0]
    onehot = (route_ids[:, None] == jnp.arange(experts, dtype=jnp.int32)[None, :]).astype(jnp.int32)
    before = jnp.cumsum(onehot, axis=0) - onehot
    rank_in = jnp.sum(before * onehot, axis=1)
    target = route_ids * capacity + rank_in
    placing = (jnp.arange(row_count, dtype=jnp.int32)[:, None] == target[None, :]).astype(
        jnp.bfloat16
    )
    outgoing = jnp.dot(placing, tokens, preferred_element_type=jnp.float32).astype(jnp.bfloat16)
    arrived = lax.all_to_all(
        outgoing.reshape(experts, capacity, model_width),
        "expert",
        split_axis=0,
        concat_axis=0,
        tiled=True,
    )
    arrived = arrived.reshape(row_count, model_width)
    hidden_in = arrived.astype(jnp.float32)
    center = jnp.mean(hidden_in, axis=1, keepdims=True)
    spread = jnp.mean((hidden_in - center) * (hidden_in - center), axis=1, keepdims=True)
    inv_std = lax.rsqrt(spread + epsilon)
    normed = (hidden_in - center) * inv_std
    gain_row = ln_gain[0].astype(jnp.float32)
    shift_row = ln_bias[0].astype(jnp.float32)
    cent_row = centroid[0].astype(jnp.float32)
    b_last = b_out[0].astype(jnp.float32)
    lowered = (normed * gain_row + shift_row).astype(jnp.bfloat16)
    gate_logit = jnp.dot(arrived, centroid[0], preferred_element_type=jnp.float32)
    mixing = jax.nn.sigmoid(gate_logit)
    w_first = w_in[0]
    w_second = w_out[0]
    b_first = b_in[0].astype(jnp.float32)
    inputs_all = lax.all_gather(lowered, "batch", axis=0, tiled=True)
    row_piece = inputs_all
    piece_act, unused = gelu_parts(
        jnp.dot(row_piece, w_first, preferred_element_type=jnp.float32) + b_first
    )
    branch = (
        lax.psum_scatter(
            jnp.dot(piece_act, w_second, preferred_element_type=jnp.float32).astype(jnp.bfloat16),
            "batch",
            scatter_dimension=0,
            tiled=True,
        ).astype(jnp.float32)
        + b_last
    )
    expert_out = hidden_in + branch
    reply_rows = (mixing[:, None] * expert_out).astype(jnp.bfloat16)
    returned = lax.all_to_all(
        reply_rows.reshape(experts, capacity, model_width),
        "expert",
        split_axis=0,
        concat_axis=0,
        tiled=True,
    )
    returned = returned.reshape(row_count, model_width)
    mixed = (tokens.astype(jnp.float32) + contract_first(placing, returned)).astype(jnp.bfloat16)
    grad_out = jnp.dot(placing, cotangent, preferred_element_type=jnp.float32).astype(jnp.bfloat16)
    grad_rows = lax.all_to_all(
        grad_out.reshape(experts, capacity, model_width),
        "expert",
        split_axis=0,
        concat_axis=0,
        tiled=True,
    )
    grad_rows = grad_rows.reshape(row_count, model_width).astype(jnp.float32)
    gate_grad = jnp.sum(grad_rows * expert_out, axis=1) * mixing * (1.0 - mixing)
    direct = grad_rows * mixing[:, None]
    branch_grad = direct.astype(jnp.bfloat16)
    b_out_part = jnp.sum(branch_grad.astype(jnp.float32), axis=0)
    centroid_part = jnp.sum(gate_grad[:, None] * hidden_in, axis=0)
    grads_all = lax.all_gather(branch_grad, "batch", axis=0, tiled=True)
    activated, gelu_slope = gelu_parts(
        jnp.dot(inputs_all, w_first, preferred_element_type=jnp.float32) + b_first
    )
    pre_grad = (contract_last(grads_all, w_second) * gelu_slope).astype(jnp.bfloat16)
    w_out_grad = contract_first(activated, grads_all)
    w_in_grad = contract_first(inputs_all, pre_grad)
    b_in_grad = jnp.sum(pre_grad.astype(jnp.float32), axis=0)
    row_piece = pre_grad
    normed_grad = lax.psum_scatter(
        contract_last(row_piece, w_first), "batch", scatter_dimension=0, tiled=True
    )
    gain_part = jnp.sum(normed_grad * normed, axis=0)
    bias_part = jnp.sum(normed_grad, axis=0)
    scaled = normed_grad * gain_row
    ln_grad = inv_std * (
        scaled
        - jnp.mean(scaled, axis=1, keepdims=True)
        - normed * jnp.mean(scaled * normed, axis=1, keepdims=True)
    )
    input_grad = direct + gate_grad[:, None] * cent_row + ln_grad
    outgoing_grads = input_grad.astype(jnp.bfloat16).reshape(experts, capacity, model_width)
    arrived_grads = lax.all_to_all(
        outgoing_grads, "expert", split_axis=0, concat_axis=0, tiled=True
    ).reshape(row_count, model_width)
    tokens_grad = cotangent.astype(jnp.float32) + contract_first(placing, arrived_grads)
    small_sums = lax.psum((centroid_part, gain_part, bias_part, b_out_part), "batch")
    return (
        mixed,
        tokens_grad,
        small_sums[0][None],
        small_sums[1][None],
        small_sums[2][None],
        w_in_grad[None],
        b_in_grad[None],
        w_out_grad[None],
        small_sums[3][None],
    )


def solution(mesh):
    in_specs = (
        P(("expert", "batch"), None),
        P(("expert", "batch"), None),
        P("expert", None),
        P("expert", None),
        P("expert", None),
        P("expert", None, "batch"),
        P("expert", "batch"),
        P("expert", "batch", None),
        P("expert", None),
        P(("expert", "batch"), None),
    )
    out_specs = (
        P(("expert", "batch"), None),
        P(("expert", "batch"), None),
        P("expert", None),
        P("expert", None),
        P("expert", None),
        P("expert", None, "batch"),
        P("expert", "batch"),
        P("expert", "batch", None),
        P("expert", None),
    )
    return jax.shard_map(local, mesh=mesh, in_specs=in_specs, out_specs=out_specs, check_vma=False)
```

profile of v0, /device:TPU:8, one launch (start us, length us, event | category | flops | bytes accessed | tf_op | source)
XLA Modules:
  0.0 321.9 jit_solution(5663673363300654412)
XLA Ops:
  7.2 0.8 fusion.49
  8.8 0.8 fusion.48
  10.3 2.5 convolution_convert_fusion.2
  12.8 6.3 %all-to-all-start = ((bf16[8,64,1024]{2,1,0:T(8,128)(2,1)}), bf16[8,64,1024]{2,1,0:T(8,128)(2,1)S(1)}, u32[]{:S(2)}, u32[]{:S(2)}) async-start(bf16[8,64,1024]{2,1,0:T(8,128)(2,1)} %bitcast.80), calls=%async_computation | async-start | bytes 2097152 | tf_op jit(solution)/shard_map/all_to_all | solution.py:47
  19.0 0.7 mul.204
  20.4 22.0 %all-to-all-done = bf16[8,64,1024]{2,1,0:T(8,128)(2,1)S(1)} async-done(((bf16[8,64,1024]{2,1,0:T(8,128)(2,1)}), bf16[8,64,1024]{2,1,0:T(8,128)(2,1)S(1)}, u32[]{:S(2)}, u32[]{:S(2)}) %all-to-all-start) | async-done | bytes 1048608 | tf_op jit(solution)/shard_map/all_to_all | solution.py:47
  43.3 1.4 fusion.22
  44.7 2.5 convolution_convert_fusion.1
  47.2 6.5 %all-to-all-start.2 = ((bf16[8,64,1024]{2,1,0:T(8,128)(2,1)}), bf16[8,64,1024]{2,1,0:T(8,128)(2,1)}, u32[]{:S(2)}, u32[]{:S(2)}) async-start(bf16[8,64,1024]{2,1,0:T(8,128)(2,1)} %bitcast.79), calls=%async_computation.3 | async-start | bytes 2097152 | tf_op jit(solution)/shard_map/all_to_all | solution.py:96
  54.1 22.7 %all-to-all-done.2 = bf16[8,64,1024]{2,1,0:T(8,128)(2,1)} async-done(((bf16[8,64,1024]{2,1,0:T(8,128)(2,1)}), bf16[8,64,1024]{2,1,0:T(8,128)(2,1)}, u32[]{:S(2)}, u32[]{:S(2)}) %all-to-all-start.2) | async-done | bytes 1048608 | tf_op jit(solution)/shard_map/all_to_all | solution.py:96
  76.8 2.4 fusion.32
  79.4 0.8 all-gather.3.cloned.1.call-done
  80.2 25.0 %fusion.2 = (bf16[2048,1024]{1,0:T(8,128)(2,1)S(1)}, f32[2048,1024]{1,0:T(8,128)}) fusion(f32[1024]{0:T(1024)S(1)} %bitcast.97, bf16[2048,1024]{1,0:T(8,128)(2,1)} %all-gather.3.cloned.1.call-done, bf16[1,1024,1024]{2,1,0:T(8,128)(2,1)S(1)} %copy-done), kind=kOutput, calls=%fused_computation.4 | convolution fusion | flops 4433379328 | bytes 18878464 | tf_op jit(solution)/shard_map/dot_general | solution.py:73
  105.2 1.9 copy-done.7
  107.1 6.0 %convolution_convert_fusion = bf16[2048,1024]{1,0:T(8,128)(2,1)} fusion(bf16[2048,1024]{1,0:T(8,128)(2,1)S(1)} %get-tuple-element.19, bf16[1,1024,1024]{2,1,0:T(8,128)(2,1)S(1)} %copy-done.6), kind=kOutput, calls=%fused_computation.27 | convolution fusion | flops 4297064448 | bytes 10485760 | tf_op jit(solution)/shard_map/dot_general | solution.py:77
  113.4 3.5 %all-gather.5.cloned.1.call-done = bf16[2048,1024]{1,0:T(8,128)(2,1)} async-done(((bf16[512,1024]{1,0:T(8,128)(2,1)}), bf16[2048,1024]{1,0:T(8,128)(2,1)}) %all-gather.5.cloned.1.call-update) | async-done | bytes 4194320 | tf_op jit(solution)/shard_map/all_gather | solution.py:109
  116.8 11.9 %convert_reduce_fusion = (f32[1024]{0:T(1024)}, bf16[2048,1024]{1,0:T(8,128)(2,1)S(1)}) fusion(f32[2048,1024]{1,0:T(8,128)} %get-tuple-element.20, f32[1024]{0:T(1024)S(1)} %bitcast.98, bf16[2048,1024]{1,0:T(8,128)(2,1)} %all-gather.5.cloned.1.call-done, bf16[1,1024,1024]{2,1,0:T(8,128)(2,1)} %param.17), kind=kOutput, calls=%fused_computation.11 | convolution fusion | flops 4322229248 | bytes 18882560 | tf_op jit(solution)/shard_map/dot_general | solution.py:27
  128.7 2.0 copy-done.9
  130.7 7.0 %fusion.38 = f32[2048,1024]{1,0:T(8,128)} fusion(bf16[2048,1024]{1,0:T(8,128)(2,1)S(1)} %get-tuple-element.22, bf16[1,1024,1024]{2,1,0:T(8,128)(2,1)S(1)} %copy-done), kind=kOutput, calls=%fused_computation.60 | convolution fusion | flops 4294967296 | bytes 14680064 | tf_op jit(solution)/shard_map/dot_general | solution.py:27
  138.4 26.1 %reduce-scatter.3.cloned.1.call-done = bf16[512,1024]{1,0:T(8,128)(2,1)} async-done(((bf16[2048,1024]{1,0:T(8,128)(2,1)}), bf16[512,1024]{1,0:T(8,128)(2,1)}) %reduce-scatter.3.cloned.1.call-update) | async-done | bytes 1048592 | tf_op jit(solution)/shard_map/reduce_scatter | solution.py:76
  164.5 74.4 %reduce-scatter.5.cloned.1.call-done = f32[512,1024]{1,0:T(8,128)} async-done(((f32[2048,1024]{1,0:T(8,128)}), f32[512,1024]{1,0:T(8,128)}) %reduce-scatter.5.cloned.1.call-update) | async-done | bytes 2097168 | tf_op jit(solution)/shard_map/reduce_scatter | solution.py:118
  238.9 4.2 %fusion.28 = (f32[1024]{0:T(1024)S(1)}, f32[512]{0:T(512)S(1)}, f32[512]{0:T(512)S(1)}, f32[1024]{0:T(1024)S(1)}, f32[512]{0:T(512)S(1)}, /*index=5*/bf16[512,1024]{1,0:T(8,128)(2,1)}) fusion(f32[512,1024]{1,0:T(8,128)} %reduce-scatter.5.cloned.1.call-done, f32[512]{0:T(512)S(1)} %rsqrt.12, f32[512]{0:T(512)S(1)} %div.19, ...), kind=kLoop, calls=%fused_computation.47 | loop fusion | flops 9433600 | bytes 6320128 | tf_op jit(solution)/shard_map/reduce_sum | solution.py:121
  243.1 3.0 fusion.27
  246.1 6.1 %all-to-all-start.3 = ((bf16[8,64,1024]{2,1,0:T(8,128)(2,1)}), bf16[8,64,1024]{2,1,0:T(8,128)(2,1)}, u32[]{:S(2)}, u32[]{:S(2)}) async-start(bf16[8,64,1024]{2,1,0:T(8,128)(2,1)} %bitcast.82), calls=%async_computation.5 | async-start | bytes 2097152 | tf_op jit(solution)/shard_map/all_to_all | solution.py:131
  252.2 1.5 convert_reduce_fusion.2
  253.7 21.9 %all-to-all-done.3 = bf16[8,64,1024]{2,1,0:T(8,128)(2,1)} async-done(((bf16[8,64,1024]{2,1,0:T(8,128)(2,1)}), bf16[8,64,1024]{2,1,0:T(8,128)(2,1)}, u32[]{:S(2)}, u32[]{:S(2)}) %all-to-all-start.3) | async-done | bytes 1048608 | tf_op jit(solution)/shard_map/all_to_all | solution.py:131
  275.7 6.5 %all-to-all-start.1 = ((bf16[8,64,1024]{2,1,0:T(8,128)(2,1)}), bf16[8,64,1024]{2,1,0:T(8,128)(2,1)}, u32[]{:S(2)}, u32[]{:S(2)}) async-start(bf16[8,64,1024]{2,1,0:T(8,128)(2,1)} %bitcast.81), calls=%async_computation.2 | async-start | bytes 2097152 | tf_op jit(solution)/shard_map/all_to_all | solution.py:86
  282.1 10.2 %convolution_bitcast_fusion.1 = f32[1,1024,1024]{2,1,0:T(8,128)} fusion(bf16[2048,1024]{1,0:T(8,128)(2,1)} %all-gather.3.cloned.1.call-done, bf16[2048,1024]{1,0:T(8,128)(2,1)} %copy-done.9), kind=kOutput, calls=%fused_computation.34 | convolution fusion | flops 4294967296 | bytes 12582912 | tf_op jit(solution)/shard_map/dot_general | solution.py:21
  292.3 6.1 %convolution_bitcast_fusion = f32[1,1024,1024]{2,1,0:T(8,128)} fusion(bf16[2048,1024]{1,0:T(8,128)(2,1)S(1)} %copy-done.8, bf16[2048,1024]{1,0:T(8,128)(2,1)S(1)} %copy-done.5), kind=kOutput, calls=%fused_computation.33 | convolution fusion | flops 4294967296 | bytes 12582912 | tf_op jit(solution)/shard_map/dot_general | solution.py:21
  298.8 11.1 %all-reduce = (f32[1,1024]{1,0:T(1,128)}, f32[1,1024]{1,0:T(1,128)}, f32[1,1024]{1,0:T(1,128)}, f32[1,1024]{1,0:T(1,128)}) all-reduce(f32[1,1024]{1,0:T(1,128)S(1)} %bitcast.90, f32[1,1024]{1,0:T(1,128)S(1)} %bitcast.92, f32[1,1024]{1,0:T(1,128)S(1)} %bitcast.93, ...), channel_id=1, replica_groups=mesh['expert'=8,'batch'=4] {'batch'}, use_global_device_ids=true, to_apply=%region_11.12 | all-reduce | flops 4096 | bytes 32768 | tf_op jit(solution)/shard_map/psum | solution.py:135
  309.9 2.8 convolution_add_fusion
  312.7 2.6 fusion.42
  (50 shorter events, 4.8 us)
Async XLA Ops:
  7.2 73.0 %copy-start = (bf16[1,1024,1024]{2,1,0:T(8,128)(2,1)S(1)}, bf16[1,1024,1024]{2,1,0:T(8,128)(2,1)}, u32[]{:S(2)}) copy-start(bf16[1,1024,1024]{2,1,0:T(8,128)(2,1)} %param.15) | copy-start | bytes 6291460
  12.8 29.7 %all-to-all-start = ((bf16[8,64,1024]{2,1,0:T(8,128)(2,1)}), bf16[8,64,1024]{2,1,0:T(8,128)(2,1)S(1)}, u32[]{:S(2)}, u32[]{:S(2)}) async-start(bf16[8,64,1024]{2,1,0:T(8,128)(2,1)} %bitcast.80), calls=%async_computation | async-start | bytes 2097152 | tf_op jit(solution)/shard_map/all_to_all | solution.py:47
  19.0 61.2 %all-gather.3.cloned.1.call-start = ((), (), s32[]{:S(2)}) async-start(), calls=%async_computation.6 | async-start | bytes 5242880 | tf_op jit(solution)/shard_map/all_gather | solution.py:70
  42.7 11.0 %copy-start.3 = (bf16[1,1024]{1,0:T(2,128)(2,1)S(1)}, bf16[1,1024]{1,0:T(2,128)(2,1)}, u32[]{:S(2)}) copy-start(bf16[1,1024]{1,0:T(2,128)(2,1)} %param.16) | copy-start | bytes 6148
  42.7 11.0 %copy-start.2 = (bf16[1,1024]{1,0:T(2,128)(2,1)S(1)}, bf16[1,1024]{1,0:T(2,128)(2,1)}, u32[]{:S(2)}) copy-start(bf16[1,1024]{1,0:T(2,128)(2,1)} %param.12) | copy-start | bytes 6148
  47.2 29.7 %all-to-all-start.2 = ((bf16[8,64,1024]{2,1,0:T(8,128)(2,1)}), bf16[8,64,1024]{2,1,0:T(8,128)(2,1)}, u32[]{:S(2)}, u32[]{:S(2)}) async-start(bf16[8,64,1024]{2,1,0:T(8,128)(2,1)} %bitcast.79), calls=%async_computation.3 | async-start | bytes 2097152 | tf_op jit(solution)/shard_map/all_to_all | solution.py:96
  53.7 63.1 %all-gather.5.cloned.1.call-start = ((), (), s32[]{:S(2)}) async-start(), calls=%async_computation.8 | async-start | bytes 5242880 | tf_op jit(solution)/shard_map/all_gather | solution.py:109
  79.3 85.2 %reduce-scatter.3.cloned.1.call-start = ((), (), s32[]{:S(2)}) async-start(), calls=%async_computation.7 | async-start | bytes 5242880 | tf_op jit(solution)/shard_map/reduce_scatter | solution.py:76
  80.2 26.9 %copy-start.6 = (bf16[1,1024,1024]{2,1,0:T(8,128)(2,1)S(1)}, bf16[1,1024,1024]{2,1,0:T(8,128)(2,1)}, u32[]{:S(2)}) copy-start(bf16[1,1024,1024]{2,1,0:T(8,128)(2,1)} %param.17) | copy-start | bytes 6291460
  105.2 1.9 copy-start.7
  113.2 125.7 %reduce-scatter.5.cloned.1.call-start = ((), (), s32[]{:S(2)}) async-start(), calls=%async_computation.9 | async-start | bytes 10485760 | tf_op jit(solution)/shard_map/reduce_scatter | solution.py:118
  128.7 2.0 copy-start.9
  137.7 0.7 copy-start.4
  238.9 4.2 %copy-start.1 = (f32[512,1024]{1,0:T(8,128)S(1)}, f32[512,1024]{1,0:T(8,128)}, u32[]{:S(2)}) copy-start(f32[512,1024]{1,0:T(8,128)} %reduce-scatter.5.cloned.1.call-done) | copy-start | bytes 6291460
  246.1 29.6 %all-to-all-start.3 = ((bf16[8,64,1024]{2,1,0:T(8,128)(2,1)}), bf16[8,64,1024]{2,1,0:T(8,128)(2,1)}, u32[]{:S(2)}, u32[]{:S(2)}) async-start(bf16[8,64,1024]{2,1,0:T(8,128)(2,1)} %bitcast.82), calls=%async_computation.5 | async-start | bytes 2097152 | tf_op jit(solution)/shard_map/all_to_all | solution.py:131
  275.7 37.1 %all-to-all-start.1 = ((bf16[8,64,1024]{2,1,0:T(8,128)(2,1)}), bf16[8,64,1024]{2,1,0:T(8,128)(2,1)}, u32[]{:S(2)}, u32[]{:S(2)}) async-start(bf16[8,64,1024]{2,1,0:T(8,128)(2,1)} %bitcast.81), calls=%async_computation.2 | async-start | bytes 2097152 | tf_op jit(solution)/shard_map/all_to_all | solution.py:86
  282.1 10.2 %copy-start.5 = (bf16[2048,1024]{1,0:T(8,128)(2,1)S(1)}, bf16[2048,1024]{1,0:T(8,128)(2,1)}, u32[]{:S(2)}) copy-start(bf16[2048,1024]{1,0:T(8,128)(2,1)} %all-gather.5.cloned.1.call-done) | copy-start | bytes 12582916
  282.1 10.2 %copy-start.8 = (bf16[2048,1024]{1,0:T(8,128)(2,1)S(1)}, bf16[2048,1024]{1,0:T(8,128)(2,1)}, u32[]{:S(2)}) copy-start(bf16[2048,1024]{1,0:T(8,128)(2,1)} %copy-done.7) | copy-start | bytes 12582916
Sparse Core Ops, SparseCore 0:
  44.8 35.2 all-gather.2
  82.3 34.4 all-gather.4
  119.9 44.5 reduce-scatter.2
  167.1 71.6 reduce-scatter.4
where the time goes:
time: 324 us; the launch traced here: 322 us
  waiting for transfers between devices  172 us (53%)
  matrix products  76.9 us (24%)
  starting transfers between devices  25.6 us (8%)
  other arithmetic  17.8 us (5%)
  between operations  13.9 us (4%)
  blocking collectives  11.1 us (3%)
  local copies, waits for them, and re-layouts  5.07 us (2%)
    reduce_scatter x1, waiting for transfers between devices, local(): lax.psum_scatter(contract_last(row_piece, w_first), 'batch', scatter_dime...  74.4 us
    reduce_scatter x1, waiting for transfers between devices, local(): lax.psum_scatter(jnp.dot(piece_act, w_second, preferred_element_type=jnp....  26.1 us
    dot_general x1, matrix products, local(): jnp.dot(row_piece, w_first, preferred_element_type=jnp.float32) + b_first  25 us
    all_to_all x1, waiting for transfers between devices, local(): lax.all_to_all(grad_out.reshape(experts, capacity, model_width), 'expert'...  22.7 us
    all_to_all x1, waiting for transfers between devices, local(): lax.all_to_all(outgoing.reshape(experts, capacity, model_width), 'expert'...  22 us
    all_to_all x1, waiting for transfers between devices, local(): lax.all_to_all(outgoing_grads, 'expert', split_axis=0, concat_axis=0, til...  21.9 us
    dot_general x4, matrix products, contract_first(): lax.dot_general(left, right, (((0,), (0,)), ((), ())), preferred_element_...  21.7 us
    dot_general x2, matrix products, contract_last(): lax.dot_general(left, right, (((1,), (1,)), ((), ())), preferred_element_...  18.9 us
  transfers between devices with their start and end apart: 8, of which 7 were waited for; matrix products, arithmetic and copies ran while one was open for 24% of the time, Pallas kernels for 0%

commit v1 on v0

--- a/solution.py
+++ b/solution.py
@@ -1,6 +1,10 @@
+import functools
+
 import jax
 import jax.numpy as jnp
 from jax import lax
+from jax.experimental import pallas as pl
+from jax.experimental.pallas import tpu as pltpu
 from jax.sharding import PartitionSpec as P
 
 epsilon = 1e-05
@@ -29,7 +33,7 @@
     )
 
 
-def local(tokens, routes, centroid, ln_gain, ln_bias, w_in, b_in, w_out, b_out, cotangent):
+def local_general(tokens, routes, centroid, ln_gain, ln_bias, w_in, b_in, w_out, b_out, cotangent):
     experts = lax.axis_size("expert")
     tok_count = tokens.shape[0]
     model_width = tokens.shape[1]
@@ -146,6 +150,385 @@
     )
 
 
+f32 = jnp.float32
+bf16 = jnp.bfloat16
+
+erfc_step = 0.3 * root_half
+erfc_half = tuple(
+    0.5 * c
+    for c in (
+        0.16918935705144628,
+        0.1706908732382945,
+        0.14852168107322075,
+        0.21417961390291307,
+        -0.09282143256694776,
+        0.5449597059025907,
+        -0.5097655323576785,
+        0.48429815524087755,
+        -0.12925243016104992,
+    )
+)
+
+
+def gelu_and_slope(a):
+    bell = jnp.exp(-0.5 * a * a)
+    t = 1.0 / (1.0 + erfc_step * jnp.abs(a))
+    poly = erfc_half[-1]
+    for c in erfc_half[-2::-1]:
+        poly = poly * t + c
+    tail = poly * t * bell
+    below = jnp.where(a < 0.0, tail, 1.0 - tail)
+    return a * below, below + a * bell * gauss_norm
+
+
+def whole():
+    return pl.BlockSpec(memory_space=pltpu.VMEM)
+
+
+def call(body, outs, args, name, scratch=(), scalars=0, flops=0, limit=12 << 20):
+    moved = sum(x.size * x.dtype.itemsize for x in args) + sum(
+        x.size * x.dtype.itemsize for x in outs
+    )
+    return pl.pallas_call(
+        body,
+        out_shape=tuple(outs),
+        in_specs=[pl.BlockSpec(memory_space=pltpu.SMEM)] * scalars
+        + [whole()] * (len(args) - scalars),
+        out_specs=tuple(whole() for _ in outs),
+        scratch_shapes=list(scratch),
+        compiler_params=pltpu.CompilerParams(vmem_limit_bytes=limit),
+        cost_estimate=pl.CostEstimate(flops=flops, bytes_accessed=moved, transcendentals=0),
+        name=name,
+    )(*args)
+
+
+def out(rows, cols, dtype):
+    return jax.ShapeDtypeStruct((rows, cols), dtype)
+
+
+def iota(shape, dim):
+    return lax.broadcasted_iota(jnp.int32, shape, dim)
+
+
+def slot_row(capacity, me, row):
+    n = row.shape[1]
+    wide = jnp.broadcast_to(row, (n, n))
+    i, j = iota((n, n), 0), iota((n, n), 1)
+    col = jnp.sum(jnp.where(i == j, wide, 0), axis=1, keepdims=True)
+    rank = jnp.sum(((col == wide) & (i < j)).astype(jnp.int32), axis=0, keepdims=True)
+    return jnp.bitwise_xor(row, me) * capacity + rank
+
+
+def slot_col(capacity, me, row):
+    n = row.shape[1]
+    wide = jnp.broadcast_to(row, (n, n))
+    i, j = iota((n, n), 0), iota((n, n), 1)
+    col = jnp.sum(jnp.where(i == j, wide, 0), axis=1, keepdims=True)
+    rank = jnp.sum(((col == wide) & (j < i)).astype(jnp.int32), axis=1, keepdims=True)
+    return jnp.bitwise_xor(col, me) * capacity + rank
+
+
+def dispatch_body(capacity, me, routes, tokens, cotangent, *parts):
+    slots = len(parts) * capacity
+    n = routes.shape[1]
+    slot = slot_row(capacity, me[0], routes[...])
+    place = (iota((slots, n), 0) == jnp.broadcast_to(slot, (slots, n))).astype(bf16)
+    rows = jnp.dot(place, tokens[...], preferred_element_type=f32).astype(bf16)
+    grads = jnp.dot(place, cotangent[...], preferred_element_type=f32).astype(bf16)
+    for d, part in enumerate(parts):
+        part[0:capacity, :] = rows[d * capacity : (d + 1) * capacity, :]
+        part[capacity:, :] = grads[d * capacity : (d + 1) * capacity, :]
+
+
+def row_mean(x):
+    return jnp.mean(x, axis=1, keepdims=True)
+
+
+def norm_parts(h):
+    center = row_mean(h)
+    spread = row_mean((h - center) * (h - center))
+    inv_std = lax.rsqrt(spread + epsilon)
+    return (h - center) * inv_std, inv_std
+
+
+def gate(h, cent):
+    return jax.nn.sigmoid(jnp.sum(h * cent, axis=1, keepdims=True))
+
+
+def enter_body(capacity, count, *refs):
+    parts, (cent, gain, shift, both) = refs[:count], refs[count:]
+    half = count * capacity
+    for j, part in enumerate(parts):
+        h = part[0:capacity, :].astype(f32)
+        normed, unused = norm_parts(h)
+        lowered = normed * gain[...].astype(f32) + shift[...].astype(f32)
+        at = j * capacity
+        both[at : at + capacity, :] = lowered.astype(bf16)
+        mixing = gate(h, cent[...].astype(f32))
+        both[half + at : half + at + capacity, :] = (
+            part[capacity:, :].astype(f32) * mixing
+        ).astype(bf16)
+
+
+def middle_body(half, first, *refs):
+    (own, other, wi0, wo0, wi1, wo1, b0, b1), refs = refs[:8], refs[8:]
+    if not first:
+        before, refs = refs[0], refs[1:]
+    keep, send, n_all, dz_all, u0, da0, u1, da1, sums, z_acc, dn_acc = refs
+    n_all[0:half, :] = own[0:half, :]
+    n_all[half:, :] = other[0:half, :]
+    dz_all[0:half, :] = own[half:, :]
+    dz_all[half:, :] = other[half:, :]
+    for q, (wi, wo, b, u_ref, da_ref) in enumerate(
+        ((wi0, wo0, b0, u0, da0), (wi1, wo1, b1, u1, da1))
+    ):
+        a = jnp.dot(n_all[...], wi[...], preferred_element_type=f32) + b[...].astype(f32)
+        u, slope = gelu_and_slope(a)
+        u = u.astype(bf16)
+        u_ref[...] = u
+        z = jnp.dot(u, wo[...], preferred_element_type=f32)
+        da = (contract_last(dz_all[...], wo[...]) * slope).astype(bf16)
+        da_ref[...] = da
+        dn = contract_last(da, wi[...])
+        total = jnp.sum(da.astype(f32), axis=0, keepdims=True)
+        if not first:
+            total = total + before[q : q + 1, :]
+        sums[q : q + 1, :] = total
+        if q == 0:
+            z_acc[...] = z
+            dn_acc[...] = dn
+        else:
+            z_acc[...] += z
+            dn_acc[...] += dn
+    sums[2:, :] = jnp.zeros_like(sums[2:, :])
+    keep[0:half, :] = z_acc[0:half, :]
+    keep[half:, :] = dn_acc[0:half, :]
+    send[0:half, :] = z_acc[half:, :].astype(bf16)
+    send[half:, :] = dn_acc[half:, :].astype(bf16)
+
+
+def leave_body(capacity, count, first, last, *refs):
+    parts, refs = refs[:count], refs[count:]
+    (keep, came, cent, gain, b_out), refs = refs[:5], refs[5:]
+    if not first:
+        before, refs = refs[0], refs[1:]
+    if last:
+        hidden_sums, refs = refs[0], refs[1:]
+    replies, sums = refs[:count], refs[count]
+    half = count * capacity
+    cent_row, gain_row = cent[...].astype(f32), gain[...].astype(f32)
+    totals = [0.0, 0.0, 0.0, 0.0]
+    for j, part in enumerate(parts):
+        at = j * capacity
+        h = part[0:capacity, :].astype(f32)
+        g = part[capacity:, :].astype(f32)
+        z = keep[at : at + capacity, :] + came[at : at + capacity, :].astype(f32)
+        dn = (
+            keep[half + at : half + at + capacity, :]
+            + came[half + at : half + at + capacity, :].astype(f32)
+        )
+        f = h + (z + b_out[...].astype(f32))
+        mixing = gate(h, cent_row)
+        replies[j][0:capacity, :] = (mixing * f).astype(bf16)
+        p = jnp.sum(g * f, axis=1, keepdims=True) * mixing * (1.0 - mixing)
+        direct = g * mixing
+        normed, inv_std = norm_parts(h)
+        w = dn * gain_row
+        dh = (
+            direct
+            + p * cent_row
+            + inv_std * (w - row_mean(w) - normed * row_mean(w * normed))
+        )
+        replies[j][capacity:, :] = dh.astype(bf16)
+        for i, rows in enumerate((p * h, dn * normed, dn, direct.astype(bf16).astype(f32))):
+            totals[i] = totals[i] + jnp.sum(rows, axis=0, keepdims=True)
+    for i, total in enumerate(totals):
+        if not first:
+            total = total + before[i : i + 1, :]
+        sums[i : i + 1, :] = total
+    if last:
+        sums[4:6, :] = hidden_sums[0:2, :]
+        sums[6:, :] = jnp.zeros_like(sums[6:, :])
+    else:
+        sums[4:, :] = jnp.zeros_like(sums[4:, :])
+
+
+def weights_body(chunks, *refs):
+    u, da, n, dz = (refs[i * chunks : (i + 1) * chunks] for i in range(4))
+    rest = refs[4 * chunks :]
+    w_in_grad, w_out_grad = rest[-2:]
+    for left, right, grad, share in (
+        (u, dz, w_out_grad, rest[1]),
+        (n, da, w_in_grad, rest[0]),
+    ):
+        right = jnp.concatenate([x[...] for x in right], axis=0)
+        width = left[0].shape[1]
+        step = min(512, width)
+        for at in range(0, width, step):
+            sl = slice(at, at + step)
+            total = contract_first(jnp.concatenate([x[:, sl] for x in left], axis=0), right)
+            if len(rest) == 4:
+                total = total + share[sl, :].astype(f32)
+            grad[sl, :] = total.astype(grad.dtype)
+
+
+def combine_body(capacity, me, routes, tokens, cotangent, *refs):
+    replies, (mixed, tokens_grad) = refs[:-2], refs[-2:]
+    slots = len(replies) * capacity
+    n = routes.shape[1]
+    slot = slot_col(capacity, me[0], routes[...])
+    place = (iota((n, slots), 1) == jnp.broadcast_to(slot, (n, slots))).astype(bf16)
+    rows = jnp.concatenate([x[0:capacity, :] for x in replies], axis=0)
+    grads = jnp.concatenate([x[capacity:, :] for x in replies], axis=0)
+    mixed[...] = (
+        tokens[...].astype(f32) + jnp.dot(place, rows, preferred_element_type=f32)
+    ).astype(bf16)
+    tokens_grad[...] = cotangent[...].astype(f32) + jnp.dot(
+        place, grads, preferred_element_type=f32
+    )
+
+
+def exchange(x, axis, offset):
+    size = lax.axis_size(axis)
+    return lax.ppermute(x, axis, [(i, i ^ offset) for i in range(size)])
+
+
+def local_paired(tokens, routes, centroid, ln_gain, ln_bias, w_in, b_in, w_out, b_out, cotangent):
+    experts = lax.axis_size("expert")
+    tok_count, width = tokens.shape
+    capacity = 2 * tok_count // experts
+    hidden = w_in.shape[2]
+    core, chip = 1, 2
+    me = lax.axis_index("expert").astype(jnp.int32).reshape(1)
+    route_row = routes.reshape(1, tok_count)
+    wi0, wo0 = w_in[0], w_out[0]
+    wi1, wo1 = exchange(wi0, "batch", core), exchange(wo0, "batch", core)
+    b1 = exchange(b_in, "batch", core)
+
+    outgoing = call(
+        functools.partial(dispatch_body, capacity),
+        [out(2 * capacity, width, bf16)] * experts,
+        (me, route_row, tokens, cotangent),
+        "dispatch",
+        scalars=1,
+        flops=8 * tok_count * tok_count * width,
+    )
+    arrived = [outgoing[0]] + [
+        exchange(outgoing[d], "expert", d) for d in range(1, experts)
+    ]
+    per_chunk = max(1, 128 // capacity)
+    chunks = [list(range(d, d + per_chunk)) for d in range(0, experts, per_chunk)]
+    half = per_chunk * capacity
+    entered = []
+    for ds in chunks:
+        both = call(
+            functools.partial(enter_body, capacity, per_chunk),
+            [out(2 * half, width, bf16)],
+            (*[arrived[d] for d in ds], centroid, ln_gain, ln_bias),
+            "enter",
+        )[0]
+        entered.append((both, exchange(both, "batch", chip)))
+    done = []
+    for c, (both, other) in enumerate(entered):
+        wide = [out(2 * half, width, bf16)] * 2 + [out(2 * half, hidden, bf16)] * 4
+        done.append(
+            call(
+                functools.partial(middle_body, half, c == 0),
+                [out(2 * half, width, f32), out(2 * half, width, bf16)]
+                + wide
+                + [out(8, hidden, f32)],
+                (both, other, wi0, wo0, wi1, wo1, b_in, b1)
+                + (() if c == 0 else (done[-1][8],)),
+                "middle",
+                scratch=[pltpu.VMEM((2 * half, width), f32)] * 2,
+                flops=32 * half * width * hidden,
+                limit=24 << 20,
+            )
+        )
+    replies = {}
+    sums = None
+    for c, ds in enumerate(chunks):
+        keep, send = done[c][:2]
+        first, last = c == 0, c == len(chunks) - 1
+        *sent, sums = call(
+            functools.partial(leave_body, capacity, per_chunk, first, last),
+            [out(2 * capacity, width, bf16)] * per_chunk + [out(8, width, f32)],
+            (
+                *[arrived[d] for d in ds],
+                keep,
+                exchange(send, "batch", chip),
+                centroid,
+                ln_gain,
+                b_out,
+                *(() if first else (sums,)),
+                *((done[-1][8],) if last else ()),
+            ),
+            "leave",
+        )
+        for d, x in zip(ds, sent):
+            replies[d] = x if d == 0 else exchange(x, "expert", d)
+
+    n_all, dz_all, u0, da0, u1, da1 = ([x[i] for x in done] for i in range(2, 8))
+    flops = 8 * len(chunks) * half * width * hidden
+    shares = call(
+        functools.partial(weights_body, len(chunks)),
+        [out(width, hidden, bf16), out(hidden, width, bf16)],
+        (*u1, *da1, *n_all, *dz_all),
+        "sibling_weights",
+        flops=flops,
+    )
+    shares = [exchange(x, "batch", core) for x in shares]
+    w_in_grad, w_out_grad = call(
+        functools.partial(weights_body, len(chunks)),
+        [out(width, hidden, f32), out(hidden, width, f32)],
+        (*u0, *da0, *n_all, *dz_all, *shares),
+        "own_weights",
+        flops=flops,
+    )
+    sums_core = exchange(sums, "batch", core)
+    b_in_grad = sums[4:5] + sums_core[5:6]
+    sums = sums + sums_core
+    sums = sums + exchange(sums, "batch", chip)
+    mixed, tokens_grad = call(
+        functools.partial(combine_body, capacity),
+        [out(tok_count, width, bf16), out(tok_count, width, f32)],
+        (me, route_row, tokens, cotangent, *[replies[d] for d in range(experts)]),
+        "combine",
+        scalars=1,
+        flops=8 * tok_count * tok_count * width,
+    )
+    return (
+        mixed,
+        tokens_grad,
+        sums[0:1],
+        sums[1:2],
+        sums[2:3],
+        w_in_grad[None],
+        b_in_grad,
+        w_out_grad[None],
+        sums[3:4],
+    )
+
+
+def local(tokens, routes, centroid, ln_gain, ln_bias, w_in, b_in, w_out, b_out, cotangent):
+    experts = lax.axis_size("expert")
+    tok_count, width = tokens.shape
+    capacity = 2 * tok_count // experts
+    power_of_two = experts & (experts - 1) == 0
+    paired = (
+        lax.axis_size("batch") == 4
+        and power_of_two
+        and capacity % 16 == 0
+        and capacity <= 128
+        and width == w_in.shape[2]
+        and width % 128 == 0
+    )
+    plan = local_paired if paired else local_general
+    return plan(
+        tokens, routes, centroid, ln_gain, ln_bias, w_in, b_in, w_out, b_out, cotangent
+    )
+
+
 def solution(mesh):
     in_specs = (
         P(("expert", "batch"), None),

time: 324 us -> 230 us (0.71)
  matrix products: 76.9 us -> 0 us
  Pallas kernels: 0 us -> 60.3 us
  waiting for transfers between devices: 172 us -> 118 us
  other arithmetic: 17.8 us -> 0.61 us
  starting transfers between devices: 25.6 us -> 40.3 us
  between operations: 13.9 us -> 1.05 us
  blocking collectives: 11.1 us -> 0 us
    ppermute x0 -> x29, waiting for transfers between devices: none -> 118 us  [exchange(): return lax.ppermute(x, axis, [(i, i ^ offset) for i in range(size)])]
    reduce_scatter x2 -> x0, waiting for transfers between devices: 100 us -> none  [the longest x1 74.4 us: local(): lax.psum_scatter(contract_last(row_piece, w_first), 'batch', scatter_dime...]
    dot_general x11 -> x0, matrix products: 76.9 us -> none  [the longest x1 25 us: local(): jnp.dot(row_piece, w_first, preferred_element_type=jnp.float32) + b_first]
    all_to_all x4 -> x0, waiting for transfers between devices: 66.7 us -> none  [the longest x1 22.7 us: local(): lax.all_to_all(grad_out.reshape(experts, capacity, model_width), 'expert'...]
    pallas_call x0 -> x16, Pallas kernels: none -> 60.3 us  [call(): pl.pallas_call(body, out_shape=tuple(outs), in_specs=[pl.BlockSpec(memory...]
    ppermute x0 -> x29, starting transfers between devices: none -> 40.3 us  [exchange(): return lax.ppermute(x, axis, [(i, i ^ offset) for i in range(size)])]
    all_to_all x4 -> x0, starting transfers between devices: 25.3 us -> none  [the longest x1 6.5 us: local(): lax.all_to_all(grad_out.reshape(experts, capacity, model_width), 'expert'...]
    psum x1 -> x0, blocking collectives: 11.1 us -> none  [local(): lax.psum((centroid_part, gain_part, bias_part, b_out_part), 'batch')]
  transfers between devices with their start and end apart: 8 -> 29, of which waited for: 7 -> 19; matrix products, arithmetic and copies ran while one was open for 24% -> 1% of each run, Pallas kernels for 0% -> 14%
where the time goes in v1:
time: 230 us; the launch traced here: 226 us
  waiting for transfers between devices  118 us (51%)
  Pallas kernels  60.3 us (26%)
  starting transfers between devices  40.3 us (18%)
  local copies, waits for them, and re-layouts  5.48 us (2%)
    ppermute x29, waiting for transfers between devices, exchange(): return lax.ppermute(x, axis, [(i, i ^ offset) for i in range(size)])  118 us
    pallas_call x16, Pallas kernels, call(): pl.pallas_call(body, out_shape=tuple(outs), in_specs=[pl.BlockSpec(memory...  60.3 us
    ppermute x29, starting transfers between devices, exchange(): return lax.ppermute(x, axis, [(i, i ^ offset) for i in range(size)])  40.3 us
    unnamed x32, local copies, waits for them, and re-layouts  4.87 us
  transfers between devices with their start and end apart: 29, of which 19 were waited for; matrix products, arithmetic and copies ran while one was open for 1% of the time, Pallas kernels for 14%

profile of v1, /device:TPU:8, one launch (start us, length us, event | category | flops | bytes accessed | tf_op | source)
XLA Modules:
  0.0 226.0 jit_solution(9030169562187148591)
XLA Ops:
  4.8 1.6 collective-permute-start
  6.9 1.5 collective-permute-start.8
  8.4 4.8 %collective-permute-done.refs_1_ = bf16[128,1024]{1,0:T(8,128)(2,1)S(1)} collective-permute-done((bf16[128,1024]{1,0:T(8,128)(2,1)S(1)}, bf16[128,1024]{1,0:T(8,128)(2,1)S(1)}, u32[]{:S(2)}, u32[]{:S(2)}) %collective-permute-start) | collective-permute-done | bytes 262176 | tf_op jit(solution)/shard_map/ppermute | solution.py:393
  13.2 2.6 %collective-permute-start.13 = (bf16[128,1024]{1,0:T(8,128)(2,1)S(1)}, bf16[128,1024]{1,0:T(8,128)(2,1)S(1)}, u32[]{:S(2)}, u32[]{:S(2)}) collective-permute-start(bf16[128,1024]{1,0:T(8,128)(2,1)S(1)} %get-tuple-element.85), channel_id=1, source_target_pairs={{0,16},{4,20},{8,24},{12,28},{16,0},{20,4},{24,8},{28,12},{1,17},{... | collective-permute-start | bytes 786440 | tf_op jit(solution)/shard_map/ppermute | solution.py:393
  15.8 2.4 %collective-permute-start.14 = (bf16[128,1024]{1,0:T(8,128)(2,1)S(1)}, bf16[128,1024]{1,0:T(8,128)(2,1)S(1)}, u32[]{:S(2)}, u32[]{:S(2)}) collective-permute-start(bf16[128,1024]{1,0:T(8,128)(2,1)S(1)} %get-tuple-element.86), channel_id=1, source_target_pairs={{0,20},{4,16},{8,28},{12,24},{16,4},{20,0},{24,12},{28,8},{1,21},{... | collective-permute-start | bytes 786440 | tf_op jit(solution)/shard_map/ppermute | solution.py:393
  20.5 3.6 %collective-permute-done.8.refs_1_ = bf16[128,1024]{1,0:T(8,128)(2,1)S(1)} collective-permute-done((bf16[128,1024]{1,0:T(8,128)(2,1)S(1)}, bf16[128,1024]{1,0:T(8,128)(2,1)S(1)}, u32[]{:S(2)}, u32[]{:S(2)}) %collective-permute-start.8) | collective-permute-done | bytes 262176 | tf_op jit(solution)/shard_map/ppermute | solution.py:393
  24.1 1.6 collective-permute-start.1
  25.7 10.9 %collective-permute-done.13.refs_0_ = bf16[128,1024]{1,0:T(8,128)(2,1)S(1)} collective-permute-done((bf16[128,1024]{1,0:T(8,128)(2,1)S(1)}, bf16[128,1024]{1,0:T(8,128)(2,1)S(1)}, u32[]{:S(2)}, u32[]{:S(2)}) %collective-permute-start.13) | collective-permute-done | bytes 262176 | tf_op jit(solution)/shard_map/ppermute | solution.py:393
  36.6 5.6 %collective-permute-done.14.refs_1_ = bf16[128,1024]{1,0:T(8,128)(2,1)S(1)} collective-permute-done((bf16[128,1024]{1,0:T(8,128)(2,1)S(1)}, bf16[128,1024]{1,0:T(8,128)(2,1)S(1)}, u32[]{:S(2)}, u32[]{:S(2)}) %collective-permute-start.14) | collective-permute-done | bytes 262176 | tf_op jit(solution)/shard_map/ppermute | solution.py:393
  42.2 5.9 %collective-permute-start.20 = (bf16[128,1024]{1,0:T(8,128)(2,1)S(1)}, bf16[128,1024]{1,0:T(8,128)(2,1)S(1)}, u32[]{:S(2)}, u32[]{:S(2)}) collective-permute-start(bf16[128,1024]{1,0:T(8,128)(2,1)S(1)} %get-tuple-element.94), channel_id=1, source_target_pairs={{0,28},{4,24},{8,20},{12,16},{16,12},{20,8},{24,4},{28,0},{1,29},{... | collective-permute-start | bytes 786440 | tf_op jit(solution)/shard_map/ppermute | solution.py:393
  48.4 5.0 %collective-permute-done.19.refs_0_ = bf16[128,1024]{1,0:T(8,128)(2,1)S(1)} collective-permute-done((bf16[128,1024]{1,0:T(8,128)(2,1)S(1)}, bf16[128,1024]{1,0:T(8,128)(2,1)S(1)}, u32[]{:S(2)}, u32[]{:S(2)}) %collective-permute-start.19) | collective-permute-done | bytes 262176 | tf_op jit(solution)/shard_map/ppermute | solution.py:393
  55.0 5.9 %collective-permute-done.20.refs_1_ = bf16[128,1024]{1,0:T(8,128)(2,1)S(1)} collective-permute-done((bf16[128,1024]{1,0:T(8,128)(2,1)S(1)}, bf16[128,1024]{1,0:T(8,128)(2,1)S(1)}, u32[]{:S(2)}, u32[]{:S(2)}) %collective-permute-start.20) | collective-permute-done | bytes 262176 | tf_op jit(solution)/shard_map/ppermute | solution.py:393
  64.1 7.9 %middle.4 = (f32[256,1024]{1,0:T(8,128)S(1)}, bf16[256,1024]{1,0:T(8,128)(2,1)S(1)}, bf16[256,1024]{1,0:T(8,128)(2,1)S(1)}, bf16[256,1024]{1,0:T(8,128)(2,1)S(1)...) custom-call(bf16[256,1024]{1,0:T(8,128)(2,1)S(1)} %enter.4.refs_0_, ...), custom_call_target="tpu_custom_call" | custom-call | flops 4294967296 | bytes 14192640 | tf_op jit(solution)/shard_map/middle/pallas_call | solution.py:192
  72.0 8.2 %middle.5 = (f32[256,1024]{1,0:T(8,128)S(1)}, bf16[256,1024]{1,0:T(8,128)(2,1)S(1)}, bf16[256,1024]{1,0:T(8,128)(2,1)S(1)}, bf16[256,1024]{1,0:T(8,128)(2,1)S(1)...) custom-call(bf16[256,1024]{1,0:T(8,128)(2,1)S(1)} %enter.5.refs_0_, ...), custom_call_target="tpu_custom_call" | custom-call | flops 4294967296 | bytes 14225408 | tf_op jit(solution)/shard_map/middle/pallas_call | solution.py:192
  80.2 7.9 %middle.6 = (f32[256,1024]{1,0:T(8,128)S(1)}, bf16[256,1024]{1,0:T(8,128)(2,1)S(1)}, bf16[256,1024]{1,0:T(8,128)(2,1)S(1)}, bf16[256,1024]{1,0:T(8,128)(2,1)S(1)...) custom-call(bf16[256,1024]{1,0:T(8,128)(2,1)S(1)} %enter.6.refs_0_, ...), custom_call_target="tpu_custom_call" | custom-call | flops 4294967296 | bytes 14225408 | tf_op jit(solution)/shard_map/middle/pallas_call | solution.py:192
  88.1 17.4 %middle.7 = (f32[256,1024]{1,0:T(8,128)S(1)}, bf16[256,1024]{1,0:T(8,128)(2,1)S(1)}, bf16[256,1024]{1,0:T(8,128)(2,1)S(1)}, bf16[256,1024]{1,0:T(8,128)(2,1)S(1)...) custom-call(bf16[256,1024]{1,0:T(8,128)(2,1)S(1)} %enter.7.refs_0_, ...), custom_call_target="tpu_custom_call" | custom-call | flops 4294967296 | bytes 14225408 | tf_op jit(solution)/shard_map/middle/pallas_call | solution.py:192
  105.6 4.6 %sibling_weights.1 = (bf16[1024,1024]{1,0:T(8,128)(2,1)S(1)}, bf16[1024,1024]{1,0:T(8,128)(2,1)S(1)}) custom-call(bf16[256,1024]{1,0:T(8,128)(2,1)S(1)} %get-tuple-element.121.refs_0_, bf16[256,1024]{1,0:T(8,128)(2,1)S(1)} %get-tuple-element.122.refs_1_, bf16[256,1024]{1,0:T(8,128)(2,1)S(1)} %get-tuple-element.123.refs_2_, ...), custom_call_target="tpu_custom_call" | custom-call | flops 4294967296 | bytes 12582912 | tf_op jit(solution)/shard_map/sibling_weights/pallas_call | solution.py:192
  110.7 1.5 collective-permute-start.5
  114.3 11.3 %collective-permute-done.5.refs_3_ = bf16[256,1024]{1,0:T(8,128)(2,1)S(1)} collective-permute-done((bf16[256,1024]{1,0:T(8,128)(2,1)S(1)}, bf16[256,1024]{1,0:T(8,128)(2,1)S(1)}, u32[]{:S(2)}, u32[]{:S(2)}) %collective-permute-start.5) | collective-permute-done | bytes 524320 | tf_op jit(solution)/shard_map/ppermute | solution.py:393
  127.9 8.9 %collective-permute-done.10.refs_3_ = bf16[256,1024]{1,0:T(8,128)(2,1)S(1)} collective-permute-done((bf16[256,1024]{1,0:T(8,128)(2,1)S(1)}, bf16[256,1024]{1,0:T(8,128)(2,1)S(1)}, u32[]{:S(2)}, u32[]{:S(2)}) %collective-permute-start.10) | collective-permute-done | bytes 524320 | tf_op jit(solution)/shard_map/ppermute | solution.py:393
  138.4 9.6 %collective-permute-done.16.refs_3_ = bf16[256,1024]{1,0:T(8,128)(2,1)S(1)} collective-permute-done((bf16[256,1024]{1,0:T(8,128)(2,1)S(1)}, bf16[256,1024]{1,0:T(8,128)(2,1)S(1)}, u32[]{:S(2)}, u32[]{:S(2)}) %collective-permute-start.16) | collective-permute-done | bytes 524320 | tf_op jit(solution)/shard_map/ppermute | solution.py:393
  148.8 9.5 %collective-permute-done.22.refs_3_ = bf16[256,1024]{1,0:T(8,128)(2,1)S(1)} collective-permute-done((bf16[256,1024]{1,0:T(8,128)(2,1)S(1)}, bf16[256,1024]{1,0:T(8,128)(2,1)S(1)}, u32[]{:S(2)}, u32[]{:S(2)}) %collective-permute-start.22) | collective-permute-done | bytes 524320 | tf_op jit(solution)/shard_map/ppermute | solution.py:393
  162.0 2.4 %collective-permute-done.26 = f32[8,1024]{1,0:T(8,128)S(1)} collective-permute-done((f32[8,1024]{1,0:T(8,128)S(1)}, f32[8,1024]{1,0:T(8,128)S(1)}, u32[]{:S(2)}, u32[]{:S(2)}) %collective-permute-start.26) | collective-permute-done | bytes 32800 | tf_op jit(solution)/shard_map/ppermute | solution.py:393
  164.4 4.1 %collective-permute-start.17 = (bf16[128,1024]{1,0:T(8,128)(2,1)S(1)}, bf16[128,1024]{1,0:T(8,128)(2,1)S(1)}, u32[]{:S(2)}, u32[]{:S(2)}) collective-permute-start(bf16[128,1024]{1,0:T(8,128)(2,1)S(1)} %get-tuple-element.91), channel_id=1, source_target_pairs={{0,16},{4,20},{8,24},{12,28},{16,0},{20,4},{24,8},{28,12},{1,17},{... | collective-permute-start | bytes 786440 | tf_op jit(solution)/shard_map/ppermute | solution.py:393
  168.5 5.8 %collective-permute-done.11.refs_2_ = bf16[128,1024]{1,0:T(8,128)(2,1)S(1)} collective-permute-done((bf16[128,1024]{1,0:T(8,128)(2,1)S(1)}, bf16[128,1024]{1,0:T(8,128)(2,1)S(1)}, u32[]{:S(2)}, u32[]{:S(2)}) %collective-permute-start.11) | collective-permute-done | bytes 262176 | tf_op jit(solution)/shard_map/ppermute | solution.py:393
  174.3 4.6 %collective-permute-start.18 = (bf16[128,1024]{1,0:T(8,128)(2,1)S(1)}, bf16[128,1024]{1,0:T(8,128)(2,1)S(1)}, u32[]{:S(2)}, u32[]{:S(2)}) collective-permute-start(bf16[128,1024]{1,0:T(8,128)(2,1)S(1)} %get-tuple-element.92), channel_id=1, source_target_pairs={{0,20},{4,16},{8,28},{12,24},{16,4},{20,0},{24,12},{28,8},{1,21},{... | collective-permute-start | bytes 786440 | tf_op jit(solution)/shard_map/ppermute | solution.py:393
  179.9 3.6 %collective-permute-start.23 = (bf16[128,1024]{1,0:T(8,128)(2,1)S(1)}, bf16[128,1024]{1,0:T(8,128)(2,1)S(1)}, u32[]{:S(2)}, u32[]{:S(2)}) collective-permute-start(bf16[128,1024]{1,0:T(8,128)(2,1)S(1)} %get-tuple-element.100), channel_id=1, source_target_pairs={{0,24},{4,28},{8,16},{12,20},{16,8},{20,12},{24,0},{28,4},{1,25},{... | collective-permute-start | bytes 786440 | tf_op jit(solution)/shard_map/ppermute | solution.py:393
  185.9 17.1 %collective-permute-done.18.refs_5_ = bf16[128,1024]{1,0:T(8,128)(2,1)S(1)} collective-permute-done((bf16[128,1024]{1,0:T(8,128)(2,1)S(1)}, bf16[128,1024]{1,0:T(8,128)(2,1)S(1)}, u32[]{:S(2)}, u32[]{:S(2)}) %collective-permute-start.18) | collective-permute-done | bytes 262176 | tf_op jit(solution)/shard_map/ppermute | solution.py:393
  202.9 8.7 %collective-permute-done.23.refs_6_ = bf16[128,1024]{1,0:T(8,128)(2,1)S(1)} collective-permute-done((bf16[128,1024]{1,0:T(8,128)(2,1)S(1)}, bf16[128,1024]{1,0:T(8,128)(2,1)S(1)}, u32[]{:S(2)}, u32[]{:S(2)}) %collective-permute-start.23) | collective-permute-done | bytes 262176 | tf_op jit(solution)/shard_map/ppermute | solution.py:393
  211.7 5.1 %collective-permute-done.24.refs_7_ = bf16[128,1024]{1,0:T(8,128)(2,1)S(1)} collective-permute-done((bf16[128,1024]{1,0:T(8,128)(2,1)S(1)}, bf16[128,1024]{1,0:T(8,128)(2,1)S(1)}, u32[]{:S(2)}, u32[]{:S(2)}) %collective-permute-start.24) | collective-permute-done | bytes 262176 | tf_op jit(solution)/shard_map/ppermute | solution.py:393
  216.8 1.9 combine.1
  218.7 7.1 %own_weights.1 = (f32[1024,1024]{1,0:T(8,128)}, f32[1024,1024]{1,0:T(8,128)}) custom-call(bf16[256,1024]{1,0:T(8,128)(2,1)S(1)} %get-tuple-element.105.refs_0_, bf16[256,1024]{1,0:T(8,128)(2,1)S(1)} %get-tuple-element.106.refs_1_, bf16[256,1024]{1,0:T(8,128)(2,1)S(1)} %get-tuple-element.107.refs_2_, bf16[256,1024]{1,0:T(8,128)(2,1)S(1)} %get-tuple-element.108.refs_3_, ...), custom_call_target="tpu_custom_call" | custom-call | flops 4294967296 | bytes 20971520 | tf_op jit(solution)/shard_map/own_weights/pallas_call | solution.py:192
  (78 shorter events, 26.5 us)
Async XLA Ops:
  0.7 63.4 %collective-permute-start.2 = (bf16[1024,1024]{1,0:T(8,128)(2,1)}, bf16[1024,1024]{1,0:T(8,128)(2,1)S(1)}, u32[]{:S(2)}, u32[]{:S(2)}) collective-permute-start(bf16[1024,1024]{1,0:T(8,128)(2,1)} %bitcast.8), channel_id=1, source_target_pairs={{0,1},{1,0},{2,3},{3,2},{4,5},{5,4},{6,7},{7,6},{8,9},{9,8},{10,11... | collective-permute-start | bytes 6291464 | tf_op jit(solution)/shard_map/ppermute | solution.py:393
  0.7 63.3 %collective-permute-start.3 = (bf16[1024,1024]{1,0:T(8,128)(2,1)}, bf16[1024,1024]{1,0:T(8,128)(2,1)}, u32[]{:S(2)}, u32[]{:S(2)}) collective-permute-start(bf16[1024,1024]{1,0:T(8,128)(2,1)} %bitcast.13), channel_id=1, source_target_pairs={{0,1},{1,0},{2,3},{3,2},{4,5},{5,4},{6,7},{7,6},{8,9},{9,8},{10,11... | collective-permute-start | bytes 6291464 | tf_op jit(solution)/shard_map/ppermute | solution.py:393
  4.8 8.4 %collective-permute-start = (bf16[128,1024]{1,0:T(8,128)(2,1)S(1)}, bf16[128,1024]{1,0:T(8,128)(2,1)S(1)}, u32[]{:S(2)}, u32[]{:S(2)}) collective-permute-start(bf16[128,1024]{1,0:T(8,128)(2,1)S(1)} %get-tuple-element.72), channel_id=1, source_target_pairs={{0,4},{4,0},{8,12},{12,8},{16,20},{20,16},{24,28},{28,24},{1,5},{5... | collective-permute-start | bytes 786440 | tf_op jit(solution)/shard_map/ppermute | solution.py:393
  6.4 9.4 %collective-permute-start.7 = (bf16[128,1024]{1,0:T(8,128)(2,1)S(1)}, bf16[128,1024]{1,0:T(8,128)(2,1)S(1)}, u32[]{:S(2)}, u32[]{:S(2)}) collective-permute-start(bf16[128,1024]{1,0:T(8,128)(2,1)S(1)} %get-tuple-element.77), channel_id=1, source_target_pairs={{0,8},{4,12},{8,0},{12,4},{16,24},{20,28},{24,16},{28,20},{1,9},{5... | collective-permute-start | bytes 786440 | tf_op jit(solution)/shard_map/ppermute | solution.py:393
  6.9 17.3 %collective-permute-start.8 = (bf16[128,1024]{1,0:T(8,128)(2,1)S(1)}, bf16[128,1024]{1,0:T(8,128)(2,1)S(1)}, u32[]{:S(2)}, u32[]{:S(2)}) collective-permute-start(bf16[128,1024]{1,0:T(8,128)(2,1)S(1)} %get-tuple-element.78), channel_id=1, source_target_pairs={{0,12},{4,8},{8,4},{12,0},{16,28},{20,24},{24,20},{28,16},{1,13},{... | collective-permute-start | bytes 786440 | tf_op jit(solution)/shard_map/ppermute | solution.py:393
  13.2 23.4 %collective-permute-start.13 = (bf16[128,1024]{1,0:T(8,128)(2,1)S(1)}, bf16[128,1024]{1,0:T(8,128)(2,1)S(1)}, u32[]{:S(2)}, u32[]{:S(2)}) collective-permute-start(bf16[128,1024]{1,0:T(8,128)(2,1)S(1)} %get-tuple-element.85), channel_id=1, source_target_pairs={{0,16},{4,20},{8,24},{12,28},{16,0},{20,4},{24,8},{28,12},{1,17},{... | collective-permute-start | bytes 786440 | tf_op jit(solution)/shard_map/ppermute | solution.py:393
  15.8 26.4 %collective-permute-start.14 = (bf16[128,1024]{1,0:T(8,128)(2,1)S(1)}, bf16[128,1024]{1,0:T(8,128)(2,1)S(1)}, u32[]{:S(2)}, u32[]{:S(2)}) collective-permute-start(bf16[128,1024]{1,0:T(8,128)(2,1)S(1)} %get-tuple-element.86), channel_id=1, source_target_pairs={{0,20},{4,16},{8,28},{12,24},{16,4},{20,0},{24,12},{28,8},{1,21},{... | collective-permute-start | bytes 786440 | tf_op jit(solution)/shard_map/ppermute | solution.py:393
  24.1 39.4 %collective-permute-start.1 = (bf16[256,1024]{1,0:T(8,128)(2,1)S(1)}, bf16[256,1024]{1,0:T(8,128)(2,1)S(1)}, u32[]{:S(2)}, u32[]{:S(2)}) collective-permute-start(bf16[256,1024]{1,0:T(8,128)(2,1)S(1)} %enter.4.refs_0_), channel_id=1, source_target_pairs={{0,2},{1,3},{2,0},{3,1},{4,6},{5,7},{6,4},{7,5},{8,10},{9,11},{10,... | collective-permute-start | bytes 1572872 | tf_op jit(solution)/shard_map/ppermute | solution.py:393
  36.6 16.9 %collective-permute-start.19 = (bf16[128,1024]{1,0:T(8,128)(2,1)S(1)}, bf16[128,1024]{1,0:T(8,128)(2,1)S(1)}, u32[]{:S(2)}, u32[]{:S(2)}) collective-permute-start(bf16[128,1024]{1,0:T(8,128)(2,1)S(1)} %get-tuple-element.93), channel_id=1, source_target_pairs={{0,24},{4,28},{8,16},{12,20},{16,8},{20,12},{24,0},{28,4},{1,25},{... | collective-permute-start | bytes 786440 | tf_op jit(solution)/shard_map/ppermute | solution.py:393
  42.2 18.7 %collective-permute-start.20 = (bf16[128,1024]{1,0:T(8,128)(2,1)S(1)}, bf16[128,1024]{1,0:T(8,128)(2,1)S(1)}, u32[]{:S(2)}, u32[]{:S(2)}) collective-permute-start(bf16[128,1024]{1,0:T(8,128)(2,1)S(1)} %get-tuple-element.94), channel_id=1, source_target_pairs={{0,28},{4,24},{8,20},{12,16},{16,12},{20,8},{24,4},{28,0},{1,29},{... | collective-permute-start | bytes 786440 | tf_op jit(solution)/shard_map/ppermute | solution.py:393
  53.5 18.6 %collective-permute-start.9 = (bf16[256,1024]{1,0:T(8,128)(2,1)S(1)}, bf16[256,1024]{1,0:T(8,128)(2,1)S(1)}, u32[]{:S(2)}, u32[]{:S(2)}) collective-permute-start(bf16[256,1024]{1,0:T(8,128)(2,1)S(1)} %enter.5.refs_0_), channel_id=1, source_target_pairs={{0,2},{1,3},{2,0},{3,1},{4,6},{5,7},{6,4},{7,5},{8,10},{9,11},{10,... | collective-permute-start | bytes 1572872 | tf_op jit(solution)/shard_map/ppermute | solution.py:393
  60.9 1.2 collective-permute-start.4
  62.0 18.2 %collective-permute-start.15 = (bf16[256,1024]{1,0:T(8,128)(2,1)S(1)}, bf16[256,1024]{1,0:T(8,128)(2,1)S(1)}, u32[]{:S(2)}, u32[]{:S(2)}) collective-permute-start(bf16[256,1024]{1,0:T(8,128)(2,1)S(1)} %enter.6.refs_0_), channel_id=1, source_target_pairs={{0,2},{1,3},{2,0},{3,1},{4,6},{5,7},{6,4},{7,5},{8,10},{9,11},{10,... | collective-permute-start | bytes 1572872 | tf_op jit(solution)/shard_map/ppermute | solution.py:393
  63.5 24.6 %collective-permute-start.21 = (bf16[256,1024]{1,0:T(8,128)(2,1)S(1)}, bf16[256,1024]{1,0:T(8,128)(2,1)S(1)}, u32[]{:S(2)}, u32[]{:S(2)}) collective-permute-start(bf16[256,1024]{1,0:T(8,128)(2,1)S(1)} %enter.7.refs_0_), channel_id=1, source_target_pairs={{0,2},{1,3},{2,0},{3,1},{4,6},{5,7},{6,4},{7,5},{8,10},{9,11},{10,... | collective-permute-start | bytes 1572872 | tf_op jit(solution)/shard_map/ppermute | solution.py:393
  110.2 108.5 %collective-permute-start.27 = (bf16[1024,1024]{1,0:T(8,128)(2,1)S(1)}, bf16[1024,1024]{1,0:T(8,128)(2,1)S(1)}, u32[]{:S(2)}, u32[]{:S(2)}) collective-permute-start(bf16[1024,1024]{1,0:T(8,128)(2,1)S(1)} %get-tuple-element.129), channel_id=1, source_target_pairs={{0,1},{1,0},{2,3},{3,2},{4,5},{5,4},{6,7},{7,6},{8,9},{9,8},{10,11... | collective-permute-start | bytes 6291464 | tf_op jit(solution)/shard_map/ppermute | solution.py:393
  110.2 108.4 %collective-permute-start.28 = (bf16[1024,1024]{1,0:T(8,128)(2,1)S(1)}, bf16[1024,1024]{1,0:T(8,128)(2,1)S(1)}, u32[]{:S(2)}, u32[]{:S(2)}) collective-permute-start(bf16[1024,1024]{1,0:T(8,128)(2,1)S(1)} %get-tuple-element.130), channel_id=1, source_target_pairs={{0,1},{1,0},{2,3},{3,2},{4,5},{5,4},{6,7},{7,6},{8,9},{9,8},{10,11... | collective-permute-start | bytes 6291464 | tf_op jit(solution)/shard_map/ppermute | solution.py:393
  110.7 14.8 %collective-permute-start.5 = (bf16[256,1024]{1,0:T(8,128)(2,1)S(1)}, bf16[256,1024]{1,0:T(8,128)(2,1)S(1)}, u32[]{:S(2)}, u32[]{:S(2)}) collective-permute-start(bf16[256,1024]{1,0:T(8,128)(2,1)S(1)} %get-tuple-element.74), channel_id=1, source_target_pairs={{0,2},{1,3},{2,0},{3,1},{4,6},{5,7},{6,4},{7,5},{8,10},{9,11},{10,... | collective-permute-start | bytes 1572872 | tf_op jit(solution)/shard_map/ppermute | solution.py:393
  112.2 24.5 %collective-permute-start.10 = (bf16[256,1024]{1,0:T(8,128)(2,1)S(1)}, bf16[256,1024]{1,0:T(8,128)(2,1)S(1)}, u32[]{:S(2)}, u32[]{:S(2)}) collective-permute-start(bf16[256,1024]{1,0:T(8,128)(2,1)S(1)} %get-tuple-element.81), channel_id=1, source_target_pairs={{0,2},{1,3},{2,0},{3,1},{4,6},{5,7},{6,4},{7,5},{8,10},{9,11},{10,... | collective-permute-start | bytes 1572872 | tf_op jit(solution)/shard_map/ppermute | solution.py:393
  112.8 35.2 %collective-permute-start.16 = (bf16[256,1024]{1,0:T(8,128)(2,1)S(1)}, bf16[256,1024]{1,0:T(8,128)(2,1)S(1)}, u32[]{:S(2)}, u32[]{:S(2)}) collective-permute-start(bf16[256,1024]{1,0:T(8,128)(2,1)S(1)} %get-tuple-element.89), channel_id=1, source_target_pairs={{0,2},{1,3},{2,0},{3,1},{4,6},{5,7},{6,4},{7,5},{8,10},{9,11},{10,... | collective-permute-start | bytes 1572872 | tf_op jit(solution)/shard_map/ppermute | solution.py:393
  125.5 32.8 %collective-permute-start.22 = (bf16[256,1024]{1,0:T(8,128)(2,1)S(1)}, bf16[256,1024]{1,0:T(8,128)(2,1)S(1)}, u32[]{:S(2)}, u32[]{:S(2)}) collective-permute-start(bf16[256,1024]{1,0:T(8,128)(2,1)S(1)} %get-tuple-element.97), channel_id=1, source_target_pairs={{0,2},{1,3},{2,0},{3,1},{4,6},{5,7},{6,4},{7,5},{8,10},{9,11},{10,... | collective-permute-start | bytes 1572872 | tf_op jit(solution)/shard_map/ppermute | solution.py:393
  136.7 27.7 %collective-permute-start.6 = (bf16[128,1024]{1,0:T(8,128)(2,1)S(1)}, bf16[128,1024]{1,0:T(8,128)(2,1)S(1)}, u32[]{:S(2)}, u32[]{:S(2)}) collective-permute-start(bf16[128,1024]{1,0:T(8,128)(2,1)S(1)} %get-tuple-element.76), channel_id=1, source_target_pairs={{0,4},{4,0},{8,12},{12,8},{16,20},{20,16},{24,28},{28,24},{1,5},{5... | collective-permute-start | bytes 786440 | tf_op jit(solution)/shard_map/ppermute | solution.py:393
  148.0 68.8 %copy-start.1 = (bf16[256,1024]{1,0:T(8,128)(2,1)S(1)}, bf16[256,1024]{1,0:T(8,128)(2,1)}, u32[]{:S(2)}) copy-start(bf16[256,1024]{1,0:T(8,128)(2,1)} %tokens.3) | copy-start | bytes 1572868
  148.0 68.8 %copy-start.3 = (bf16[256,1024]{1,0:T(8,128)(2,1)S(1)}, bf16[256,1024]{1,0:T(8,128)(2,1)}, u32[]{:S(2)}) copy-start(bf16[256,1024]{1,0:T(8,128)(2,1)} %cotangent.3) | copy-start | bytes 1572868
  148.0 68.8 %copy-start.12 = (s32[256,1]{0,1:T(1,128)S(1)}, s32[256,1]{0,1:T(1,128)}, u32[]{:S(2)}) copy-start(s32[256,1]{0,1:T(1,128)} %param.11) | copy-start | bytes 3076
  159.2 1.3 collective-permute-start.25
  160.5 3.9 %collective-permute-start.26 = (f32[8,1024]{1,0:T(8,128)S(1)}, f32[8,1024]{1,0:T(8,128)S(1)}, u32[]{:S(2)}, u32[]{:S(2)}) collective-permute-start(f32[8,1024]{1,0:T(8,128)S(1)} %add.9), channel_id=1, source_target_pairs={{0,2},{1,3},{2,0},{3,1},{4,6},{5,7},{6,4},{7,5},{8,10},{9,11},{10,... | collective-permute-start | bytes 98312 | tf_op jit(solution)/shard_map/ppermute | solution.py:393
  162.0 12.3 %collective-permute-start.11 = (bf16[128,1024]{1,0:T(8,128)(2,1)S(1)}, bf16[128,1024]{1,0:T(8,128)(2,1)S(1)}, u32[]{:S(2)}, u32[]{:S(2)}) collective-permute-start(bf16[128,1024]{1,0:T(8,128)(2,1)S(1)} %get-tuple-element.83), channel_id=1, source_target_pairs={{0,8},{4,12},{8,0},{12,4},{16,24},{20,28},{24,16},{28,20},{1,9},{5... | collective-permute-start | bytes 786440 | tf_op jit(solution)/shard_map/ppermute | solution.py:393
  164.4 15.5 %collective-permute-start.12 = (bf16[128,1024]{1,0:T(8,128)(2,1)S(1)}, bf16[128,1024]{1,0:T(8,128)(2,1)S(1)}, u32[]{:S(2)}, u32[]{:S(2)}) collective-permute-start(bf16[128,1024]{1,0:T(8,128)(2,1)S(1)} %get-tuple-element.84), channel_id=1, source_target_pairs={{0,12},{4,8},{8,4},{12,0},{16,28},{20,24},{24,20},{28,16},{1,13},{... | collective-permute-start | bytes 786440 | tf_op jit(solution)/shard_map/ppermute | solution.py:393
  164.4 20.2 %collective-permute-start.17 = (bf16[128,1024]{1,0:T(8,128)(2,1)S(1)}, bf16[128,1024]{1,0:T(8,128)(2,1)S(1)}, u32[]{:S(2)}, u32[]{:S(2)}) collective-permute-start(bf16[128,1024]{1,0:T(8,128)(2,1)S(1)} %get-tuple-element.91), channel_id=1, source_target_pairs={{0,16},{4,20},{8,24},{12,28},{16,0},{20,4},{24,8},{28,12},{1,17},{... | collective-permute-start | bytes 786440 | tf_op jit(solution)/shard_map/ppermute | solution.py:393
  174.3 28.6 %collective-permute-start.18 = (bf16[128,1024]{1,0:T(8,128)(2,1)S(1)}, bf16[128,1024]{1,0:T(8,128)(2,1)S(1)}, u32[]{:S(2)}, u32[]{:S(2)}) collective-permute-start(bf16[128,1024]{1,0:T(8,128)(2,1)S(1)} %get-tuple-element.92), channel_id=1, source_target_pairs={{0,20},{4,16},{8,28},{12,24},{16,4},{20,0},{24,12},{28,8},{1,21},{... | collective-permute-start | bytes 786440 | tf_op jit(solution)/shard_map/ppermute | solution.py:393
  179.9 31.8 %collective-permute-start.23 = (bf16[128,1024]{1,0:T(8,128)(2,1)S(1)}, bf16[128,1024]{1,0:T(8,128)(2,1)S(1)}, u32[]{:S(2)}, u32[]{:S(2)}) collective-permute-start(bf16[128,1024]{1,0:T(8,128)(2,1)S(1)} %get-tuple-element.100), channel_id=1, source_target_pairs={{0,24},{4,28},{8,16},{12,20},{16,8},{20,12},{24,0},{28,4},{1,25},{... | collective-permute-start | bytes 786440 | tf_op jit(solution)/shard_map/ppermute | solution.py:393
  184.6 32.2 %collective-permute-start.24 = (bf16[128,1024]{1,0:T(8,128)(2,1)S(1)}, bf16[128,1024]{1,0:T(8,128)(2,1)S(1)}, u32[]{:S(2)}, u32[]{:S(2)}) collective-permute-start(bf16[128,1024]{1,0:T(8,128)(2,1)S(1)} %get-tuple-element.101), channel_id=1, source_target_pairs={{0,28},{4,24},{8,20},{12,16},{16,12},{20,8},{24,4},{28,0},{1,29},{... | collective-permute-start | bytes 786440 | tf_op jit(solution)/shard_map/ppermute | solution.py:393
  (13 other events, 264.5 us)

commit v2 on v1

--- a/solution.py
+++ b/solution.py
@@ -185,21 +185,29 @@
     return pl.BlockSpec(memory_space=pltpu.VMEM)
 
 
-def call(body, outs, args, name, scratch=(), scalars=0, flops=0, limit=12 << 20):
-    moved = sum(x.size * x.dtype.itemsize for x in args) + sum(
-        x.size * x.dtype.itemsize for x in outs
-    )
+def call(body, outs, args, name, scratch=(), scalars=0, far=0, limit=12 << 20, after=()):
+    count, extra = len(args), len(after)
+    args = tuple(
+        pltpu.with_memory_space_constraint(x, pltpu.HBM) if scalars <= i < scalars + far else x
+        for i, x in enumerate(args)
+    )
+
+    def run(*refs):
+        body(*refs[:count], *refs[count + extra :])
+
     return pl.pallas_call(
-        body,
+        run,
         out_shape=tuple(outs),
         in_specs=[pl.BlockSpec(memory_space=pltpu.SMEM)] * scalars
-        + [whole()] * (len(args) - scalars),
+        + [pl.BlockSpec(memory_space=pltpu.HBM)] * far
+        + [whole()] * (count - scalars - far)
+        + [pl.BlockSpec(memory_space=pl.ANY)] * extra,
         out_specs=tuple(whole() for _ in outs),
         scratch_shapes=list(scratch),
         compiler_params=pltpu.CompilerParams(vmem_limit_bytes=limit),
-        cost_estimate=pl.CostEstimate(flops=flops, bytes_accessed=moved, transcendentals=0),
+        cost_estimate=pl.CostEstimate(flops=0, bytes_accessed=0, transcendentals=0),
         name=name,
-    )(*args)
+    )(*args, *after)
 
 
 def out(rows, cols, dtype):
@@ -228,16 +236,44 @@
     return jnp.bitwise_xor(col, me) * capacity + rank
 
 
-def dispatch_body(capacity, me, routes, tokens, cotangent, *parts):
-    slots = len(parts) * capacity
+def dispatch_body(capacity, experts, me, *refs):
+    far, parts, rest = refs[:10], refs[10 : 10 + experts], refs[10 + experts :]
+    weights, params, tokens, cotangent, routes, sems, *lines = rest
+    rows_in, rows_out = far[3].shape[0], far[4].shape[0]
+    places = [
+        routes,
+        tokens,
+        cotangent,
+        weights.at[0:rows_in],
+        weights.at[rows_in : rows_in + rows_out],
+        *lines,
+    ]
+    copies = [
+        pltpu.make_async_copy(x, place, sems.at[i])
+        for i, (x, place) in enumerate(zip(far, places))
+    ]
+    for copy in copies:
+        copy.start()
+    slots = experts * capacity
+    copies[0].wait()
     n = routes.shape[1]
     slot = slot_row(capacity, me[0], routes[...])
     place = (iota((slots, n), 0) == jnp.broadcast_to(slot, (slots, n))).astype(bf16)
+    copies[1].wait()
     rows = jnp.dot(place, tokens[...], preferred_element_type=f32).astype(bf16)
+    for d, part in enumerate(parts):
+        part[0:capacity, :] = rows[d * capacity : (d + 1) * capacity, :]
+    copies[2].wait()
     grads = jnp.dot(place, cotangent[...], preferred_element_type=f32).astype(bf16)
     for d, part in enumerate(parts):
-        part[0:capacity, :] = rows[d * capacity : (d + 1) * capacity, :]
         part[capacity:, :] = grads[d * capacity : (d + 1) * capacity, :]
+    for copy in copies[3:]:
+        copy.wait()
+    spare = weights.shape[0] - rows_in - rows_out
+    weights[rows_in + rows_out :, :] = jnp.broadcast_to(lines[0][...], (spare, lines[0].shape[1]))
+    for i, line in enumerate(lines[1:]):
+        params[i : i + 1, :] = line[...].astype(f32)
+    params[len(lines) - 1 :, :] = jnp.zeros_like(params[len(lines) - 1 :, :])
 
 
 def row_mean(x):
@@ -256,38 +292,46 @@
 
 
 def enter_body(capacity, count, *refs):
-    parts, (cent, gain, shift, both) = refs[:count], refs[count:]
+    parts, (params, both) = refs[:count], refs[count:]
+    cent, gain, shift = (params[i : i + 1, :] for i in range(3))
     half = count * capacity
     for j, part in enumerate(parts):
         h = part[0:capacity, :].astype(f32)
         normed, unused = norm_parts(h)
-        lowered = normed * gain[...].astype(f32) + shift[...].astype(f32)
+        lowered = normed * gain + shift
         at = j * capacity
         both[at : at + capacity, :] = lowered.astype(bf16)
-        mixing = gate(h, cent[...].astype(f32))
+        mixing = gate(h, cent)
         both[half + at : half + at + capacity, :] = (
             part[capacity:, :].astype(f32) * mixing
         ).astype(bf16)
 
 
-def middle_body(half, first, *refs):
-    (own, other, wi0, wo0, wi1, wo1, b0, b1), refs = refs[:8], refs[8:]
+def middle_body(count, half, first, *refs):
+    own, other, refs = refs[:count], refs[count : 2 * count], refs[2 * count :]
+    quarters, refs = refs[:2], refs[2:]
     if not first:
         before, refs = refs[0], refs[1:]
     keep, send, n_all, dz_all, u0, da0, u1, da1, sums, z_acc, dn_acc = refs
-    n_all[0:half, :] = own[0:half, :]
-    n_all[half:, :] = other[0:half, :]
-    dz_all[0:half, :] = own[half:, :]
-    dz_all[half:, :] = other[half:, :]
-    for q, (wi, wo, b, u_ref, da_ref) in enumerate(
-        ((wi0, wo0, b0, u0, da0), (wi1, wo1, b1, u1, da1))
+    at = 0
+    for both in own + other:
+        rows = both.shape[0] // 2
+        n_all[at : at + rows, :] = both[0:rows, :]
+        dz_all[at : at + rows, :] = both[rows:, :]
+        at += rows
+    width, hidden = n_all.shape[1], u0.shape[1]
+    for q, (weights, u_ref, da_ref) in enumerate(
+        ((quarters[0], u0, da0), (quarters[1], u1, da1))
     ):
+        wi, wo = weights.at[0:width], weights.at[width : width + hidden]
+        b = weights.at[width + hidden : width + hidden + 1]
         a = jnp.dot(n_all[...], wi[...], preferred_element_type=f32) + b[...].astype(f32)
+        t = contract_last(dz_all[...], wo[...])
         u, slope = gelu_and_slope(a)
         u = u.astype(bf16)
         u_ref[...] = u
         z = jnp.dot(u, wo[...], preferred_element_type=f32)
-        da = (contract_last(dz_all[...], wo[...]) * slope).astype(bf16)
+        da = (t * slope).astype(bf16)
         da_ref[...] = da
         dn = contract_last(da, wi[...])
         total = jnp.sum(da.astype(f32), axis=0, keepdims=True)
@@ -309,14 +353,14 @@
 
 def leave_body(capacity, count, first, last, *refs):
     parts, refs = refs[:count], refs[count:]
-    (keep, came, cent, gain, b_out), refs = refs[:5], refs[5:]
+    (keep, came, params), refs = refs[:3], refs[3:]
     if not first:
         before, refs = refs[0], refs[1:]
     if last:
         hidden_sums, refs = refs[0], refs[1:]
     replies, sums = refs[:count], refs[count]
     half = count * capacity
-    cent_row, gain_row = cent[...].astype(f32), gain[...].astype(f32)
+    cent_row, gain_row, last_row = (params[i : i + 1, :] for i in (0, 1, 3))
     totals = [0.0, 0.0, 0.0, 0.0]
     for j, part in enumerate(parts):
         at = j * capacity
@@ -327,7 +371,7 @@
             keep[half + at : half + at + capacity, :]
             + came[half + at : half + at + capacity, :].astype(f32)
         )
-        f = h + (z + b_out[...].astype(f32))
+        f = h + (z + last_row)
         mixing = gate(h, cent_row)
         replies[j][0:capacity, :] = (mixing * f).astype(bf16)
         p = jnp.sum(g * f, axis=1, keepdims=True) * mixing * (1.0 - mixing)
@@ -356,20 +400,24 @@
 def weights_body(chunks, *refs):
     u, da, n, dz = (refs[i * chunks : (i + 1) * chunks] for i in range(4))
     rest = refs[4 * chunks :]
-    w_in_grad, w_out_grad = rest[-2:]
-    for left, right, grad, share in (
-        (u, dz, w_out_grad, rest[1]),
-        (n, da, w_in_grad, rest[0]),
-    ):
-        right = jnp.concatenate([x[...] for x in right], axis=0)
-        width = left[0].shape[1]
-        step = min(512, width)
-        for at in range(0, width, step):
-            sl = slice(at, at + step)
-            total = contract_first(jnp.concatenate([x[:, sl] for x in left], axis=0), right)
-            if len(rest) == 4:
-                total = total + share[sl, :].astype(f32)
-            grad[sl, :] = total.astype(grad.dtype)
+    width, hidden = n[0].shape[1], u[0].shape[1]
+    step = 512
+    for k, (left, right) in enumerate(((n, da), (u, dz))):
+        size = left[0].shape[1]
+        grad, offset = (rest[0], k * width) if len(rest) == 1 else (rest[1 + k], 0)
+
+        def some(i, unused, left=left, right=right, grad=grad, offset=offset, k=k):
+            at = pl.multiple_of(i * step, step)
+            total = contract_first(
+                jnp.concatenate([x[:, pl.ds(at, step)] for x in left], axis=0),
+                jnp.concatenate([x[...] for x in right], axis=0),
+            )
+            if len(rest) == 3:
+                total = total + rest[0][pl.ds(k * width + at, step), :].astype(f32)
+            grad[pl.ds(offset + at, step), :] = total.astype(grad.dtype)
+            return unused
+
+        lax.fori_loop(0, size // step, some, 0)
 
 
 def combine_body(capacity, me, routes, tokens, cotangent, *refs):
@@ -388,9 +436,27 @@
     )
 
 
-def exchange(x, axis, offset):
-    size = lax.axis_size(axis)
-    return lax.ppermute(x, axis, [(i, i ^ offset) for i in range(size)])
+class Order:
+    def __init__(self):
+        self.fence = []
+
+    def kernel(self, body, outs, args, name, **more):
+        mine = {id(x) for x in args}
+        after = [x for x in self.fence if id(x) not in mine]
+        got = call(body, outs, args, name, after=after, **more)
+        self.fence = [got[-1]]
+        return got
+
+    def start(self, x, axis, offset, name="rows"):
+        others = [y for y in self.fence if y is not x]
+        if others:
+            x = lax.optimization_barrier((x, *others))[0]
+        size = lax.axis_size(axis)
+        with jax.named_scope(name):
+            return lax.ppermute(x, axis, [(i, i ^ offset) for i in range(size)])
+
+    def wait(self, *arrays):
+        self.fence = self.fence + list(arrays)
 
 
 def local_paired(tokens, routes, centroid, ln_gain, ln_bias, w_in, b_in, w_out, b_out, cotangent):
@@ -399,114 +465,178 @@
     capacity = 2 * tok_count // experts
     hidden = w_in.shape[2]
     core, chip = 1, 2
+    order = Order()
     me = lax.axis_index("expert").astype(jnp.int32).reshape(1)
-    route_row = routes.reshape(1, tok_count)
-    wi0, wo0 = w_in[0], w_out[0]
-    wi1, wo1 = exchange(wi0, "batch", core), exchange(wo0, "batch", core)
-    b1 = exchange(b_in, "batch", core)
-
-    outgoing = call(
-        functools.partial(dispatch_body, capacity),
-        [out(2 * capacity, width, bf16)] * experts,
-        (me, route_row, tokens, cotangent),
+    *parts, weights, params, tokens_near, cotangent_near, routes_near = order.kernel(
+        functools.partial(dispatch_body, capacity, experts),
+        [out(2 * capacity, width, bf16)] * experts
+        + [
+            out(width + hidden + 16, hidden, bf16),
+            out(8, width, f32),
+            out(tok_count, width, bf16),
+            out(tok_count, width, bf16),
+            out(1, tok_count, jnp.int32),
+        ],
+        (
+            *(me, routes.reshape(1, tok_count), tokens, cotangent, w_in[0], w_out[0], b_in),
+            *(centroid, ln_gain, ln_bias, b_out),
+        ),
         "dispatch",
         scalars=1,
-        flops=8 * tok_count * tok_count * width,
-    )
-    arrived = [outgoing[0]] + [
-        exchange(outgoing[d], "expert", d) for d in range(1, experts)
-    ]
-    per_chunk = max(1, 128 // capacity)
-    chunks = [list(range(d, d + per_chunk)) for d in range(0, experts, per_chunk)]
-    half = per_chunk * capacity
-    entered = []
-    for ds in chunks:
-        both = call(
-            functools.partial(enter_body, capacity, per_chunk),
-            [out(2 * half, width, bf16)],
-            (*[arrived[d] for d in ds], centroid, ln_gain, ln_bias),
+        far=10,
+        scratch=[pltpu.SemaphoreType.DMA((10,))]
+        + [pltpu.VMEM((1, x.shape[1]), bf16) for x in (b_in, centroid, ln_gain, ln_bias, b_out)],
+    )
+    order.fence = [params]
+    arrived = {0: parts[0]}
+    both, other, mids, replies, left = {}, {}, {}, {}, {}
+    sums = {"middle": (), "leave": ()}
+
+    def send(*ds):
+        for d in ds:
+            arrived[d] = order.start(parts[d], "expert", d, f"out_{d}")
+
+    def sent(*ds):
+        order.wait(*[arrived[d] for d in ds])
+
+    def enter(c, ds):
+        both[c] = order.kernel(
+            functools.partial(enter_body, capacity, len(ds)),
+            [out(2 * len(ds) * capacity, width, bf16)],
+            (*[arrived[d] for d in ds], params),
             "enter",
         )[0]
-        entered.append((both, exchange(both, "batch", chip)))
-    done = []
-    for c, (both, other) in enumerate(entered):
-        wide = [out(2 * half, width, bf16)] * 2 + [out(2 * half, hidden, bf16)] * 4
-        done.append(
-            call(
-                functools.partial(middle_body, half, c == 0),
-                [out(2 * half, width, f32), out(2 * half, width, bf16)]
-                + wide
-                + [out(8, hidden, f32)],
-                (both, other, wi0, wo0, wi1, wo1, b_in, b1)
-                + (() if c == 0 else (done[-1][8],)),
-                "middle",
-                scratch=[pltpu.VMEM((2 * half, width), f32)] * 2,
-                flops=32 * half * width * hidden,
-                limit=24 << 20,
-            )
+        other[c] = order.start(both[c], "batch", chip, f"share_{c}")
+
+    def middle(c, cs):
+        half = sum(both[i].shape[0] for i in cs) // 2
+        mids[c] = order.kernel(
+            functools.partial(middle_body, len(cs), half, not sums["middle"]),
+            [out(2 * half, width, f32), out(2 * half, width, bf16)]
+            + [out(2 * half, width, bf16)] * 2
+            + [out(2 * half, hidden, bf16)] * 4
+            + [out(8, hidden, f32)],
+            (
+                *[both[i] for i in cs],
+                *[other[i] for i in cs],
+                *(weights, sibling),
+                *sums["middle"],
+            ),
+            "middle",
+            scratch=[pltpu.VMEM((2 * half, width), f32)] * 2,
+            limit=24 << 20,
         )
-    replies = {}
-    sums = None
-    for c, ds in enumerate(chunks):
-        keep, send = done[c][:2]
-        first, last = c == 0, c == len(chunks) - 1
-        *sent, sums = call(
-            functools.partial(leave_body, capacity, per_chunk, first, last),
-            [out(2 * capacity, width, bf16)] * per_chunk + [out(8, width, f32)],
+        sums["middle"] = (mids[c][8],)
+        left[c] = order.start(mids[c][1], "batch", chip, f"sums_{c}")
+
+    def leave(c, ds, last=False):
+        *gone, total = order.kernel(
+            functools.partial(leave_body, capacity, len(ds), not sums["leave"], last),
+            [out(2 * capacity, width, bf16)] * len(ds) + [out(8, width, f32)],
             (
                 *[arrived[d] for d in ds],
-                keep,
-                exchange(send, "batch", chip),
-                centroid,
-                ln_gain,
-                b_out,
-                *(() if first else (sums,)),
-                *((done[-1][8],) if last else ()),
+                *(mids[c][0], left[c], params),
+                *sums["leave"],
+                *(sums["middle"] if last else ()),
             ),
             "leave",
         )
-        for d, x in zip(ds, sent):
-            replies[d] = x if d == 0 else exchange(x, "expert", d)
-
-    n_all, dz_all, u0, da0, u1, da1 = ([x[i] for x in done] for i in range(2, 8))
-    flops = 8 * len(chunks) * half * width * hidden
-    shares = call(
-        functools.partial(weights_body, len(chunks)),
-        [out(width, hidden, bf16), out(hidden, width, bf16)],
-        (*u1, *da1, *n_all, *dz_all),
+        sums["leave"] = (total,)
+        for d, x in zip(ds, gone):
+            replies[d] = x
+
+    def reply(*ds):
+        for d in ds:
+            replies[d] = order.start(replies[d], "expert", d, f"reply_{d}")
+
+    def replied(*ds):
+        order.wait(*[replies[d] for d in ds])
+
+    per = max(1, 128 // capacity)
+    near, z1, z2, z3 = (list(range(d, d + per)) for d in range(0, experts, per))
+    enter("0a", near[:1])
+    send(*z3)
+    send(*near[1:])
+    sibling = order.start(weights, "batch", core, "weights")
+    sent(*near[1:])
+    enter("0b", near[1:])
+    order.wait(other["0a"])
+    send(z1[0])
+    order.wait(sibling)
+    send(z1[1])
+    order.wait(other["0b"])
+    middle(0, ["0a", "0b"])
+    sent(*z1)
+    enter(1, z1)
+    sent(*z3)
+    send(*z2)
+    enter(3, z3)
+    order.wait(left[0])
+    leave(0, near)
+    reply(*near[1:])
+    order.wait(other[1])
+    middle(1, [1])
+    order.wait(other[3])
+    middle(3, [3])
+    replied(*near[1:])
+    sent(*z2)
+    enter(2, z2)
+    order.wait(left[1])
+    leave(1, z1)
+    reply(*z1)
+    order.wait(other[2])
+    middle(2, [2])
+    order.wait(left[3])
+    leave(3, z3)
+    reply(*z3)
+    own = [mids[c] for c in mids]
+
+    def pick(*which):
+        return [x[i] for i in which for x in own]
+
+    (shares,) = order.kernel(
+        functools.partial(weights_body, len(own)),
+        [out(width + hidden, hidden, bf16)],
+        pick(6, 7, 2, 3),
         "sibling_weights",
-        flops=flops,
-    )
-    shares = [exchange(x, "batch", core) for x in shares]
-    w_in_grad, w_out_grad = call(
-        functools.partial(weights_body, len(chunks)),
+    )
+    replied(*z1)
+    shares = order.start(shares, "batch", core, "grads")
+    order.wait(left[2])
+    leave(2, z2, last=True)
+    order.wait(shares)
+    reply(*z2)
+    total = sums["leave"][0]
+    total_core = order.start(total, "batch", core, "total")
+    order.wait(total_core)
+    b_in_grad = total[4:5] + total_core[5:6]
+    total = total + total_core
+    total_chip = order.start(total, "batch", chip, "total")
+    replied(*z3)
+    w_in_grad, w_out_grad = order.kernel(
+        functools.partial(weights_body, len(own)),
         [out(width, hidden, f32), out(hidden, width, f32)],
-        (*u0, *da0, *n_all, *dz_all, *shares),
+        (*pick(4, 5, 2, 3), shares),
         "own_weights",
-        flops=flops,
-    )
-    sums_core = exchange(sums, "batch", core)
-    b_in_grad = sums[4:5] + sums_core[5:6]
-    sums = sums + sums_core
-    sums = sums + exchange(sums, "batch", chip)
-    mixed, tokens_grad = call(
+    )
+    total = total + total_chip
+    mixed, tokens_grad = order.kernel(
         functools.partial(combine_body, capacity),
         [out(tok_count, width, bf16), out(tok_count, width, f32)],
-        (me, route_row, tokens, cotangent, *[replies[d] for d in range(experts)]),
+        (me, routes_near, tokens_near, cotangent_near, *[replies[d] for d in range(experts)]),
         "combine",
         scalars=1,
-        flops=8 * tok_count * tok_count * width,
     )
     return (
         mixed,
         tokens_grad,
-        sums[0:1],
-        sums[1:2],
-        sums[2:3],
+        total[0:1],
+        total[1:2],
+        total[2:3],
         w_in_grad[None],
         b_in_grad,
         w_out_grad[None],
-        sums[3:4],
+        total[3:4],
     )
 
 

time: 230 us -> 158 us (0.69)
  the two profiles are of different devices: /device:TPU:8 before, /device:TPU:0 now
where the time goes in v2:
time: 158 us
  waiting for transfers between devices  68.5 us (43%)
  Pallas kernels  47.1 us (30%)
  starting transfers between devices  38.3 us (24%)
  local copies, waits for them, and re-layouts  2.8 us (2%)
    ppermute x27, waiting for transfers between devices, start(): return lax.ppermute(x, axis, [(i, i ^ offset) for i in range(size)])  68.5 us
    pallas_call x17, Pallas kernels, call(): pl.pallas_call(run, out_shape=tuple(outs), in_specs=[pl.BlockSpec(memory_...  47.1 us
    ppermute x27, starting transfers between devices, start(): return lax.ppermute(x, axis, [(i, i ^ offset) for i in range(size)])  38.3 us
  transfers between devices with their start and end apart: 27, of which 12 were waited for; matrix products, arithmetic and copies ran while one was open for 1% of the time, Pallas kernels for 27%

profile of v2, /device:TPU:0, one launch (start us, length us, event | category | flops | bytes accessed | tf_op | source)
XLA Modules:
  0.0 158.1 jit_solution(12067897738938343191)
XLA Ops:
  0.7 2.7 %dispatch.1 = (bf16[128,1024]{1,0:T(8,128)(2,1)S(1)}, bf16[128,1024]{1,0:T(8,128)(2,1)S(1)}, bf16[128,1024]{1,0:T(8,128)(2,1)S(1)}, bf16[128,1024]{1,0:T(8,128)(...) custom-call(s32[1]{0:T(128)} %bitcast.refs_0_, ...), custom_call_target="tpu_custom_call" | custom-call | tf_op jit(solution)/shard_map/dispatch/pallas_call | solution.py:198
  4.1 2.6 %collective-permute-start = (bf16[128,1024]{1,0:T(8,128)(2,1)S(1)}, bf16[128,1024]{1,0:T(8,128)(2,1)S(1)}, u32[]{:S(2)}, u32[]{:S(2)}) collective-permute-start(bf16[128,1024]{1,0:T(8,128)(2,1)S(1)} %get-tuple-element.102), channel_id=1, source_target_pairs={{0,4},{4,0},{8,12},{12,8},{16,20},{20,16},{24,28},{28,24},{1,5},{5... | collective-permute-start | bytes 786440 | tf_op jit(solution)/shard_map/out_1/ppermute | solution.py:456
  6.7 1.5 collective-permute-start.1
  8.2 5.4 %collective-permute-done.refs_0_.refs_1_ = bf16[128,1024]{1,0:T(8,128)(2,1)S(1)} collective-permute-done((bf16[128,1024]{1,0:T(8,128)(2,1)S(1)}, bf16[128,1024]{1,0:T(8,128)(2,1)S(1)}, u32[]{:S(2)}, u32[]{:S(2)}) %collective-permute-start) | collective-permute-done | bytes 262176 | tf_op jit(solution)/shard_map/out_1/ppermute | solution.py:456
  13.8 1.8 %collective-permute-start.2 = (bf16[128,1024]{1,0:T(8,128)(2,1)S(1)}, bf16[128,1024]{1,0:T(8,128)(2,1)S(1)}, u32[]{:S(2)}, u32[]{:S(2)}) collective-permute-start(bf16[128,1024]{1,0:T(8,128)(2,1)S(1)} %enter.6.refs_1_), channel_id=1, source_target_pairs={{0,2},{1,3},{2,0},{3,1},{4,6},{5,7},{6,4},{7,5},{8,10},{9,11},{10,... | collective-permute-start | bytes 786440 | tf_op jit(solution)/shard_map/share_0b/ppermute | solution.py:456
  15.6 1.6 collective-permute-start.7
  17.2 1.4 collective-permute-start.8
  18.6 3.6 %collective-permute-start.5 = (bf16[128,1024]{1,0:T(8,128)(2,1)S(1)}, bf16[128,1024]{1,0:T(8,128)(2,1)S(1)}, u32[]{:S(2)}, u32[]{:S(2)}) collective-permute-start(bf16[128,1024]{1,0:T(8,128)(2,1)S(1)} %get-tuple-element.110), channel_id=1, source_target_pairs={{0,24},{4,28},{8,16},{12,20},{16,8},{20,12},{24,0},{28,4},{1,25},{... | collective-permute-start | bytes 786440 | tf_op jit(solution)/shard_map/out_6/ppermute | solution.py:456
  22.4 5.9 %middle.4 = (f32[256,1024]{1,0:T(8,128)S(1)}, bf16[256,1024]{1,0:T(8,128)(2,1)S(1)}, bf16[256,1024]{1,0:T(8,128)(2,1)S(1)}, bf16[256,1024]{1,0:T(8,128)(2,1)S(1)...) custom-call(bf16[128,1024]{1,0:T(8,128)(2,1)S(1)} %enter.5.refs_2_.r, ...), custom_call_target="tpu_custom_call" | custom-call | tf_op jit(solution)/shard_map/middle/pallas_call | solution.py:198
  31.5 7.3 %collective-permute-done.5.refs_0_ = bf16[128,1024]{1,0:T(8,128)(2,1)S(1)} collective-permute-done((bf16[128,1024]{1,0:T(8,128)(2,1)S(1)}, bf16[128,1024]{1,0:T(8,128)(2,1)S(1)}, u32[]{:S(2)}, u32[]{:S(2)}) %collective-permute-start.5) | collective-permute-done | bytes 262176 | tf_op jit(solution)/shard_map/out_6/ppermute | solution.py:456
  38.8 5.0 %collective-permute-done.6.refs_1_ = bf16[128,1024]{1,0:T(8,128)(2,1)S(1)} collective-permute-done((bf16[128,1024]{1,0:T(8,128)(2,1)S(1)}, bf16[128,1024]{1,0:T(8,128)(2,1)S(1)}, u32[]{:S(2)}, u32[]{:S(2)}) %collective-permute-start.6) | collective-permute-done | bytes 262176 | tf_op jit(solution)/shard_map/out_7/ppermute | solution.py:456
  44.8 1.6 %collective-permute-start.12 = (bf16[128,1024]{1,0:T(8,128)(2,1)S(1)}, bf16[128,1024]{1,0:T(8,128)(2,1)S(1)}, u32[]{:S(2)}, u32[]{:S(2)}) collective-permute-start(bf16[128,1024]{1,0:T(8,128)(2,1)S(1)} %get-tuple-element.126), channel_id=1, source_target_pairs={{0,16},{4,20},{8,24},{12,28},{16,0},{20,4},{24,8},{28,12},{1,17},{... | collective-permute-start | bytes 786440 | tf_op jit(solution)/shard_map/out_4/ppermute | solution.py:456
  48.6 1.4 collective-permute-start.9
  50.1 4.4 %collective-permute-done.10.refs_1_ = bf16[256,1024]{1,0:T(8,128)(2,1)S(1)} collective-permute-done((bf16[256,1024]{1,0:T(8,128)(2,1)S(1)}, bf16[256,1024]{1,0:T(8,128)(2,1)S(1)}, u32[]{:S(2)}, u32[]{:S(2)}) %collective-permute-start.10) | collective-permute-done | bytes 524320 | tf_op jit(solution)/shard_map/share_1/ppermute | solution.py:456
  54.5 6.1 %middle.5 = (f32[256,1024]{1,0:T(8,128)S(1)}, bf16[256,1024]{1,0:T(8,128)(2,1)S(1)}, bf16[256,1024]{1,0:T(8,128)(2,1)S(1)}, bf16[256,1024]{1,0:T(8,128)(2,1)S(1)...) custom-call(bf16[256,1024]{1,0:T(8,128)(2,1)S(1)} %enter.7.refs_3_.r, ...), custom_call_target="tpu_custom_call" | custom-call | tf_op jit(solution)/shard_map/middle/pallas_call | solution.py:198
  61.8 3.9 %collective-permute-done.14.refs_1_ = bf16[256,1024]{1,0:T(8,128)(2,1)S(1)} collective-permute-done((bf16[256,1024]{1,0:T(8,128)(2,1)S(1)}, bf16[256,1024]{1,0:T(8,128)(2,1)S(1)}, u32[]{:S(2)}, u32[]{:S(2)}) %collective-permute-start.14) | collective-permute-done | bytes 524320 | tf_op jit(solution)/shard_map/share_3/ppermute | solution.py:456
  65.7 5.9 %middle.6 = (f32[256,1024]{1,0:T(8,128)S(1)}, bf16[256,1024]{1,0:T(8,128)(2,1)S(1)}, bf16[256,1024]{1,0:T(8,128)(2,1)S(1)}, bf16[256,1024]{1,0:T(8,128)(2,1)S(1)...) custom-call(bf16[256,1024]{1,0:T(8,128)(2,1)S(1)} %enter.8.refs_5_.r, ...), custom_call_target="tpu_custom_call" | custom-call | tf_op jit(solution)/shard_map/middle/pallas_call | solution.py:198
  74.1 2.9 %collective-permute-done.11.refs_3_ = bf16[256,1024]{1,0:T(8,128)(2,1)S(1)} collective-permute-done((bf16[256,1024]{1,0:T(8,128)(2,1)S(1)}, bf16[256,1024]{1,0:T(8,128)(2,1)S(1)}, u32[]{:S(2)}, u32[]{:S(2)}) %collective-permute-start.11) | collective-permute-done | bytes 524320 | tf_op jit(solution)/shard_map/sums_1/ppermute | solution.py:456
  77.8 2.2 %collective-permute-start.16 = (bf16[128,1024]{1,0:T(8,128)(2,1)S(1)}, bf16[128,1024]{1,0:T(8,128)(2,1)S(1)}, u32[]{:S(2)}, u32[]{:S(2)}) collective-permute-start(bf16[128,1024]{1,0:T(8,128)(2,1)S(1)} %get-tuple-element.134), channel_id=1, source_target_pairs={{0,12},{4,8},{8,4},{12,0},{16,28},{20,24},{24,20},{28,16},{1,13},{... | collective-permute-start | bytes 786440 | tf_op jit(solution)/shard_map/reply_3/ppermute | solution.py:456
  80.8 7.3 %collective-permute-done.17.refs_1_ = bf16[256,1024]{1,0:T(8,128)(2,1)S(1)} collective-permute-done((bf16[256,1024]{1,0:T(8,128)(2,1)S(1)}, bf16[256,1024]{1,0:T(8,128)(2,1)S(1)}, u32[]{:S(2)}, u32[]{:S(2)}) %collective-permute-start.17) | collective-permute-done | bytes 524320 | tf_op jit(solution)/shard_map/share_2/ppermute | solution.py:456
  88.2 6.2 %middle.7 = (f32[256,1024]{1,0:T(8,128)S(1)}, bf16[256,1024]{1,0:T(8,128)(2,1)S(1)}, bf16[256,1024]{1,0:T(8,128)(2,1)S(1)}, bf16[256,1024]{1,0:T(8,128)(2,1)S(1)...) custom-call(bf16[256,1024]{1,0:T(8,128)(2,1)S(1)} %enter.9.refs_6_.r, ...), custom_call_target="tpu_custom_call" | custom-call | tf_op jit(solution)/shard_map/middle/pallas_call | solution.py:198
  94.4 2.6 %collective-permute-done.19.refs_3_ = bf16[256,1024]{1,0:T(8,128)(2,1)S(1)} collective-permute-done((bf16[256,1024]{1,0:T(8,128)(2,1)S(1)}, bf16[256,1024]{1,0:T(8,128)(2,1)S(1)}, u32[]{:S(2)}, u32[]{:S(2)}) %collective-permute-start.19) | collective-permute-done | bytes 524320 | tf_op jit(solution)/shard_map/sums_3/ppermute | solution.py:456
  97.8 5.2 %sibling_weights.1.refs_7_ = bf16[2048,1024]{1,0:T(8,128)(2,1)S(1)} custom-call(bf16[256,1024]{1,0:T(8,128)(2,1)S(1)} %get-tuple-element.143.refs_0_, bf16[256,1024]{1,0:T(8,128)(2,1)S(1)} %get-tuple-element.144.refs_1_, bf16[256,1024]{1,0:T(8,128)(2,1)S(1)} %get-tuple-element.145.refs_2_, bf16[256,1024]{1,0:T(8,128)(2,1)S(1)} %get-tuple-element.146.refs_3_, ...), custom_call_target="tpu_custom_call" | custom-call | tf_op jit(solution)/shard_map/sibling_weights/pallas_call | solution.py:198
  104.5 4.6 %collective-permute-start.24 = (bf16[128,1024]{1,0:T(8,128)(2,1)S(1)}, bf16[128,1024]{1,0:T(8,128)(2,1)S(1)}, u32[]{:S(2)}, u32[]{:S(2)}) collective-permute-start(bf16[128,1024]{1,0:T(8,128)(2,1)S(1)} %get-tuple-element.168), channel_id=1, source_target_pairs={{0,28},{4,24},{8,20},{12,16},{16,12},{20,8},{24,4},{28,0},{1,29},{... | collective-permute-start | bytes 786440 | tf_op jit(solution)/shard_map/reply_7/ppermute | solution.py:456
  109.2 8.2 %collective-permute-done.18.refs_3_ = bf16[256,1024]{1,0:T(8,128)(2,1)S(1)} collective-permute-done((bf16[256,1024]{1,0:T(8,128)(2,1)S(1)}, bf16[256,1024]{1,0:T(8,128)(2,1)S(1)}, u32[]{:S(2)}, u32[]{:S(2)}) %collective-permute-start.18) | collective-permute-done | bytes 524320 | tf_op jit(solution)/shard_map/sums_2/ppermute | solution.py:456
  118.3 2.5 %collective-permute-start.21 = (bf16[128,1024]{1,0:T(8,128)(2,1)S(1)}, bf16[128,1024]{1,0:T(8,128)(2,1)S(1)}, u32[]{:S(2)}, u32[]{:S(2)}) collective-permute-start(bf16[128,1024]{1,0:T(8,128)(2,1)S(1)} %get-tuple-element.162), channel_id=1, source_target_pairs={{0,16},{4,20},{8,24},{12,28},{16,0},{20,4},{24,8},{28,12},{1,17},{... | collective-permute-start | bytes 786440 | tf_op jit(solution)/shard_map/reply_4/ppermute | solution.py:456
  122.1 1.6 collective-permute-start.26
  124.3 8.5 %own_weights.1 = (f32[1024,1024]{1,0:T(8,128)}, f32[1024,1024]{1,0:T(8,128)}) custom-call(bf16[256,1024]{1,0:T(8,128)(2,1)S(1)} %get-tuple-element.169.refs_0_, bf16[256,1024]{1,0:T(8,128)(2,1)S(1)} %get-tuple-element.170.refs_1_, bf16[256,1024]{1,0:T(8,128)(2,1)S(1)} %get-tuple-element.171.refs_2_, bf16[256,1024]{1,0:T(8,128)(2,1)S(1)} %get-tuple-element.172.refs_3_, ...), custom_call_target="tpu_custom_call" | custom-call | tf_op jit(solution)/shard_map/own_weights/pallas_call | solution.py:198
  133.5 15.8 %collective-permute-done.21.refs_8_ = bf16[128,1024]{1,0:T(8,128)(2,1)S(1)} collective-permute-done((bf16[128,1024]{1,0:T(8,128)(2,1)S(1)}, bf16[128,1024]{1,0:T(8,128)(2,1)S(1)}, u32[]{:S(2)}, u32[]{:S(2)}) %collective-permute-start.21) | collective-permute-done | bytes 262176 | tf_op jit(solution)/shard_map/reply_4/ppermute | solution.py:456
  149.3 4.8 %collective-permute-done.22.refs_9_ = bf16[128,1024]{1,0:T(8,128)(2,1)S(1)} collective-permute-done((bf16[128,1024]{1,0:T(8,128)(2,1)S(1)}, bf16[128,1024]{1,0:T(8,128)(2,1)S(1)}, u32[]{:S(2)}, u32[]{:S(2)}) %collective-permute-start.22) | collective-permute-done | bytes 262176 | tf_op jit(solution)/shard_map/reply_5/ppermute | solution.py:456
  154.1 2.2 %copy-done = f32[1024,1024]{1,0:T(8,128)S(1)} copy-done((f32[1024,1024]{1,0:T(8,128)S(1)}, f32[1024,1024]{1,0:T(8,128)}, u32[]{:S(2)}) %copy-start) | copy-done | bytes 4194328
  156.2 1.8 %combine.1 = (bf16[256,1024]{1,0:T(8,128)(2,1)}, f32[256,1024]{1,0:T(8,128)}) custom-call(s32[1]{0:T(128)} %bitcast.refs_0_, s32[1,256]{1,0:T(1,128)S(1)} %get-tuple-element.96.refs_1_, bf16[256,1024]{1,0:T(8,128)(2,1)S(1)} %get-tuple-element.97.refs_2_, bf16[256,1024]{1,0:T(8,128)(2,1)S(1)} %get-tuple-element.98.refs_3_, ...), custom_call_target="tpu_custom_call" | custom-call | tf_op jit(solution)/shard_map/combine/pallas_call | solution.py:198
  (45 shorter events, 18.7 us)
Async XLA Ops:
  3.6 13.6 %collective-permute-start.3 = (bf16[2064,1024]{1,0:T(8,128)(2,1)S(1)}, bf16[2064,1024]{1,0:T(8,128)(2,1)S(1)}, u32[]{:S(2)}, u32[]{:S(2)}) collective-permute-start(bf16[2064,1024]{1,0:T(8,128)(2,1)S(1)} %get-tuple-element.104.refs_4_.refs_2_), channel_id=1, source_target_pairs={{0,1},{1,0},{2,3},{3,2},{4,5},{5,4},{6,7},{7,6},{8,9},{9,8},{10,11... | collective-permute-start | bytes 12681224 | tf_op jit(solution)/shard_map/weights/ppermute | solution.py:456
  4.1 9.5 %collective-permute-start = (bf16[128,1024]{1,0:T(8,128)(2,1)S(1)}, bf16[128,1024]{1,0:T(8,128)(2,1)S(1)}, u32[]{:S(2)}, u32[]{:S(2)}) collective-permute-start(bf16[128,1024]{1,0:T(8,128)(2,1)S(1)} %get-tuple-element.102), channel_id=1, source_target_pairs={{0,4},{4,0},{8,12},{12,8},{16,20},{20,16},{24,28},{28,24},{1,5},{5... | collective-permute-start | bytes 786440 | tf_op jit(solution)/shard_map/out_1/ppermute | solution.py:456
  6.7 8.9 %collective-permute-start.1 = (bf16[128,1024]{1,0:T(8,128)(2,1)S(1)}, bf16[128,1024]{1,0:T(8,128)(2,1)S(1)}, u32[]{:S(2)}, u32[]{:S(2)}) collective-permute-start(bf16[128,1024]{1,0:T(8,128)(2,1)S(1)} %enter.5.refs_2_.refs_0_), channel_id=1, source_target_pairs={{0,2},{1,3},{2,0},{3,1},{4,6},{5,7},{6,4},{7,5},{8,10},{9,11},{10,... | collective-permute-start | bytes 786440 | tf_op jit(solution)/shard_map/share_0a/ppermute | solution.py:456
  13.8 8.6 %collective-permute-start.2 = (bf16[128,1024]{1,0:T(8,128)(2,1)S(1)}, bf16[128,1024]{1,0:T(8,128)(2,1)S(1)}, u32[]{:S(2)}, u32[]{:S(2)}) collective-permute-start(bf16[128,1024]{1,0:T(8,128)(2,1)S(1)} %enter.6.refs_1_), channel_id=1, source_target_pairs={{0,2},{1,3},{2,0},{3,1},{4,6},{5,7},{6,4},{7,5},{8,10},{9,11},{10,... | collective-permute-start | bytes 786440 | tf_op jit(solution)/shard_map/share_0b/ppermute | solution.py:456
  15.6 13.9 %collective-permute-start.7 = (bf16[128,1024]{1,0:T(8,128)(2,1)S(1)}, bf16[128,1024]{1,0:T(8,128)(2,1)S(1)}, u32[]{:S(2)}, u32[]{:S(2)}) collective-permute-start(bf16[128,1024]{1,0:T(8,128)(2,1)S(1)} %get-tuple-element.114), channel_id=1, source_target_pairs={{0,8},{4,12},{8,0},{12,4},{16,24},{20,28},{24,16},{28,20},{1,9},{5... | collective-permute-start | bytes 786440 | tf_op jit(solution)/shard_map/out_2/ppermute | solution.py:456
  17.2 13.1 %collective-permute-start.8 = (bf16[128,1024]{1,0:T(8,128)(2,1)S(1)}, bf16[128,1024]{1,0:T(8,128)(2,1)S(1)}, u32[]{:S(2)}, u32[]{:S(2)}) collective-permute-start(bf16[128,1024]{1,0:T(8,128)(2,1)S(1)} %get-tuple-element.116), channel_id=1, source_target_pairs={{0,12},{4,8},{8,4},{12,0},{16,28},{20,24},{24,20},{28,16},{1,13},{... | collective-permute-start | bytes 786440 | tf_op jit(solution)/shard_map/out_3/ppermute | solution.py:456
  18.6 20.2 %collective-permute-start.5 = (bf16[128,1024]{1,0:T(8,128)(2,1)S(1)}, bf16[128,1024]{1,0:T(8,128)(2,1)S(1)}, u32[]{:S(2)}, u32[]{:S(2)}) collective-permute-start(bf16[128,1024]{1,0:T(8,128)(2,1)S(1)} %get-tuple-element.110), channel_id=1, source_target_pairs={{0,24},{4,28},{8,16},{12,20},{16,8},{20,12},{24,0},{28,4},{1,25},{... | collective-permute-start | bytes 786440 | tf_op jit(solution)/shard_map/out_6/ppermute | solution.py:456
  22.2 21.6 %collective-permute-start.6 = (bf16[128,1024]{1,0:T(8,128)(2,1)S(1)}, bf16[128,1024]{1,0:T(8,128)(2,1)S(1)}, u32[]{:S(2)}, u32[]{:S(2)}) collective-permute-start(bf16[128,1024]{1,0:T(8,128)(2,1)S(1)} %get-tuple-element.112), channel_id=1, source_target_pairs={{0,28},{4,24},{8,20},{12,16},{16,12},{20,8},{24,4},{28,0},{1,29},{... | collective-permute-start | bytes 786440 | tf_op jit(solution)/shard_map/out_7/ppermute | solution.py:456
  28.3 19.5 %collective-permute-start.4 = (bf16[256,1024]{1,0:T(8,128)(2,1)S(1)}, bf16[256,1024]{1,0:T(8,128)(2,1)S(1)}, u32[]{:S(2)}, u32[]{:S(2)}) collective-permute-start(bf16[256,1024]{1,0:T(8,128)(2,1)S(1)} %get-tuple-element.108), channel_id=1, source_target_pairs={{0,2},{1,3},{2,0},{3,1},{4,6},{5,7},{6,4},{7,5},{8,10},{9,11},{10,... | collective-permute-start | bytes 1572872 | tf_op jit(solution)/shard_map/sums_0/ppermute | solution.py:456
  30.6 23.9 %collective-permute-start.10 = (bf16[256,1024]{1,0:T(8,128)(2,1)S(1)}, bf16[256,1024]{1,0:T(8,128)(2,1)S(1)}, u32[]{:S(2)}, u32[]{:S(2)}) collective-permute-start(bf16[256,1024]{1,0:T(8,128)(2,1)S(1)} %enter.7.refs_3_.refs_0_), channel_id=1, source_target_pairs={{0,2},{1,3},{2,0},{3,1},{4,6},{5,7},{6,4},{7,5},{8,10},{9,11},{10,... | collective-permute-start | bytes 1572872 | tf_op jit(solution)/shard_map/share_1/ppermute | solution.py:456
  44.1 21.6 %collective-permute-start.14 = (bf16[256,1024]{1,0:T(8,128)(2,1)S(1)}, bf16[256,1024]{1,0:T(8,128)(2,1)S(1)}, u32[]{:S(2)}, u32[]{:S(2)}) collective-permute-start(bf16[256,1024]{1,0:T(8,128)(2,1)S(1)} %enter.8.refs_5_.refs_0_), channel_id=1, source_target_pairs={{0,2},{1,3},{2,0},{3,1},{4,6},{5,7},{6,4},{7,5},{8,10},{9,11},{10,... | collective-permute-start | bytes 1572872 | tf_op jit(solution)/shard_map/share_3/ppermute | solution.py:456
  44.8 26.9 %collective-permute-start.12 = (bf16[128,1024]{1,0:T(8,128)(2,1)S(1)}, bf16[128,1024]{1,0:T(8,128)(2,1)S(1)}, u32[]{:S(2)}, u32[]{:S(2)}) collective-permute-start(bf16[128,1024]{1,0:T(8,128)(2,1)S(1)} %get-tuple-element.126), channel_id=1, source_target_pairs={{0,16},{4,20},{8,24},{12,28},{16,0},{20,4},{24,8},{28,12},{1,17},{... | collective-permute-start | bytes 786440 | tf_op jit(solution)/shard_map/out_4/ppermute | solution.py:456
  46.4 25.3 %collective-permute-start.13 = (bf16[128,1024]{1,0:T(8,128)(2,1)S(1)}, bf16[128,1024]{1,0:T(8,128)(2,1)S(1)}, u32[]{:S(2)}, u32[]{:S(2)}) collective-permute-start(bf16[128,1024]{1,0:T(8,128)(2,1)S(1)} %get-tuple-element.128), channel_id=1, source_target_pairs={{0,20},{4,16},{8,28},{12,24},{16,4},{20,0},{24,12},{28,8},{1,21},{... | collective-permute-start | bytes 786440 | tf_op jit(solution)/shard_map/out_5/ppermute | solution.py:456
  48.6 23.0 %collective-permute-start.9 = (bf16[128,1024]{1,0:T(8,128)(2,1)S(1)}, bf16[128,1024]{1,0:T(8,128)(2,1)S(1)}, u32[]{:S(2)}, u32[]{:S(2)}) collective-permute-start(bf16[128,1024]{1,0:T(8,128)(2,1)S(1)} %get-tuple-element.120), channel_id=1, source_target_pairs={{0,4},{4,0},{8,12},{12,8},{16,20},{20,16},{24,28},{28,24},{1,5},{5... | collective-permute-start | bytes 786440 | tf_op jit(solution)/shard_map/reply_1/ppermute | solution.py:456
  60.6 16.3 %collective-permute-start.11 = (bf16[256,1024]{1,0:T(8,128)(2,1)S(1)}, bf16[256,1024]{1,0:T(8,128)(2,1)S(1)}, u32[]{:S(2)}, u32[]{:S(2)}) collective-permute-start(bf16[256,1024]{1,0:T(8,128)(2,1)S(1)} %get-tuple-element.124), channel_id=1, source_target_pairs={{0,2},{1,3},{2,0},{3,1},{4,6},{5,7},{6,4},{7,5},{8,10},{9,11},{10,... | collective-permute-start | bytes 1572872 | tf_op jit(solution)/shard_map/sums_1/ppermute | solution.py:456
  72.0 16.2 %collective-permute-start.17 = (bf16[256,1024]{1,0:T(8,128)(2,1)S(1)}, bf16[256,1024]{1,0:T(8,128)(2,1)S(1)}, u32[]{:S(2)}, u32[]{:S(2)}) collective-permute-start(bf16[256,1024]{1,0:T(8,128)(2,1)S(1)} %enter.9.refs_6_.refs_0_), channel_id=1, source_target_pairs={{0,2},{1,3},{2,0},{3,1},{4,6},{5,7},{6,4},{7,5},{8,10},{9,11},{10,... | collective-permute-start | bytes 1572872 | tf_op jit(solution)/shard_map/share_2/ppermute | solution.py:456
  73.2 23.8 %collective-permute-start.19 = (bf16[256,1024]{1,0:T(8,128)(2,1)S(1)}, bf16[256,1024]{1,0:T(8,128)(2,1)S(1)}, u32[]{:S(2)}, u32[]{:S(2)}) collective-permute-start(bf16[256,1024]{1,0:T(8,128)(2,1)S(1)} %get-tuple-element.141), channel_id=1, source_target_pairs={{0,2},{1,3},{2,0},{3,1},{4,6},{5,7},{6,4},{7,5},{8,10},{9,11},{10,... | collective-permute-start | bytes 1572872 | tf_op jit(solution)/shard_map/sums_3/ppermute | solution.py:456
  77.8 25.2 %collective-permute-start.16 = (bf16[128,1024]{1,0:T(8,128)(2,1)S(1)}, bf16[128,1024]{1,0:T(8,128)(2,1)S(1)}, u32[]{:S(2)}, u32[]{:S(2)}) collective-permute-start(bf16[128,1024]{1,0:T(8,128)(2,1)S(1)} %get-tuple-element.134), channel_id=1, source_target_pairs={{0,12},{4,8},{8,4},{12,0},{16,28},{20,24},{24,20},{28,16},{1,13},{... | collective-permute-start | bytes 786440 | tf_op jit(solution)/shard_map/reply_3/ppermute | solution.py:456
  80.0 23.0 %collective-permute-start.15 = (bf16[128,1024]{1,0:T(8,128)(2,1)S(1)}, bf16[128,1024]{1,0:T(8,128)(2,1)S(1)}, u32[]{:S(2)}, u32[]{:S(2)}) collective-permute-start(bf16[128,1024]{1,0:T(8,128)(2,1)S(1)} %get-tuple-element.132), channel_id=1, source_target_pairs={{0,8},{4,12},{8,0},{12,4},{16,24},{20,28},{24,16},{28,20},{1,9},{5... | collective-permute-start | bytes 786440 | tf_op jit(solution)/shard_map/reply_2/ppermute | solution.py:456
  103.0 15.3 %collective-permute-start.20 = (bf16[2048,1024]{1,0:T(8,128)(2,1)S(1)}, bf16[2048,1024]{1,0:T(8,128)(2,1)S(1)}, u32[]{:S(2)}, u32[]{:S(2)}) collective-permute-start(bf16[2048,1024]{1,0:T(8,128)(2,1)S(1)} %sibling_weights.1.refs_7_), channel_id=1, source_target_pairs={{0,1},{1,0},{2,3},{3,2},{4,5},{5,4},{6,7},{7,6},{8,9},{9,8},{10,11... | collective-permute-start | bytes 12582920 | tf_op jit(solution)/shard_map/grads/ppermute | solution.py:456
  103.1 14.3 %collective-permute-start.18 = (bf16[256,1024]{1,0:T(8,128)(2,1)S(1)}, bf16[256,1024]{1,0:T(8,128)(2,1)S(1)}, u32[]{:S(2)}, u32[]{:S(2)}) collective-permute-start(bf16[256,1024]{1,0:T(8,128)(2,1)S(1)} %get-tuple-element.138), channel_id=1, source_target_pairs={{0,2},{1,3},{2,0},{3,1},{4,6},{5,7},{6,4},{7,5},{8,10},{9,11},{10,... | collective-permute-start | bytes 1572872 | tf_op jit(solution)/shard_map/sums_2/ppermute | solution.py:456
  104.5 19.8 %collective-permute-start.24 = (bf16[128,1024]{1,0:T(8,128)(2,1)S(1)}, bf16[128,1024]{1,0:T(8,128)(2,1)S(1)}, u32[]{:S(2)}, u32[]{:S(2)}) collective-permute-start(bf16[128,1024]{1,0:T(8,128)(2,1)S(1)} %get-tuple-element.168), channel_id=1, source_target_pairs={{0,28},{4,24},{8,20},{12,16},{16,12},{20,8},{24,4},{28,0},{1,29},{... | collective-permute-start | bytes 786440 | tf_op jit(solution)/shard_map/reply_7/ppermute | solution.py:456
  109.0 15.3 %collective-permute-start.23 = (bf16[128,1024]{1,0:T(8,128)(2,1)S(1)}, bf16[128,1024]{1,0:T(8,128)(2,1)S(1)}, u32[]{:S(2)}, u32[]{:S(2)}) collective-permute-start(bf16[128,1024]{1,0:T(8,128)(2,1)S(1)} %get-tuple-element.166), channel_id=1, source_target_pairs={{0,24},{4,28},{8,16},{12,20},{16,8},{20,12},{24,0},{28,4},{1,25},{... | collective-permute-start | bytes 786440 | tf_op jit(solution)/shard_map/reply_6/ppermute | solution.py:456
  118.3 3.9 %collective-permute-start.25 = (f32[8,1024]{1,0:T(8,128)S(1)}, f32[8,1024]{1,0:T(8,128)S(1)}, u32[]{:S(2)}, u32[]{:S(2)}) collective-permute-start(f32[8,1024]{1,0:T(8,128)S(1)} %get-tuple-element.177.refs_17_), channel_id=1, source_target_pairs={{0,1},{1,0},{2,3},{3,2},{4,5},{5,4},{6,7},{7,6},{8,9},{9,8},{10,11... | collective-permute-start | bytes 98312 | tf_op jit(solution)/shard_map/total/ppermute | solution.py:456
  118.3 30.9 %collective-permute-start.21 = (bf16[128,1024]{1,0:T(8,128)(2,1)S(1)}, bf16[128,1024]{1,0:T(8,128)(2,1)S(1)}, u32[]{:S(2)}, u32[]{:S(2)}) collective-permute-start(bf16[128,1024]{1,0:T(8,128)(2,1)S(1)} %get-tuple-element.162), channel_id=1, source_target_pairs={{0,16},{4,20},{8,24},{12,28},{16,0},{20,4},{24,8},{28,12},{1,17},{... | collective-permute-start | bytes 786440 | tf_op jit(solution)/shard_map/reply_4/ppermute | solution.py:456
  120.8 33.2 %collective-permute-start.22 = (bf16[128,1024]{1,0:T(8,128)(2,1)S(1)}, bf16[128,1024]{1,0:T(8,128)(2,1)S(1)}, u32[]{:S(2)}, u32[]{:S(2)}) collective-permute-start(bf16[128,1024]{1,0:T(8,128)(2,1)S(1)} %get-tuple-element.164), channel_id=1, source_target_pairs={{0,20},{4,16},{8,28},{12,24},{16,4},{20,0},{24,12},{28,8},{1,21},{... | collective-permute-start | bytes 786440 | tf_op jit(solution)/shard_map/reply_5/ppermute | solution.py:456
  122.1 10.7 %collective-permute-start.26 = (f32[8,1024]{1,0:T(8,128)S(1)}, f32[8,1024]{1,0:T(8,128)S(1)}, u32[]{:S(2)}, u32[]{:S(2)}) collective-permute-start(f32[8,1024]{1,0:T(8,128)S(1)} %add.9), channel_id=1, source_target_pairs={{0,2},{1,3},{2,0},{3,1},{4,6},{5,7},{6,4},{7,5},{8,10},{9,11},{10,... | collective-permute-start | bytes 98312 | tf_op jit(solution)/shard_map/total/ppermute | solution.py:456
  154.1 2.2 %copy-start = (f32[1024,1024]{1,0:T(8,128)S(1)}, f32[1024,1024]{1,0:T(8,128)}, u32[]{:S(2)}) copy-start(f32[1024,1024]{1,0:T(8,128)} %get-tuple-element.178.refs_12_) | copy-start | bytes 12582916

commit v3 on v2

--- a/solution.py
+++ b/solution.py
@@ -412,12 +412,14 @@
                 jnp.concatenate([x[:, pl.ds(at, step)] for x in left], axis=0),
                 jnp.concatenate([x[...] for x in right], axis=0),
             )
-            if len(rest) == 3:
+            if len(rest) == 4:
                 total = total + rest[0][pl.ds(k * width + at, step), :].astype(f32)
             grad[pl.ds(offset + at, step), :] = total.astype(grad.dtype)
             return unused
 
         lax.fori_loop(0, size // step, some, 0)
+    if len(rest) == 4:
+        rest[3][...] = jnp.zeros_like(rest[3])
 
 
 def combine_body(capacity, me, routes, tokens, cotangent, *refs):
@@ -447,16 +449,120 @@
         self.fence = [got[-1]]
         return got
 
-    def start(self, x, axis, offset, name="rows"):
+    def start(self, x, axis, offset, what, index=None):
         others = [y for y in self.fence if y is not x]
         if others:
             x = lax.optimization_barrier((x, *others))[0]
         size = lax.axis_size(axis)
-        with jax.named_scope(name):
+        with jax.named_scope(f"t{what}_{offset if index is None else index}"):
             return lax.ppermute(x, axis, [(i, i ^ offset) for i in range(size)])
 
-    def wait(self, *arrays):
-        self.fence = self.fence + list(arrays)
+    def wait(self, array):
+        self.fence = self.fence + [array]
+
+
+(
+    DISPATCH,
+    ENTER,
+    MIDDLE,
+    LEAVE,
+    SIBLING,
+    OWN,
+    ADD,
+    FINISH,
+    COMBINE,
+    ROWS,
+    SHARE,
+    SUMS,
+    REPLY,
+    WEIGHTS,
+    GRADS,
+    TOTAL,
+    BOTH,
+    PARAMS,
+    NEAR,
+    BIAS,
+) = range(20)
+RUN, SEND, WAIT = range(3)
+
+shares = ((0,), (6,), (1, 5), (2, 4), (3, 7))
+chunks = ((0, 1), (2,), (3,), (4,))
+
+plan = (
+    (RUN, DISPATCH, 0),
+    (SEND, ROWS, 4),
+    (SEND, ROWS, 5),
+    (SEND, WEIGHTS, 0),
+    (SEND, ROWS, 2),
+    (RUN, ENTER, 0),
+    (SEND, SHARE, 0),
+    (WAIT, WEIGHTS, 0),
+    (SEND, ROWS, 1),
+    (SEND, ROWS, 6),
+    (SEND, ROWS, 3),
+    (WAIT, ROWS, 4),
+    (WAIT, ROWS, 2),
+    (RUN, ENTER, 3),
+    (SEND, SHARE, 3),
+    (SEND, ROWS, 7),
+    (WAIT, SHARE, 0),
+    (WAIT, ROWS, 1),
+    (WAIT, ROWS, 5),
+    (RUN, ENTER, 2),
+    (SEND, SHARE, 2),
+    (WAIT, SHARE, 3),
+    (RUN, MIDDLE, 2),
+    (SEND, SUMS, 2),
+    (WAIT, SHARE, 2),
+    (RUN, MIDDLE, 1),
+    (SEND, SUMS, 1),
+    (WAIT, ROWS, 6),
+    (RUN, ENTER, 1),
+    (WAIT, ROWS, 3),
+    (SEND, SHARE, 1),
+    (WAIT, SHARE, 1),
+    (WAIT, ROWS, 7),
+    (RUN, ENTER, 4),
+    (SEND, SHARE, 4),
+    (WAIT, SUMS, 2),
+    (RUN, LEAVE, 2),
+    (SEND, REPLY, 2),
+    (SEND, REPLY, 4),
+    (WAIT, SUMS, 1),
+    (RUN, LEAVE, 1),
+    (SEND, REPLY, 5),
+    (RUN, MIDDLE, 0),
+    (SEND, REPLY, 1),
+    (WAIT, REPLY, 4),
+    (SEND, SUMS, 0),
+    (WAIT, SHARE, 4),
+    (RUN, MIDDLE, 3),
+    (SEND, SUMS, 3),
+    (RUN, SIBLING, 0),
+    (WAIT, SUMS, 0),
+    (WAIT, REPLY, 5),
+    (SEND, GRADS, 0),
+    (RUN, LEAVE, 0),
+    (SEND, REPLY, 6),
+    (WAIT, REPLY, 1),
+    (WAIT, REPLY, 2),
+    (WAIT, SUMS, 3),
+    (RUN, LEAVE, 3),
+    (SEND, REPLY, 7),
+    (SEND, TOTAL, 0),
+    (WAIT, GRADS, 0),
+    (SEND, REPLY, 3),
+    (WAIT, TOTAL, 0),
+    (RUN, ADD, 0),
+    (SEND, BOTH, 0),
+    (WAIT, REPLY, 6),
+    (RUN, OWN, 0),
+    (WAIT, REPLY, 7),
+    (WAIT, BOTH, 0),
+    (WAIT, REPLY, 3),
+    (RUN, FINISH, 0),
+    (RUN, COMBINE, 0),
+)
 
 
 def local_paired(tokens, routes, centroid, ln_gain, ln_bias, w_in, b_in, w_out, b_out, cotangent):
@@ -467,175 +573,161 @@
     core, chip = 1, 2
     order = Order()
     me = lax.axis_index("expert").astype(jnp.int32).reshape(1)
-    *parts, weights, params, tokens_near, cotangent_near, routes_near = order.kernel(
-        functools.partial(dispatch_body, capacity, experts),
-        [out(2 * capacity, width, bf16)] * experts
-        + [
-            out(width + hidden + 16, hidden, bf16),
-            out(8, width, f32),
-            out(tok_count, width, bf16),
-            out(tok_count, width, bf16),
-            out(1, tok_count, jnp.int32),
-        ],
-        (
-            *(me, routes.reshape(1, tok_count), tokens, cotangent, w_in[0], w_out[0], b_in),
-            *(centroid, ln_gain, ln_bias, b_out),
-        ),
-        "dispatch",
-        scalars=1,
-        far=10,
-        scratch=[pltpu.SemaphoreType.DMA((10,))]
-        + [pltpu.VMEM((1, x.shape[1]), bf16) for x in (b_in, centroid, ln_gain, ln_bias, b_out)],
-    )
-    order.fence = [params]
-    arrived = {0: parts[0]}
-    both, other, mids, replies, left = {}, {}, {}, {}, {}
-    sums = {"middle": (), "leave": ()}
-
-    def send(*ds):
-        for d in ds:
-            arrived[d] = order.start(parts[d], "expert", d, f"out_{d}")
-
-    def sent(*ds):
-        order.wait(*[arrived[d] for d in ds])
-
-    def enter(c, ds):
-        both[c] = order.kernel(
+    made, moved = {}, {}
+    sums = {MIDDLE: (), LEAVE: ()}
+    final = [index for kind, what, index in plan if what == LEAVE and kind == RUN][-1]
+
+    def dispatch(index):
+        *parts, weights, params, tokens_near, cotangent_near, routes_near = order.kernel(
+            functools.partial(dispatch_body, capacity, experts),
+            [out(2 * capacity, width, bf16)] * experts
+            + [
+                out(width + hidden + 16, hidden, bf16),
+                out(8, width, f32),
+                out(tok_count, width, bf16),
+                out(tok_count, width, bf16),
+                out(1, tok_count, jnp.int32),
+            ],
+            (
+                *(me, routes.reshape(1, tok_count), tokens, cotangent, w_in[0], w_out[0], b_in),
+                *(centroid, ln_gain, ln_bias, b_out),
+            ),
+            "dispatch",
+            scalars=1,
+            far=10,
+            scratch=[pltpu.SemaphoreType.DMA((10,))]
+            + [pltpu.VMEM((1, x.shape[1]), bf16) for x in (b_in, centroid, ln_gain, ln_bias, b_out)],
+        )
+        order.fence = [params]
+        for d, part in enumerate(parts):
+            made[ROWS, d] = part
+        moved[ROWS, 0] = parts[0]
+        made[WEIGHTS, 0] = weights
+        made[PARAMS] = params
+        made[NEAR] = (me, routes_near, tokens_near, cotangent_near)
+
+    def enter(index):
+        ds = shares[index]
+        made[SHARE, index] = order.kernel(
             functools.partial(enter_body, capacity, len(ds)),
             [out(2 * len(ds) * capacity, width, bf16)],
-            (*[arrived[d] for d in ds], params),
+            (*[moved[ROWS, d] for d in ds], made[PARAMS]),
             "enter",
         )[0]
-        other[c] = order.start(both[c], "batch", chip, f"share_{c}")
-
-    def middle(c, cs):
-        half = sum(both[i].shape[0] for i in cs) // 2
-        mids[c] = order.kernel(
-            functools.partial(middle_body, len(cs), half, not sums["middle"]),
+
+    def middle(index):
+        own = [made[SHARE, i] for i in chunks[index]]
+        half = sum(x.shape[0] for x in own) // 2
+        got = order.kernel(
+            functools.partial(middle_body, len(own), half, not sums[MIDDLE]),
             [out(2 * half, width, f32), out(2 * half, width, bf16)]
             + [out(2 * half, width, bf16)] * 2
             + [out(2 * half, hidden, bf16)] * 4
             + [out(8, hidden, f32)],
             (
-                *[both[i] for i in cs],
-                *[other[i] for i in cs],
-                *(weights, sibling),
-                *sums["middle"],
+                *own,
+                *[moved[SHARE, i] for i in chunks[index]],
+                *(made[WEIGHTS, 0], moved[WEIGHTS, 0]),
+                *sums[MIDDLE],
             ),
             "middle",
             scratch=[pltpu.VMEM((2 * half, width), f32)] * 2,
             limit=24 << 20,
         )
-        sums["middle"] = (mids[c][8],)
-        left[c] = order.start(mids[c][1], "batch", chip, f"sums_{c}")
-
-    def leave(c, ds, last=False):
+        sums[MIDDLE] = (got[8],)
+        made[MIDDLE, index] = got
+        made[SUMS, index] = got[1]
+
+    def leave(index):
+        ds = [d for i in chunks[index] for d in shares[i]]
         *gone, total = order.kernel(
-            functools.partial(leave_body, capacity, len(ds), not sums["leave"], last),
+            functools.partial(leave_body, capacity, len(ds), not sums[LEAVE], index == final),
             [out(2 * capacity, width, bf16)] * len(ds) + [out(8, width, f32)],
             (
-                *[arrived[d] for d in ds],
-                *(mids[c][0], left[c], params),
-                *sums["leave"],
-                *(sums["middle"] if last else ()),
+                *[moved[ROWS, d] for d in ds],
+                *(made[MIDDLE, index][0], moved[SUMS, index], made[PARAMS]),
+                *sums[LEAVE],
+                *(sums[MIDDLE] if index == final else ()),
             ),
             "leave",
         )
-        sums["leave"] = (total,)
+        sums[LEAVE] = (total,)
         for d, x in zip(ds, gone):
-            replies[d] = x
-
-    def reply(*ds):
-        for d in ds:
-            replies[d] = order.start(replies[d], "expert", d, f"reply_{d}")
-
-    def replied(*ds):
-        order.wait(*[replies[d] for d in ds])
-
-    per = max(1, 128 // capacity)
-    near, z1, z2, z3 = (list(range(d, d + per)) for d in range(0, experts, per))
-    enter("0a", near[:1])
-    send(*z3)
-    send(*near[1:])
-    sibling = order.start(weights, "batch", core, "weights")
-    sent(*near[1:])
-    enter("0b", near[1:])
-    order.wait(other["0a"])
-    send(z1[0])
-    order.wait(sibling)
-    send(z1[1])
-    order.wait(other["0b"])
-    middle(0, ["0a", "0b"])
-    sent(*z1)
-    enter(1, z1)
-    sent(*z3)
-    send(*z2)
-    enter(3, z3)
-    order.wait(left[0])
-    leave(0, near)
-    reply(*near[1:])
-    order.wait(other[1])
-    middle(1, [1])
-    order.wait(other[3])
-    middle(3, [3])
-    replied(*near[1:])
-    sent(*z2)
-    enter(2, z2)
-    order.wait(left[1])
-    leave(1, z1)
-    reply(*z1)
-    order.wait(other[2])
-    middle(2, [2])
-    order.wait(left[3])
-    leave(3, z3)
-    reply(*z3)
-    own = [mids[c] for c in mids]
+            made[REPLY, d] = x
+            if d == 0:
+                moved[REPLY, d] = x
+        made[TOTAL, 0] = total
+
+    done = [index for kind, what, index in plan if what == MIDDLE and kind == RUN]
 
     def pick(*which):
-        return [x[i] for i in which for x in own]
-
-    (shares,) = order.kernel(
-        functools.partial(weights_body, len(own)),
-        [out(width + hidden, hidden, bf16)],
-        pick(6, 7, 2, 3),
-        "sibling_weights",
-    )
-    replied(*z1)
-    shares = order.start(shares, "batch", core, "grads")
-    order.wait(left[2])
-    leave(2, z2, last=True)
-    order.wait(shares)
-    reply(*z2)
-    total = sums["leave"][0]
-    total_core = order.start(total, "batch", core, "total")
-    order.wait(total_core)
-    b_in_grad = total[4:5] + total_core[5:6]
-    total = total + total_core
-    total_chip = order.start(total, "batch", chip, "total")
-    replied(*z3)
-    w_in_grad, w_out_grad = order.kernel(
-        functools.partial(weights_body, len(own)),
-        [out(width, hidden, f32), out(hidden, width, f32)],
-        (*pick(4, 5, 2, 3), shares),
-        "own_weights",
-    )
-    total = total + total_chip
-    mixed, tokens_grad = order.kernel(
-        functools.partial(combine_body, capacity),
-        [out(tok_count, width, bf16), out(tok_count, width, f32)],
-        (me, routes_near, tokens_near, cotangent_near, *[replies[d] for d in range(experts)]),
-        "combine",
-        scalars=1,
-    )
+        return [made[MIDDLE, c][i] for i in which for c in done]
+
+    def sibling(index):
+        (made[GRADS, 0],) = order.kernel(
+            functools.partial(weights_body, len(pick(2))),
+            [out(width + hidden, hidden, bf16)],
+            pick(6, 7, 2, 3),
+            "sibling_weights",
+        )
+
+    def own(index):
+        made[OWN] = order.kernel(
+            functools.partial(weights_body, len(pick(2))),
+            [out(width, hidden, f32), out(hidden, width, f32), out(8, 128, f32)],
+            (*pick(4, 5, 2, 3), moved[GRADS, 0]),
+            "own_weights",
+        )
+
+    def add(index):
+        total, came = made[TOTAL, 0], moved[TOTAL, 0]
+        made[BIAS] = total[4:5] + came[5:6]
+        made[BOTH, 0] = total + came
+
+    def finish(index):
+        made[FINISH] = made[BOTH, 0] + moved[BOTH, 0]
+
+    def combine(index):
+        made[COMBINE] = order.kernel(
+            functools.partial(combine_body, capacity),
+            [out(tok_count, width, bf16), out(tok_count, width, f32)],
+            (*made[NEAR], *[moved[REPLY, d] for d in range(experts)]),
+            "combine",
+            scalars=1,
+        )
+
+    kernels = {
+        DISPATCH: dispatch,
+        ENTER: enter,
+        MIDDLE: middle,
+        LEAVE: leave,
+        SIBLING: sibling,
+        OWN: own,
+        ADD: add,
+        FINISH: finish,
+        COMBINE: combine,
+    }
+    for kind, what, index in plan:
+        if kind == RUN:
+            kernels[what](index)
+        elif kind == WAIT:
+            order.wait(moved[what, index])
+        elif what in (ROWS, REPLY):
+            moved[what, index] = order.start(made[what, index], "expert", index, what)
+        else:
+            offset = core if what in (WEIGHTS, GRADS, TOTAL) else chip
+            moved[what, index] = order.start(made[what, index], "batch", offset, what, index)
+    mixed, tokens_grad = made[COMBINE]
+    total = made[FINISH]
     return (
         mixed,
         tokens_grad,
         total[0:1],
         total[1:2],
         total[2:3],
-        w_in_grad[None],
-        b_in_grad,
-        w_out_grad[None],
+        made[OWN][0][None],
+        made[BIAS],
+        made[OWN][1][None],
         total[3:4],
     )
 
@@ -647,6 +739,7 @@
     power_of_two = experts & (experts - 1) == 0
     paired = (
         lax.axis_size("batch") == 4
+        and experts == sum(len(ds) for ds in shares)
         and power_of_two
         and capacity % 16 == 0
         and capacity <= 128

time: 158 us -> 135 us (0.85)
  the two profiles are of different devices: /device:TPU:0 before, /device:TPU:8 now
where the time goes in v3:
time: 135 us
  waiting for transfers between devices  49 us (36%)
  Pallas kernels  46.1 us (34%)
  starting transfers between devices  37.8 us (28%)
    ppermute x27, waiting for transfers between devices, start(): return lax.ppermute(x, axis, [(i, i ^ offset) for i in range(size)])  49 us
    pallas_call x17, Pallas kernels, call(): pl.pallas_call(run, out_shape=tuple(outs), in_specs=[pl.BlockSpec(memory_...  46.1 us
    ppermute x27, starting transfers between devices, start(): return lax.ppermute(x, axis, [(i, i ^ offset) for i in range(size)])  37.8 us
  transfers between devices with their start and end apart: 27, of which 15 were waited for; matrix products, arithmetic and copies ran while one was open for 1% of the time, Pallas kernels for 31%

profile of v3, /device:TPU:8, one launch (start us, length us, event | category | flops | bytes accessed | tf_op | source)
XLA Modules:
  0.0 135.0 jit_solution(9648779219626748416)
XLA Ops:
  0.7 2.7 %dispatch.1 = (bf16[128,1024]{1,0:T(8,128)(2,1)S(1)}, bf16[128,1024]{1,0:T(8,128)(2,1)S(1)}, bf16[128,1024]{1,0:T(8,128)(2,1)S(1)}, bf16[128,1024]{1,0:T(8,128)(...) custom-call(s32[1]{0:T(128)} %bitcast.refs_0_, ...), custom_call_target="tpu_custom_call" | custom-call | tf_op jit(solution)/shard_map/dispatch/pallas_call | solution.py:198
  3.4 2.7 %collective-permute-start.5 = (bf16[128,1024]{1,0:T(8,128)(2,1)S(1)}, bf16[128,1024]{1,0:T(8,128)(2,1)S(1)}, u32[]{:S(2)}, u32[]{:S(2)}) collective-permute-start(bf16[128,1024]{1,0:T(8,128)(2,1)S(1)} %get-tuple-element.113), channel_id=1, source_target_pairs={{0,16},{4,20},{8,24},{12,28},{16,0},{20,4},{24,8},{28,12},{1,17},{... | collective-permute-start | bytes 786440 | tf_op jit(solution)/shard_map/t9_4/ppermute | solution.py:458
  6.8 1.6 %collective-permute-start.6 = (bf16[128,1024]{1,0:T(8,128)(2,1)S(1)}, bf16[128,1024]{1,0:T(8,128)(2,1)S(1)}, u32[]{:S(2)}, u32[]{:S(2)}) collective-permute-start(bf16[128,1024]{1,0:T(8,128)(2,1)S(1)} %enter.5.refs_3_.refs_0_), channel_id=1, source_target_pairs={{0,2},{1,3},{2,0},{3,1},{4,6},{5,7},{6,4},{7,5},{8,10},{9,11},{10,... | collective-permute-start | bytes 786440 | tf_op jit(solution)/shard_map/t10_0/ppermute | solution.py:458
  8.3 1.3 collective-permute-start.3
  10.6 1.5 %collective-permute-start.2 = (bf16[128,1024]{1,0:T(8,128)(2,1)S(1)}, bf16[128,1024]{1,0:T(8,128)(2,1)S(1)}, u32[]{:S(2)}, u32[]{:S(2)}) collective-permute-start(bf16[128,1024]{1,0:T(8,128)(2,1)S(1)} %get-tuple-element.107), channel_id=1, source_target_pairs={{0,4},{4,0},{8,12},{12,8},{16,20},{20,16},{24,28},{28,24},{1,5},{5... | collective-permute-start | bytes 786440 | tf_op jit(solution)/shard_map/t9_1/ppermute | solution.py:458
  12.1 5.9 %collective-permute-done.5.refs_1_ = bf16[128,1024]{1,0:T(8,128)(2,1)S(1)} collective-permute-done((bf16[128,1024]{1,0:T(8,128)(2,1)S(1)}, bf16[128,1024]{1,0:T(8,128)(2,1)S(1)}, u32[]{:S(2)}, u32[]{:S(2)}) %collective-permute-start.5) | collective-permute-done | bytes 262176 | tf_op jit(solution)/shard_map/t9_4/ppermute | solution.py:458
  18.0 1.2 collective-permute-done.4.refs_0_
  19.6 1.6 %collective-permute-start.8 = (bf16[256,1024]{1,0:T(8,128)(2,1)S(1)}, bf16[256,1024]{1,0:T(8,128)(2,1)S(1)}, u32[]{:S(2)}, u32[]{:S(2)}) collective-permute-start(bf16[256,1024]{1,0:T(8,128)(2,1)S(1)} %enter.6.refs_3_.refs_0_), channel_id=1, source_target_pairs={{0,2},{1,3},{2,0},{3,1},{4,6},{5,7},{6,4},{7,5},{8,10},{9,11},{10,... | collective-permute-start | bytes 1572872 | tf_op jit(solution)/shard_map/t10_3/ppermute | solution.py:458
  21.1 7.9 %collective-permute-done.3.refs_1_ = bf16[128,1024]{1,0:T(8,128)(2,1)S(1)} collective-permute-done((bf16[128,1024]{1,0:T(8,128)(2,1)S(1)}, bf16[128,1024]{1,0:T(8,128)(2,1)S(1)}, u32[]{:S(2)}, u32[]{:S(2)}) %collective-permute-start.3) | collective-permute-done | bytes 262176 | tf_op jit(solution)/shard_map/t9_5/ppermute | solution.py:458
  29.3 1.6 %collective-permute-start.7 = (bf16[256,1024]{1,0:T(8,128)(2,1)S(1)}, bf16[256,1024]{1,0:T(8,128)(2,1)S(1)}, u32[]{:S(2)}, u32[]{:S(2)}) collective-permute-start(bf16[256,1024]{1,0:T(8,128)(2,1)S(1)} %enter.7.refs_4_.refs_0_), channel_id=1, source_target_pairs={{0,2},{1,3},{2,0},{3,1},{4,6},{5,7},{6,4},{7,5},{8,10},{9,11},{10,... | collective-permute-start | bytes 1572872 | tf_op jit(solution)/shard_map/t10_2/ppermute | solution.py:458
  30.9 5.7 %collective-permute-start.9 = (bf16[128,1024]{1,0:T(8,128)(2,1)S(1)}, bf16[128,1024]{1,0:T(8,128)(2,1)S(1)}, u32[]{:S(2)}, u32[]{:S(2)}) collective-permute-start(bf16[128,1024]{1,0:T(8,128)(2,1)S(1)} %get-tuple-element.117), channel_id=1, source_target_pairs={{0,12},{4,8},{8,4},{12,0},{16,28},{20,24},{24,20},{28,16},{1,13},{... | collective-permute-start | bytes 786440 | tf_op jit(solution)/shard_map/t9_3/ppermute | solution.py:458
  36.6 5.9 %middle.4 = (f32[256,1024]{1,0:T(8,128)S(1)}, bf16[256,1024]{1,0:T(8,128)(2,1)S(1)}, bf16[256,1024]{1,0:T(8,128)(2,1)S(1)}, bf16[256,1024]{1,0:T(8,128)(2,1)S(1)...) custom-call(bf16[256,1024]{1,0:T(8,128)(2,1)S(1)} %enter.6.refs_3_.r, ...), custom_call_target="tpu_custom_call" | custom-call | tf_op jit(solution)/shard_map/middle/pallas_call | solution.py:198
  43.9 6.1 %middle.5 = (f32[256,1024]{1,0:T(8,128)S(1)}, bf16[256,1024]{1,0:T(8,128)(2,1)S(1)}, bf16[256,1024]{1,0:T(8,128)(2,1)S(1)}, bf16[256,1024]{1,0:T(8,128)(2,1)S(1)...) custom-call(bf16[256,1024]{1,0:T(8,128)(2,1)S(1)} %enter.7.refs_4_.r, ...), custom_call_target="tpu_custom_call" | custom-call | tf_op jit(solution)/shard_map/middle/pallas_call | solution.py:198
  50.3 1.9 %collective-permute-start.10 = (bf16[128,1024]{1,0:T(8,128)(2,1)S(1)}, bf16[128,1024]{1,0:T(8,128)(2,1)S(1)}, u32[]{:S(2)}, u32[]{:S(2)}) collective-permute-start(bf16[128,1024]{1,0:T(8,128)(2,1)S(1)} %enter.8.refs_3_.refs_1_), channel_id=1, source_target_pairs={{0,2},{1,3},{2,0},{3,1},{4,6},{5,7},{6,4},{7,5},{8,10},{9,11},{10,... | collective-permute-start | bytes 786440 | tf_op jit(solution)/shard_map/t10_1/ppermute | solution.py:458
  52.4 4.4 %collective-permute-done.13.refs_1_ = bf16[128,1024]{1,0:T(8,128)(2,1)S(1)} collective-permute-done((bf16[128,1024]{1,0:T(8,128)(2,1)S(1)}, bf16[128,1024]{1,0:T(8,128)(2,1)S(1)}, u32[]{:S(2)}, u32[]{:S(2)}) %collective-permute-start.13) | collective-permute-done | bytes 262176 | tf_op jit(solution)/shard_map/t9_7/ppermute | solution.py:458
  56.8 6.3 %collective-permute-done.10.refs_4_.refs_3_ = bf16[128,1024]{1,0:T(8,128)(2,1)S(1)} collective-permute-done((bf16[128,1024]{1,0:T(8,128)(2,1)S(1)}, bf16[128,1024]{1,0:T(8,128)(2,1)S(1)}, u32[]{:S(2)}, u32[]{:S(2)}) %collective-permute-start.10) | collective-permute-done | bytes 262176 | tf_op jit(solution)/shard_map/t10_1/ppermute | solution.py:458
  64.2 2.3 %collective-permute-start.14 = (bf16[128,1024]{1,0:T(8,128)(2,1)S(1)}, bf16[128,1024]{1,0:T(8,128)(2,1)S(1)}, u32[]{:S(2)}, u32[]{:S(2)}) collective-permute-start(bf16[128,1024]{1,0:T(8,128)(2,1)S(1)} %get-tuple-element.133), channel_id=1, source_target_pairs={{0,16},{4,20},{8,24},{12,28},{16,0},{20,4},{24,8},{28,12},{1,17},{... | collective-permute-start | bytes 786440 | tf_op jit(solution)/shard_map/t12_4/ppermute | solution.py:458
  66.5 1.5 %collective-permute-start.16 = (bf16[256,1024]{1,0:T(8,128)(2,1)S(1)}, bf16[256,1024]{1,0:T(8,128)(2,1)S(1)}, u32[]{:S(2)}, u32[]{:S(2)}) collective-permute-start(bf16[256,1024]{1,0:T(8,128)(2,1)S(1)} %enter.9.refs_5_.refs_0_), channel_id=1, source_target_pairs={{0,2},{1,3},{2,0},{3,1},{4,6},{5,7},{6,4},{7,5},{8,10},{9,11},{10,... | collective-permute-start | bytes 1572872 | tf_op jit(solution)/shard_map/t10_4/ppermute | solution.py:458
  68.0 6.3 %collective-permute-done.11.refs_3_ = bf16[256,1024]{1,0:T(8,128)(2,1)S(1)} collective-permute-done((bf16[256,1024]{1,0:T(8,128)(2,1)S(1)}, bf16[256,1024]{1,0:T(8,128)(2,1)S(1)}, u32[]{:S(2)}, u32[]{:S(2)}) %collective-permute-start.11) | collective-permute-done | bytes 524320 | tf_op jit(solution)/shard_map/t11_1/ppermute | solution.py:458
  75.1 6.0 %middle.6 = (f32[256,1024]{1,0:T(8,128)S(1)}, bf16[256,1024]{1,0:T(8,128)(2,1)S(1)}, bf16[256,1024]{1,0:T(8,128)(2,1)S(1)}, bf16[256,1024]{1,0:T(8,128)(2,1)S(1)...) custom-call(bf16[128,1024]{1,0:T(8,128)(2,1)S(1)} %enter.5.refs_3_.r, ...), custom_call_target="tpu_custom_call" | custom-call | tf_op jit(solution)/shard_map/middle/pallas_call | solution.py:198
  81.7 3.1 %collective-permute-start.17 = (bf16[128,1024]{1,0:T(8,128)(2,1)S(1)}, bf16[128,1024]{1,0:T(8,128)(2,1)S(1)}, u32[]{:S(2)}, u32[]{:S(2)}) collective-permute-start(bf16[128,1024]{1,0:T(8,128)(2,1)S(1)} %get-tuple-element.153), channel_id=1, source_target_pairs={{0,20},{4,16},{8,28},{12,24},{16,4},{20,0},{24,12},{28,8},{1,21},{... | collective-permute-start | bytes 786440 | tf_op jit(solution)/shard_map/t12_5/ppermute | solution.py:458
  85.5 6.2 %middle.7 = (f32[256,1024]{1,0:T(8,128)S(1)}, bf16[256,1024]{1,0:T(8,128)(2,1)S(1)}, bf16[256,1024]{1,0:T(8,128)(2,1)S(1)}, bf16[256,1024]{1,0:T(8,128)(2,1)S(1)...) custom-call(bf16[256,1024]{1,0:T(8,128)(2,1)S(1)} %enter.9.refs_5_.r, ...), custom_call_target="tpu_custom_call" | custom-call | tf_op jit(solution)/shard_map/middle/pallas_call | solution.py:198
  91.7 5.2 %sibling_weights.1.refs_6_ = bf16[2048,1024]{1,0:T(8,128)(2,1)S(1)} custom-call(bf16[256,1024]{1,0:T(8,128)(2,1)S(1)} %get-tuple-element.135.refs_0_, bf16[256,1024]{1,0:T(8,128)(2,1)S(1)} %get-tuple-element.136.refs_1_, bf16[256,1024]{1,0:T(8,128)(2,1)S(1)} %get-tuple-element.137.refs_2_, bf16[256,1024]{1,0:T(8,128)(2,1)S(1)} %get-tuple-element.138.refs_3_, ...), custom_call_target="tpu_custom_call" | custom-call | tf_op jit(solution)/shard_map/sibling_weights/pallas_call | solution.py:198
  97.6 1.3 collective-permute-start.19
  100.2 2.6 %collective-permute-start.23 = (bf16[128,1024]{1,0:T(8,128)(2,1)S(1)}, bf16[128,1024]{1,0:T(8,128)(2,1)S(1)}, u32[]{:S(2)}, u32[]{:S(2)}) collective-permute-start(bf16[128,1024]{1,0:T(8,128)(2,1)S(1)} %get-tuple-element.168), channel_id=1, source_target_pairs={{0,24},{4,28},{8,16},{12,20},{16,8},{20,12},{24,0},{28,4},{1,25},{... | collective-permute-start | bytes 786440 | tf_op jit(solution)/shard_map/t12_6/ppermute | solution.py:458
  102.8 3.9 %collective-permute-done.19.refs_8_.refs_6_ = bf16[128,1024]{1,0:T(8,128)(2,1)S(1)} collective-permute-done((bf16[128,1024]{1,0:T(8,128)(2,1)S(1)}, bf16[128,1024]{1,0:T(8,128)(2,1)S(1)}, u32[]{:S(2)}, u32[]{:S(2)}) %collective-permute-start.19) | collective-permute-done | bytes 262176 | tf_op jit(solution)/shard_map/t12_2/ppermute | solution.py:458
  107.0 4.3 %collective-permute-done.20.refs_3_ = bf16[256,1024]{1,0:T(8,128)(2,1)S(1)} collective-permute-done((bf16[256,1024]{1,0:T(8,128)(2,1)S(1)}, bf16[256,1024]{1,0:T(8,128)(2,1)S(1)}, u32[]{:S(2)}, u32[]{:S(2)}) %collective-permute-start.20) | collective-permute-done | bytes 524320 | tf_op jit(solution)/shard_map/t11_3/ppermute | solution.py:458
  114.4 4.1 %collective-permute-start.22 = (bf16[128,1024]{1,0:T(8,128)(2,1)S(1)}, bf16[128,1024]{1,0:T(8,128)(2,1)S(1)}, u32[]{:S(2)}, u32[]{:S(2)}) collective-permute-start(bf16[128,1024]{1,0:T(8,128)(2,1)S(1)} %get-tuple-element.166), channel_id=1, source_target_pairs={{0,12},{4,8},{8,4},{12,0},{16,28},{20,24},{24,20},{28,16},{1,13},{... | collective-permute-start | bytes 786440 | tf_op jit(solution)/shard_map/t12_3/ppermute | solution.py:458
  119.1 7.6 %own_weights.1 = (f32[1024,1024]{1,0:T(8,128)}, f32[1024,1024]{1,0:T(8,128)}, f32[8,128]{1,0:T(8,128)S(1)}) custom-call(bf16[256,1024]{1,0:T(8,128)(2,1)S(1)} %get-tuple-element.171.refs_0_, bf16[256,1024]{1,0:T(8,128)(2,1)S(1)} %get-tuple-element.172.refs_1_, bf16[256,1024]{1,0:T(8,128)(2,1)S(1)} %get-tuple-element.173.refs_2_, ...), custom_call_target="tpu_custom_call" | custom-call | tf_op jit(solution)/shard_map/own_weights/pallas_call | solution.py:198
  127.3 2.8 %collective-permute-done.24.refs_11_ = bf16[128,1024]{1,0:T(8,128)(2,1)S(1)} collective-permute-done((bf16[128,1024]{1,0:T(8,128)(2,1)S(1)}, bf16[128,1024]{1,0:T(8,128)(2,1)S(1)}, u32[]{:S(2)}, u32[]{:S(2)}) %collective-permute-start.24) | collective-permute-done | bytes 262176 | tf_op jit(solution)/shard_map/t12_7/ppermute | solution.py:458
  130.2 2.9 %collective-permute-done.22.refs_7_ = bf16[128,1024]{1,0:T(8,128)(2,1)S(1)} collective-permute-done((bf16[128,1024]{1,0:T(8,128)(2,1)S(1)}, bf16[128,1024]{1,0:T(8,128)(2,1)S(1)}, u32[]{:S(2)}, u32[]{:S(2)}) %collective-permute-start.22) | collective-permute-done | bytes 262176 | tf_op jit(solution)/shard_map/t12_3/ppermute | solution.py:458
  133.1 1.9 %combine.1 = (bf16[256,1024]{1,0:T(8,128)(2,1)}, f32[256,1024]{1,0:T(8,128)}) custom-call(s32[1]{0:T(128)} %bitcast.refs_0_, s32[1,256]{1,0:T(1,128)S(1)} %get-tuple-element.97.refs_1_, bf16[256,1024]{1,0:T(8,128)(2,1)S(1)} %get-tuple-element.98.refs_2_, bf16[256,1024]{1,0:T(8,128)(2,1)S(1)} %get-tuple-element.99.refs_3_, ...), custom_call_target="tpu_custom_call" | custom-call | tf_op jit(solution)/shard_map/combine/pallas_call | solution.py:198
  (43 shorter events, 13.9 us)
Async XLA Ops:
  3.3 7.3 %collective-permute-start = (bf16[2064,1024]{1,0:T(8,128)(2,1)S(1)}, bf16[2064,1024]{1,0:T(8,128)(2,1)S(1)}, u32[]{:S(2)}, u32[]{:S(2)}) collective-permute-start(bf16[2064,1024]{1,0:T(8,128)(2,1)S(1)} %get-tuple-element.104.refs_2_.refs_4_), channel_id=1, source_target_pairs={{0,1},{1,0},{2,3},{3,2},{4,5},{5,4},{6,7},{7,6},{8,9},{9,8},{10,11... | collective-permute-start | bytes 12681224 | tf_op jit(solution)/shard_map/t13_0/ppermute | solution.py:458
  3.4 14.6 %collective-permute-start.5 = (bf16[128,1024]{1,0:T(8,128)(2,1)S(1)}, bf16[128,1024]{1,0:T(8,128)(2,1)S(1)}, u32[]{:S(2)}, u32[]{:S(2)}) collective-permute-start(bf16[128,1024]{1,0:T(8,128)(2,1)S(1)} %get-tuple-element.113), channel_id=1, source_target_pairs={{0,16},{4,20},{8,24},{12,28},{16,0},{20,4},{24,8},{28,12},{1,17},{... | collective-permute-start | bytes 786440 | tf_op jit(solution)/shard_map/t9_4/ppermute | solution.py:458
  6.1 13.2 %collective-permute-start.4 = (bf16[128,1024]{1,0:T(8,128)(2,1)S(1)}, bf16[128,1024]{1,0:T(8,128)(2,1)S(1)}, u32[]{:S(2)}, u32[]{:S(2)}) collective-permute-start(bf16[128,1024]{1,0:T(8,128)(2,1)S(1)} %get-tuple-element.111), channel_id=1, source_target_pairs={{0,8},{4,12},{8,0},{12,4},{16,24},{20,28},{24,16},{28,20},{1,9},{5... | collective-permute-start | bytes 786440 | tf_op jit(solution)/shard_map/t9_2/ppermute | solution.py:458
  6.8 14.3 %collective-permute-start.6 = (bf16[128,1024]{1,0:T(8,128)(2,1)S(1)}, bf16[128,1024]{1,0:T(8,128)(2,1)S(1)}, u32[]{:S(2)}, u32[]{:S(2)}) collective-permute-start(bf16[128,1024]{1,0:T(8,128)(2,1)S(1)} %enter.5.refs_3_.refs_0_), channel_id=1, source_target_pairs={{0,2},{1,3},{2,0},{3,1},{4,6},{5,7},{6,4},{7,5},{8,10},{9,11},{10,... | collective-permute-start | bytes 786440 | tf_op jit(solution)/shard_map/t10_0/ppermute | solution.py:458
  8.3 20.7 %collective-permute-start.3 = (bf16[128,1024]{1,0:T(8,128)(2,1)S(1)}, bf16[128,1024]{1,0:T(8,128)(2,1)S(1)}, u32[]{:S(2)}, u32[]{:S(2)}) collective-permute-start(bf16[128,1024]{1,0:T(8,128)(2,1)S(1)} %get-tuple-element.109), channel_id=1, source_target_pairs={{0,20},{4,16},{8,28},{12,24},{16,4},{20,0},{24,12},{28,8},{1,21},{... | collective-permute-start | bytes 786440 | tf_op jit(solution)/shard_map/t9_5/ppermute | solution.py:458
  10.6 18.4 %collective-permute-start.2 = (bf16[128,1024]{1,0:T(8,128)(2,1)S(1)}, bf16[128,1024]{1,0:T(8,128)(2,1)S(1)}, u32[]{:S(2)}, u32[]{:S(2)}) collective-permute-start(bf16[128,1024]{1,0:T(8,128)(2,1)S(1)} %get-tuple-element.107), channel_id=1, source_target_pairs={{0,4},{4,0},{8,12},{12,8},{16,20},{20,16},{24,28},{28,24},{1,5},{5... | collective-permute-start | bytes 786440 | tf_op jit(solution)/shard_map/t9_1/ppermute | solution.py:458
  19.6 17.0 %collective-permute-start.8 = (bf16[256,1024]{1,0:T(8,128)(2,1)S(1)}, bf16[256,1024]{1,0:T(8,128)(2,1)S(1)}, u32[]{:S(2)}, u32[]{:S(2)}) collective-permute-start(bf16[256,1024]{1,0:T(8,128)(2,1)S(1)} %enter.6.refs_3_.refs_0_), channel_id=1, source_target_pairs={{0,2},{1,3},{2,0},{3,1},{4,6},{5,7},{6,4},{7,5},{8,10},{9,11},{10,... | collective-permute-start | bytes 1572872 | tf_op jit(solution)/shard_map/t10_3/ppermute | solution.py:458
  29.3 14.6 %collective-permute-start.7 = (bf16[256,1024]{1,0:T(8,128)(2,1)S(1)}, bf16[256,1024]{1,0:T(8,128)(2,1)S(1)}, u32[]{:S(2)}, u32[]{:S(2)}) collective-permute-start(bf16[256,1024]{1,0:T(8,128)(2,1)S(1)} %enter.7.refs_4_.refs_0_), channel_id=1, source_target_pairs={{0,2},{1,3},{2,0},{3,1},{4,6},{5,7},{6,4},{7,5},{8,10},{9,11},{10,... | collective-permute-start | bytes 1572872 | tf_op jit(solution)/shard_map/t10_2/ppermute | solution.py:458
  30.9 19.2 %collective-permute-start.1 = (bf16[128,1024]{1,0:T(8,128)(2,1)S(1)}, bf16[128,1024]{1,0:T(8,128)(2,1)S(1)}, u32[]{:S(2)}, u32[]{:S(2)}) collective-permute-start(bf16[128,1024]{1,0:T(8,128)(2,1)S(1)} %get-tuple-element.105), channel_id=1, source_target_pairs={{0,24},{4,28},{8,16},{12,20},{16,8},{20,12},{24,0},{28,4},{1,25},{... | collective-permute-start | bytes 786440 | tf_op jit(solution)/shard_map/t9_6/ppermute | solution.py:458
  30.9 19.4 %collective-permute-start.9 = (bf16[128,1024]{1,0:T(8,128)(2,1)S(1)}, bf16[128,1024]{1,0:T(8,128)(2,1)S(1)}, u32[]{:S(2)}, u32[]{:S(2)}) collective-permute-start(bf16[128,1024]{1,0:T(8,128)(2,1)S(1)} %get-tuple-element.117), channel_id=1, source_target_pairs={{0,12},{4,8},{8,4},{12,0},{16,28},{20,24},{24,20},{28,16},{1,13},{... | collective-permute-start | bytes 786440 | tf_op jit(solution)/shard_map/t9_3/ppermute | solution.py:458
  42.5 20.8 %collective-permute-start.12 = (bf16[256,1024]{1,0:T(8,128)(2,1)S(1)}, bf16[256,1024]{1,0:T(8,128)(2,1)S(1)}, u32[]{:S(2)}, u32[]{:S(2)}) collective-permute-start(bf16[256,1024]{1,0:T(8,128)(2,1)S(1)} %get-tuple-element.124), channel_id=1, source_target_pairs={{0,2},{1,3},{2,0},{3,1},{4,6},{5,7},{6,4},{7,5},{8,10},{9,11},{10,... | collective-permute-start | bytes 1572872 | tf_op jit(solution)/shard_map/t11_2/ppermute | solution.py:458
  43.1 13.7 %collective-permute-start.13 = (bf16[128,1024]{1,0:T(8,128)(2,1)S(1)}, bf16[128,1024]{1,0:T(8,128)(2,1)S(1)}, u32[]{:S(2)}, u32[]{:S(2)}) collective-permute-start(bf16[128,1024]{1,0:T(8,128)(2,1)S(1)} %get-tuple-element.126), channel_id=1, source_target_pairs={{0,28},{4,24},{8,20},{12,16},{16,12},{20,8},{24,4},{28,0},{1,29},{... | collective-permute-start | bytes 786440 | tf_op jit(solution)/shard_map/t9_7/ppermute | solution.py:458
  50.3 12.8 %collective-permute-start.10 = (bf16[128,1024]{1,0:T(8,128)(2,1)S(1)}, bf16[128,1024]{1,0:T(8,128)(2,1)S(1)}, u32[]{:S(2)}, u32[]{:S(2)}) collective-permute-start(bf16[128,1024]{1,0:T(8,128)(2,1)S(1)} %enter.8.refs_3_.refs_1_), channel_id=1, source_target_pairs={{0,2},{1,3},{2,0},{3,1},{4,6},{5,7},{6,4},{7,5},{8,10},{9,11},{10,... | collective-permute-start | bytes 786440 | tf_op jit(solution)/shard_map/t10_1/ppermute | solution.py:458
  52.2 22.1 %collective-permute-start.11 = (bf16[256,1024]{1,0:T(8,128)(2,1)S(1)}, bf16[256,1024]{1,0:T(8,128)(2,1)S(1)}, u32[]{:S(2)}, u32[]{:S(2)}) collective-permute-start(bf16[256,1024]{1,0:T(8,128)(2,1)S(1)} %get-tuple-element.121), channel_id=1, source_target_pairs={{0,2},{1,3},{2,0},{3,1},{4,6},{5,7},{6,4},{7,5},{8,10},{9,11},{10,... | collective-permute-start | bytes 1572872 | tf_op jit(solution)/shard_map/t11_1/ppermute | solution.py:458
  64.2 16.9 %collective-permute-start.14 = (bf16[128,1024]{1,0:T(8,128)(2,1)S(1)}, bf16[128,1024]{1,0:T(8,128)(2,1)S(1)}, u32[]{:S(2)}, u32[]{:S(2)}) collective-permute-start(bf16[128,1024]{1,0:T(8,128)(2,1)S(1)} %get-tuple-element.133), channel_id=1, source_target_pairs={{0,16},{4,20},{8,24},{12,28},{16,0},{20,4},{24,8},{28,12},{1,17},{... | collective-permute-start | bytes 786440 | tf_op jit(solution)/shard_map/t12_4/ppermute | solution.py:458
  66.5 19.0 %collective-permute-start.16 = (bf16[256,1024]{1,0:T(8,128)(2,1)S(1)}, bf16[256,1024]{1,0:T(8,128)(2,1)S(1)}, u32[]{:S(2)}, u32[]{:S(2)}) collective-permute-start(bf16[256,1024]{1,0:T(8,128)(2,1)S(1)} %enter.9.refs_5_.refs_0_), channel_id=1, source_target_pairs={{0,2},{1,3},{2,0},{3,1},{4,6},{5,7},{6,4},{7,5},{8,10},{9,11},{10,... | collective-permute-start | bytes 1572872 | tf_op jit(solution)/shard_map/t10_4/ppermute | solution.py:458
  81.1 15.8 %collective-permute-start.15 = (bf16[256,1024]{1,0:T(8,128)(2,1)S(1)}, bf16[256,1024]{1,0:T(8,128)(2,1)S(1)}, u32[]{:S(2)}, u32[]{:S(2)}) collective-permute-start(bf16[256,1024]{1,0:T(8,128)(2,1)S(1)} %get-tuple-element.134), channel_id=1, source_target_pairs={{0,2},{1,3},{2,0},{3,1},{4,6},{5,7},{6,4},{7,5},{8,10},{9,11},{10,... | collective-permute-start | bytes 1572872 | tf_op jit(solution)/shard_map/t11_0/ppermute | solution.py:458
  81.7 15.2 %collective-permute-start.17 = (bf16[128,1024]{1,0:T(8,128)(2,1)S(1)}, bf16[128,1024]{1,0:T(8,128)(2,1)S(1)}, u32[]{:S(2)}, u32[]{:S(2)}) collective-permute-start(bf16[128,1024]{1,0:T(8,128)(2,1)S(1)} %get-tuple-element.153), channel_id=1, source_target_pairs={{0,20},{4,16},{8,28},{12,24},{16,4},{20,0},{24,12},{28,8},{1,21},{... | collective-permute-start | bytes 786440 | tf_op jit(solution)/shard_map/t12_5/ppermute | solution.py:458
  96.9 16.5 %collective-permute-start.21 = (bf16[2048,1024]{1,0:T(8,128)(2,1)S(1)}, bf16[2048,1024]{1,0:T(8,128)(2,1)S(1)}, u32[]{:S(2)}, u32[]{:S(2)}) collective-permute-start(bf16[2048,1024]{1,0:T(8,128)(2,1)S(1)} %sibling_weights.1.refs_6_), channel_id=1, source_target_pairs={{0,1},{1,0},{2,3},{3,2},{4,5},{5,4},{6,7},{7,6},{8,9},{9,8},{10,11... | collective-permute-start | bytes 12582920 | tf_op jit(solution)/shard_map/t14_0/ppermute | solution.py:458
  97.0 14.3 %collective-permute-start.20 = (bf16[256,1024]{1,0:T(8,128)(2,1)S(1)}, bf16[256,1024]{1,0:T(8,128)(2,1)S(1)}, u32[]{:S(2)}, u32[]{:S(2)}) collective-permute-start(bf16[256,1024]{1,0:T(8,128)(2,1)S(1)} %get-tuple-element.161), channel_id=1, source_target_pairs={{0,2},{1,3},{2,0},{3,1},{4,6},{5,7},{6,4},{7,5},{8,10},{9,11},{10,... | collective-permute-start | bytes 1572872 | tf_op jit(solution)/shard_map/t11_3/ppermute | solution.py:458
  97.6 9.2 %collective-permute-start.19 = (bf16[128,1024]{1,0:T(8,128)(2,1)S(1)}, bf16[128,1024]{1,0:T(8,128)(2,1)S(1)}, u32[]{:S(2)}, u32[]{:S(2)}) collective-permute-start(bf16[128,1024]{1,0:T(8,128)(2,1)S(1)} %get-tuple-element.158), channel_id=1, source_target_pairs={{0,8},{4,12},{8,0},{12,4},{16,24},{20,28},{24,16},{28,20},{1,9},{5... | collective-permute-start | bytes 786440 | tf_op jit(solution)/shard_map/t12_2/ppermute | solution.py:458
  98.9 8.1 %collective-permute-start.18 = (bf16[128,1024]{1,0:T(8,128)(2,1)S(1)}, bf16[128,1024]{1,0:T(8,128)(2,1)S(1)}, u32[]{:S(2)}, u32[]{:S(2)}) collective-permute-start(bf16[128,1024]{1,0:T(8,128)(2,1)S(1)} %get-tuple-element.156), channel_id=1, source_target_pairs={{0,4},{4,0},{8,12},{12,8},{16,20},{20,16},{24,28},{28,24},{1,5},{5... | collective-permute-start | bytes 786440 | tf_op jit(solution)/shard_map/t12_1/ppermute | solution.py:458
  100.2 18.9 %collective-permute-start.23 = (bf16[128,1024]{1,0:T(8,128)(2,1)S(1)}, bf16[128,1024]{1,0:T(8,128)(2,1)S(1)}, u32[]{:S(2)}, u32[]{:S(2)}) collective-permute-start(bf16[128,1024]{1,0:T(8,128)(2,1)S(1)} %get-tuple-element.168), channel_id=1, source_target_pairs={{0,24},{4,28},{8,16},{12,20},{16,8},{20,12},{24,0},{28,4},{1,25},{... | collective-permute-start | bytes 786440 | tf_op jit(solution)/shard_map/t12_6/ppermute | solution.py:458
  112.2 1.3 collective-permute-start.25
  112.2 17.9 %collective-permute-start.24 = (bf16[128,1024]{1,0:T(8,128)(2,1)S(1)}, bf16[128,1024]{1,0:T(8,128)(2,1)S(1)}, u32[]{:S(2)}, u32[]{:S(2)}) collective-permute-start(bf16[128,1024]{1,0:T(8,128)(2,1)S(1)} %get-tuple-element.170), channel_id=1, source_target_pairs={{0,28},{4,24},{8,20},{12,16},{16,12},{20,8},{24,4},{28,0},{1,29},{... | collective-permute-start | bytes 786440 | tf_op jit(solution)/shard_map/t12_7/ppermute | solution.py:458
  113.4 13.3 %collective-permute-start.26 = (f32[8,1024]{1,0:T(8,128)S(1)}, f32[8,1024]{1,0:T(8,128)S(1)}, u32[]{:S(2)}, u32[]{:S(2)}) collective-permute-start(f32[8,1024]{1,0:T(8,128)S(1)} %add.9), channel_id=1, source_target_pairs={{0,2},{1,3},{2,0},{3,1},{4,6},{5,7},{6,4},{7,5},{8,10},{9,11},{10,... | collective-permute-start | bytes 98312 | tf_op jit(solution)/shard_map/t16_0/ppermute | solution.py:458
  114.4 18.7 %collective-permute-start.22 = (bf16[128,1024]{1,0:T(8,128)(2,1)S(1)}, bf16[128,1024]{1,0:T(8,128)(2,1)S(1)}, u32[]{:S(2)}, u32[]{:S(2)}) collective-permute-start(bf16[128,1024]{1,0:T(8,128)(2,1)S(1)} %get-tuple-element.166), channel_id=1, source_target_pairs={{0,12},{4,8},{8,4},{12,0},{16,28},{20,24},{24,20},{28,16},{1,13},{... | collective-permute-start | bytes 786440 | tf_op jit(solution)/shard_map/t12_3/ppermute | solution.py:458

commit v4 on v3

--- a/solution.py
+++ b/solution.py
@@ -185,7 +185,7 @@
     return pl.BlockSpec(memory_space=pltpu.VMEM)
 
 
-def call(body, outs, args, name, scratch=(), scalars=0, far=0, limit=12 << 20, after=()):
+def call(body, outs, args, name, scratch=(), scalars=0, far=0, limit=12 << 20, after=(), flops=0):
     count, extra = len(args), len(after)
     args = tuple(
         pltpu.with_memory_space_constraint(x, pltpu.HBM) if scalars <= i < scalars + far else x
@@ -205,7 +205,7 @@
         out_specs=tuple(whole() for _ in outs),
         scratch_shapes=list(scratch),
         compiler_params=pltpu.CompilerParams(vmem_limit_bytes=limit),
-        cost_estimate=pl.CostEstimate(flops=0, bytes_accessed=0, transcendentals=0),
+        cost_estimate=pl.CostEstimate(flops=flops, bytes_accessed=0, transcendentals=0),
         name=name,
     )(*args, *after)
 
@@ -441,11 +441,12 @@
 class Order:
     def __init__(self):
         self.fence = []
+        self.flops = 0
 
     def kernel(self, body, outs, args, name, **more):
         mine = {id(x) for x in args}
         after = [x for x in self.fence if id(x) not in mine]
-        got = call(body, outs, args, name, after=after, **more)
+        got = call(body, outs, args, name, after=after, flops=self.flops, **more)
         self.fence = [got[-1]]
         return got
 
@@ -485,23 +486,25 @@
 ) = range(20)
 RUN, SEND, WAIT = range(3)
 
-shares = ((0,), (6,), (1, 5), (2, 4), (3, 7))
+shares = ((0,), (6,), (1, 5), (3, 4), (2, 7))
 chunks = ((0, 1), (2,), (3,), (4,))
+
+work = {(LEAVE, 3): 40}
 
 plan = (
     (RUN, DISPATCH, 0),
     (SEND, ROWS, 4),
+    (SEND, WEIGHTS, 0),
+    (SEND, ROWS, 3),
+    (WAIT, WEIGHTS, 0),
     (SEND, ROWS, 5),
-    (SEND, WEIGHTS, 0),
-    (SEND, ROWS, 2),
     (RUN, ENTER, 0),
     (SEND, SHARE, 0),
-    (WAIT, WEIGHTS, 0),
     (SEND, ROWS, 1),
     (SEND, ROWS, 6),
-    (SEND, ROWS, 3),
+    (SEND, ROWS, 2),
     (WAIT, ROWS, 4),
-    (WAIT, ROWS, 2),
+    (WAIT, ROWS, 3),
     (RUN, ENTER, 3),
     (SEND, SHARE, 3),
     (SEND, ROWS, 7),
@@ -518,18 +521,18 @@
     (SEND, SUMS, 1),
     (WAIT, ROWS, 6),
     (RUN, ENTER, 1),
-    (WAIT, ROWS, 3),
+    (WAIT, ROWS, 2),
     (SEND, SHARE, 1),
-    (WAIT, SHARE, 1),
     (WAIT, ROWS, 7),
     (RUN, ENTER, 4),
     (SEND, SHARE, 4),
     (WAIT, SUMS, 2),
     (RUN, LEAVE, 2),
-    (SEND, REPLY, 2),
+    (SEND, REPLY, 3),
     (SEND, REPLY, 4),
     (WAIT, SUMS, 1),
     (RUN, LEAVE, 1),
+    (WAIT, SHARE, 1),
     (SEND, REPLY, 5),
     (RUN, MIDDLE, 0),
     (SEND, REPLY, 1),
@@ -540,26 +543,26 @@
     (SEND, SUMS, 3),
     (RUN, SIBLING, 0),
     (WAIT, SUMS, 0),
+    (WAIT, REPLY, 3),
     (WAIT, REPLY, 5),
     (SEND, GRADS, 0),
     (RUN, LEAVE, 0),
     (SEND, REPLY, 6),
     (WAIT, REPLY, 1),
-    (WAIT, REPLY, 2),
     (WAIT, SUMS, 3),
     (RUN, LEAVE, 3),
-    (SEND, REPLY, 7),
+    (SEND, REPLY, 2),
     (SEND, TOTAL, 0),
     (WAIT, GRADS, 0),
-    (SEND, REPLY, 3),
     (WAIT, TOTAL, 0),
     (RUN, ADD, 0),
+    (SEND, REPLY, 7),
     (SEND, BOTH, 0),
     (WAIT, REPLY, 6),
     (RUN, OWN, 0),
     (WAIT, REPLY, 7),
     (WAIT, BOTH, 0),
-    (WAIT, REPLY, 3),
+    (WAIT, REPLY, 2),
     (RUN, FINISH, 0),
     (RUN, COMBINE, 0),
 )
@@ -709,6 +712,7 @@
     }
     for kind, what, index in plan:
         if kind == RUN:
+            order.flops = 10**9 * work.get((what, index), 0)
             kernels[what](index)
         elif kind == WAIT:
             order.wait(moved[what, index])

time: 135 us -> 128 us (0.948)
  waiting for transfers between devices: 49 us -> 45 us
  starting transfers between devices: 37.8 us -> 34.5 us
    ppermute x27, waiting for transfers between devices: 49 us -> 45 us  [start(): return lax.ppermute(x, axis, [(i, i ^ offset) for i in range(size)])]
    ppermute x27, starting transfers between devices: 37.8 us -> 34.5 us  [start(): return lax.ppermute(x, axis, [(i, i ^ offset) for i in range(size)])]
  transfers between devices with their start and end apart: 27 -> 27, of which waited for: 15 -> 14; matrix products, arithmetic and copies ran while one was open for 1% -> 1% of each run, Pallas kernels for 31% -> 33%
where the time goes in v4:
time: 128 us
  Pallas kernels  46.1 us (36%)
  waiting for transfers between devices  45 us (35%)
  starting transfers between devices  34.5 us (27%)
    pallas_call x17, Pallas kernels, call(): pl.pallas_call(run, out_shape=tuple(outs), in_specs=[pl.BlockSpec(memory_...  46.1 us
    ppermute x27, waiting for transfers between devices, start(): return lax.ppermute(x, axis, [(i, i ^ offset) for i in range(size)])  45 us
    ppermute x27, starting transfers between devices, start(): return lax.ppermute(x, axis, [(i, i ^ offset) for i in range(size)])  34.5 us
  transfers between devices with their start and end apart: 27, of which 14 were waited for; matrix products, arithmetic and copies ran while one was open for 1% of the time, Pallas kernels for 33%

profile of v4, /device:TPU:8, one launch (start us, length us, event | category | flops | bytes accessed | tf_op | source)
XLA Modules:
  0.0 127.7 jit_solution(6621730343046611770)
XLA Ops:
  0.7 2.7 %dispatch.1 = (bf16[128,1024]{1,0:T(8,128)(2,1)S(1)}, bf16[128,1024]{1,0:T(8,128)(2,1)S(1)}, bf16[128,1024]{1,0:T(8,128)(2,1)S(1)}, bf16[128,1024]{1,0:T(8,128)(...) custom-call(s32[1]{0:T(128)} %bitcast.refs_0_, ...), custom_call_target="tpu_custom_call" | custom-call | tf_op jit(solution)/shard_map/dispatch/pallas_call | solution.py:198
  3.4 2.7 %collective-permute-start.5 = (bf16[128,1024]{1,0:T(8,128)(2,1)S(1)}, bf16[128,1024]{1,0:T(8,128)(2,1)S(1)}, u32[]{:S(2)}, u32[]{:S(2)}) collective-permute-start(bf16[128,1024]{1,0:T(8,128)(2,1)S(1)} %get-tuple-element.113), channel_id=1, source_target_pairs={{0,16},{4,20},{8,24},{12,28},{16,0},{20,4},{24,8},{28,12},{1,17},{... | collective-permute-start | bytes 786440 | tf_op jit(solution)/shard_map/t9_4/ppermute | solution.py:459
  6.1 1.4 %collective-permute-start.4 = (bf16[128,1024]{1,0:T(8,128)(2,1)S(1)}, bf16[128,1024]{1,0:T(8,128)(2,1)S(1)}, u32[]{:S(2)}, u32[]{:S(2)}) collective-permute-start(bf16[128,1024]{1,0:T(8,128)(2,1)S(1)} %get-tuple-element.111), channel_id=1, source_target_pairs={{0,12},{4,8},{8,4},{12,0},{16,28},{20,24},{24,20},{28,16},{1,13},{... | collective-permute-start | bytes 786440 | tf_op jit(solution)/shard_map/t9_3/ppermute | solution.py:459
  7.5 3.1 %collective-permute-done.refs_2_.refs_3_.refs_5_ = bf16[2064,1024]{1,0:T(8,128)(2,1)S(1)} collective-permute-done((bf16[2064,1024]{1,0:T(8,128)(2,1)S(1)}, bf16[2064,1024]{1,0:T(8,128)(2,1)S(1)}, u32[]{:S(2)}, u32[]{:S(2)}) %collective-permute-start) | collective-permute-done | bytes 4227104 | tf_op jit(solution)/shard_map/t13_0/ppermute | solution.py:459
  10.9 1.6 %collective-permute-start.6 = (bf16[128,1024]{1,0:T(8,128)(2,1)S(1)}, bf16[128,1024]{1,0:T(8,128)(2,1)S(1)}, u32[]{:S(2)}, u32[]{:S(2)}) collective-permute-start(bf16[128,1024]{1,0:T(8,128)(2,1)S(1)} %enter.5.refs_3_.refs_0_), channel_id=1, source_target_pairs={{0,2},{1,3},{2,0},{3,1},{4,6},{5,7},{6,4},{7,5},{8,10},{9,11},{10,... | collective-permute-start | bytes 786440 | tf_op jit(solution)/shard_map/t10_0/ppermute | solution.py:459
  12.4 1.5 %collective-permute-start.2 = (bf16[128,1024]{1,0:T(8,128)(2,1)S(1)}, bf16[128,1024]{1,0:T(8,128)(2,1)S(1)}, u32[]{:S(2)}, u32[]{:S(2)}) collective-permute-start(bf16[128,1024]{1,0:T(8,128)(2,1)S(1)} %get-tuple-element.107), channel_id=1, source_target_pairs={{0,4},{4,0},{8,12},{12,8},{16,20},{20,16},{24,28},{28,24},{1,5},{5... | collective-permute-start | bytes 786440 | tf_op jit(solution)/shard_map/t9_1/ppermute | solution.py:459
  13.9 2.5 %collective-permute-start.3 = (bf16[128,1024]{1,0:T(8,128)(2,1)S(1)}, bf16[128,1024]{1,0:T(8,128)(2,1)S(1)}, u32[]{:S(2)}, u32[]{:S(2)}) collective-permute-start(bf16[128,1024]{1,0:T(8,128)(2,1)S(1)} %get-tuple-element.109), channel_id=1, source_target_pairs={{0,20},{4,16},{8,28},{12,24},{16,4},{20,0},{24,12},{28,8},{1,21},{... | collective-permute-start | bytes 786440 | tf_op jit(solution)/shard_map/t9_5/ppermute | solution.py:459
  16.5 1.6 %collective-permute-done.5.refs_1_ = bf16[128,1024]{1,0:T(8,128)(2,1)S(1)} collective-permute-done((bf16[128,1024]{1,0:T(8,128)(2,1)S(1)}, bf16[128,1024]{1,0:T(8,128)(2,1)S(1)}, u32[]{:S(2)}, u32[]{:S(2)}) %collective-permute-start.5) | collective-permute-done | bytes 262176 | tf_op jit(solution)/shard_map/t9_4/ppermute | solution.py:459
  18.1 2.3 %collective-permute-done.4.refs_0_ = bf16[128,1024]{1,0:T(8,128)(2,1)S(1)} collective-permute-done((bf16[128,1024]{1,0:T(8,128)(2,1)S(1)}, bf16[128,1024]{1,0:T(8,128)(2,1)S(1)}, u32[]{:S(2)}, u32[]{:S(2)}) %collective-permute-start.4) | collective-permute-done | bytes 262176 | tf_op jit(solution)/shard_map/t9_3/ppermute | solution.py:459
  20.7 1.6 %collective-permute-start.8 = (bf16[256,1024]{1,0:T(8,128)(2,1)S(1)}, bf16[256,1024]{1,0:T(8,128)(2,1)S(1)}, u32[]{:S(2)}, u32[]{:S(2)}) collective-permute-start(bf16[256,1024]{1,0:T(8,128)(2,1)S(1)} %enter.6.refs_3_.refs_0_), channel_id=1, source_target_pairs={{0,2},{1,3},{2,0},{3,1},{4,6},{5,7},{6,4},{7,5},{8,10},{9,11},{10,... | collective-permute-start | bytes 1572872 | tf_op jit(solution)/shard_map/t10_3/ppermute | solution.py:459
  22.2 8.8 %collective-permute-done.2.refs_0_ = bf16[128,1024]{1,0:T(8,128)(2,1)S(1)} collective-permute-done((bf16[128,1024]{1,0:T(8,128)(2,1)S(1)}, bf16[128,1024]{1,0:T(8,128)(2,1)S(1)}, u32[]{:S(2)}, u32[]{:S(2)}) %collective-permute-start.2) | collective-permute-done | bytes 262176 | tf_op jit(solution)/shard_map/t9_1/ppermute | solution.py:459
  31.3 1.2 collective-permute-start.7
  33.7 5.9 %middle.4 = (f32[256,1024]{1,0:T(8,128)S(1)}, bf16[256,1024]{1,0:T(8,128)(2,1)S(1)}, bf16[256,1024]{1,0:T(8,128)(2,1)S(1)}, bf16[256,1024]{1,0:T(8,128)(2,1)S(1)...) custom-call(bf16[256,1024]{1,0:T(8,128)(2,1)S(1)} %enter.6.refs_3_.r, ...), custom_call_target="tpu_custom_call" | custom-call | tf_op jit(solution)/shard_map/middle/pallas_call | solution.py:198
  39.6 1.9 %collective-permute-start.12 = (bf16[256,1024]{1,0:T(8,128)(2,1)S(1)}, bf16[256,1024]{1,0:T(8,128)(2,1)S(1)}, u32[]{:S(2)}, u32[]{:S(2)}) collective-permute-start(bf16[256,1024]{1,0:T(8,128)(2,1)S(1)} %get-tuple-element.124), channel_id=1, source_target_pairs={{0,2},{1,3},{2,0},{3,1},{4,6},{5,7},{6,4},{7,5},{8,10},{9,11},{10,... | collective-permute-start | bytes 1572872 | tf_op jit(solution)/shard_map/t11_2/ppermute | solution.py:459
  41.6 3.1 %collective-permute-start.9 = (bf16[128,1024]{1,0:T(8,128)(2,1)S(1)}, bf16[128,1024]{1,0:T(8,128)(2,1)S(1)}, u32[]{:S(2)}, u32[]{:S(2)}) collective-permute-start(bf16[128,1024]{1,0:T(8,128)(2,1)S(1)} %get-tuple-element.117), channel_id=1, source_target_pairs={{0,8},{4,12},{8,0},{12,4},{16,24},{20,28},{24,16},{28,20},{1,9},{5... | collective-permute-start | bytes 786440 | tf_op jit(solution)/shard_map/t9_2/ppermute | solution.py:459
  44.7 3.3 %collective-permute-start.13 = (bf16[128,1024]{1,0:T(8,128)(2,1)S(1)}, bf16[128,1024]{1,0:T(8,128)(2,1)S(1)}, u32[]{:S(2)}, u32[]{:S(2)}) collective-permute-start(bf16[128,1024]{1,0:T(8,128)(2,1)S(1)} %get-tuple-element.126), channel_id=1, source_target_pairs={{0,28},{4,24},{8,20},{12,16},{16,12},{20,8},{24,4},{28,0},{1,29},{... | collective-permute-start | bytes 786440 | tf_op jit(solution)/shard_map/t9_7/ppermute | solution.py:459
  48.1 6.1 %middle.5 = (f32[256,1024]{1,0:T(8,128)S(1)}, bf16[256,1024]{1,0:T(8,128)(2,1)S(1)}, bf16[256,1024]{1,0:T(8,128)(2,1)S(1)}, bf16[256,1024]{1,0:T(8,128)(2,1)S(1)...) custom-call(bf16[256,1024]{1,0:T(8,128)(2,1)S(1)} %enter.7.refs_4_.r, ...), custom_call_target="tpu_custom_call" | custom-call | tf_op jit(solution)/shard_map/middle/pallas_call | solution.py:198
  54.9 5.0 %collective-permute-done.1.refs_0_.refs_1_ = bf16[128,1024]{1,0:T(8,128)(2,1)S(1)} collective-permute-done((bf16[128,1024]{1,0:T(8,128)(2,1)S(1)}, bf16[128,1024]{1,0:T(8,128)(2,1)S(1)}, u32[]{:S(2)}, u32[]{:S(2)}) %collective-permute-start.1) | collective-permute-done | bytes 262176 | tf_op jit(solution)/shard_map/t9_6/ppermute | solution.py:459
  60.9 3.5 %collective-permute-done.13.refs_1_ = bf16[128,1024]{1,0:T(8,128)(2,1)S(1)} collective-permute-done((bf16[128,1024]{1,0:T(8,128)(2,1)S(1)}, bf16[128,1024]{1,0:T(8,128)(2,1)S(1)}, u32[]{:S(2)}, u32[]{:S(2)}) %collective-permute-start.13) | collective-permute-done | bytes 262176 | tf_op jit(solution)/shard_map/t9_7/ppermute | solution.py:459
  66.6 2.5 %collective-permute-done.11.refs_3_ = bf16[256,1024]{1,0:T(8,128)(2,1)S(1)} collective-permute-done((bf16[256,1024]{1,0:T(8,128)(2,1)S(1)}, bf16[256,1024]{1,0:T(8,128)(2,1)S(1)}, u32[]{:S(2)}, u32[]{:S(2)}) %collective-permute-start.11) | collective-permute-done | bytes 524320 | tf_op jit(solution)/shard_map/t11_1/ppermute | solution.py:459
  70.0 4.8 %collective-permute-done.10.refs_3_ = bf16[128,1024]{1,0:T(8,128)(2,1)S(1)} collective-permute-done((bf16[128,1024]{1,0:T(8,128)(2,1)S(1)}, bf16[128,1024]{1,0:T(8,128)(2,1)S(1)}, u32[]{:S(2)}, u32[]{:S(2)}) %collective-permute-start.10) | collective-permute-done | bytes 262176 | tf_op jit(solution)/shard_map/t10_1/ppermute | solution.py:459
  74.8 5.9 %middle.6 = (f32[256,1024]{1,0:T(8,128)S(1)}, bf16[256,1024]{1,0:T(8,128)(2,1)S(1)}, bf16[256,1024]{1,0:T(8,128)(2,1)S(1)}, bf16[256,1024]{1,0:T(8,128)(2,1)S(1)...) custom-call(bf16[128,1024]{1,0:T(8,128)(2,1)S(1)} %enter.5.refs_3_.r, ...), custom_call_target="tpu_custom_call" | custom-call | tf_op jit(solution)/shard_map/middle/pallas_call | solution.py:198
  81.5 3.0 %collective-permute-start.17 = (bf16[128,1024]{1,0:T(8,128)(2,1)S(1)}, bf16[128,1024]{1,0:T(8,128)(2,1)S(1)}, u32[]{:S(2)}, u32[]{:S(2)}) collective-permute-start(bf16[128,1024]{1,0:T(8,128)(2,1)S(1)} %get-tuple-element.153), channel_id=1, source_target_pairs={{0,12},{4,8},{8,4},{12,0},{16,28},{20,24},{24,20},{28,16},{1,13},{... | collective-permute-start | bytes 786440 | tf_op jit(solution)/shard_map/t12_3/ppermute | solution.py:459
  84.6 1.4 %collective-permute-done.16.refs_1_ = bf16[256,1024]{1,0:T(8,128)(2,1)S(1)} collective-permute-done((bf16[256,1024]{1,0:T(8,128)(2,1)S(1)}, bf16[256,1024]{1,0:T(8,128)(2,1)S(1)}, u32[]{:S(2)}, u32[]{:S(2)}) %collective-permute-start.16) | collective-permute-done | bytes 524320 | tf_op jit(solution)/shard_map/t10_4/ppermute | solution.py:459
  86.0 6.2 %middle.7 = (f32[256,1024]{1,0:T(8,128)S(1)}, bf16[256,1024]{1,0:T(8,128)(2,1)S(1)}, bf16[256,1024]{1,0:T(8,128)(2,1)S(1)}, bf16[256,1024]{1,0:T(8,128)(2,1)S(1)...) custom-call(bf16[256,1024]{1,0:T(8,128)(2,1)S(1)} %enter.9.refs_5_.r, ...), custom_call_target="tpu_custom_call" | custom-call | tf_op jit(solution)/shard_map/middle/pallas_call | solution.py:198
  92.9 5.2 %sibling_weights.1.refs_6_ = bf16[2048,1024]{1,0:T(8,128)(2,1)S(1)} custom-call(bf16[256,1024]{1,0:T(8,128)(2,1)S(1)} %get-tuple-element.135.refs_0_, bf16[256,1024]{1,0:T(8,128)(2,1)S(1)} %get-tuple-element.136.refs_1_, bf16[256,1024]{1,0:T(8,128)(2,1)S(1)} %get-tuple-element.137.refs_2_, bf16[256,1024]{1,0:T(8,128)(2,1)S(1)} %get-tuple-element.138.refs_3_, ...), custom_call_target="tpu_custom_call" | custom-call | tf_op jit(solution)/shard_map/sibling_weights/pallas_call | solution.py:198
  100.4 6.5 %collective-permute-done.19.refs_7_.refs_5_ = bf16[128,1024]{1,0:T(8,128)(2,1)S(1)} collective-permute-done((bf16[128,1024]{1,0:T(8,128)(2,1)S(1)}, bf16[128,1024]{1,0:T(8,128)(2,1)S(1)}, u32[]{:S(2)}, u32[]{:S(2)}) %collective-permute-start.19) | collective-permute-done | bytes 262176 | tf_op jit(solution)/shard_map/t12_1/ppermute | solution.py:459
  107.9 1.8 %collective-permute-start.21 = (bf16[128,1024]{1,0:T(8,128)(2,1)S(1)}, bf16[128,1024]{1,0:T(8,128)(2,1)S(1)}, u32[]{:S(2)}, u32[]{:S(2)}) collective-permute-start(bf16[128,1024]{1,0:T(8,128)(2,1)S(1)} %get-tuple-element.165), channel_id=1, source_target_pairs={{0,8},{4,12},{8,0},{12,4},{16,24},{20,28},{24,16},{28,20},{1,9},{5... | collective-permute-start | bytes 786440 | tf_op jit(solution)/shard_map/t12_2/ppermute | solution.py:459
  110.5 2.3 %collective-permute-start.25 = (bf16[128,1024]{1,0:T(8,128)(2,1)S(1)}, bf16[128,1024]{1,0:T(8,128)(2,1)S(1)}, u32[]{:S(2)}, u32[]{:S(2)}) collective-permute-start(bf16[128,1024]{1,0:T(8,128)(2,1)S(1)} %get-tuple-element.170), channel_id=1, source_target_pairs={{0,28},{4,24},{8,20},{12,16},{16,12},{20,8},{24,4},{28,0},{1,29},{... | collective-permute-start | bytes 786440 | tf_op jit(solution)/shard_map/t12_7/ppermute | solution.py:459
  114.0 7.6 %own_weights.1 = (f32[1024,1024]{1,0:T(8,128)}, f32[1024,1024]{1,0:T(8,128)}, f32[8,128]{1,0:T(8,128)S(1)}) custom-call(bf16[256,1024]{1,0:T(8,128)(2,1)S(1)} %get-tuple-element.171.refs_0_, bf16[256,1024]{1,0:T(8,128)(2,1)S(1)} %get-tuple-element.172.refs_1_, bf16[256,1024]{1,0:T(8,128)(2,1)S(1)} %get-tuple-element.173.refs_2_, ...), custom_call_target="tpu_custom_call" | custom-call | tf_op jit(solution)/shard_map/own_weights/pallas_call | solution.py:198
  122.2 3.7 %collective-permute-done.25.refs_11_ = bf16[128,1024]{1,0:T(8,128)(2,1)S(1)} collective-permute-done((bf16[128,1024]{1,0:T(8,128)(2,1)S(1)}, bf16[128,1024]{1,0:T(8,128)(2,1)S(1)}, u32[]{:S(2)}, u32[]{:S(2)}) %collective-permute-start.25) | collective-permute-done | bytes 262176 | tf_op jit(solution)/shard_map/t12_7/ppermute | solution.py:459
  125.9 1.9 %combine.1 = (bf16[256,1024]{1,0:T(8,128)(2,1)}, f32[256,1024]{1,0:T(8,128)}) custom-call(s32[1]{0:T(128)} %bitcast.refs_0_, s32[1,256]{1,0:T(1,128)S(1)} %get-tuple-element.97.refs_1_, bf16[256,1024]{1,0:T(8,128)(2,1)S(1)} %get-tuple-element.98.refs_2_, bf16[256,1024]{1,0:T(8,128)(2,1)S(1)} %get-tuple-element.99.refs_3_, ...), custom_call_target="tpu_custom_call" | custom-call | tf_op jit(solution)/shard_map/combine/pallas_call | solution.py:198
  (43 shorter events, 14.2 us)
Async XLA Ops:
  3.3 7.3 %collective-permute-start = (bf16[2064,1024]{1,0:T(8,128)(2,1)S(1)}, bf16[2064,1024]{1,0:T(8,128)(2,1)S(1)}, u32[]{:S(2)}, u32[]{:S(2)}) collective-permute-start(bf16[2064,1024]{1,0:T(8,128)(2,1)S(1)} %get-tuple-element.104.refs_2_.refs_4_), channel_id=1, source_target_pairs={{0,1},{1,0},{2,3},{3,2},{4,5},{5,4},{6,7},{7,6},{8,9},{9,8},{10,11... | collective-permute-start | bytes 12681224 | tf_op jit(solution)/shard_map/t13_0/ppermute | solution.py:459
  3.4 14.6 %collective-permute-start.5 = (bf16[128,1024]{1,0:T(8,128)(2,1)S(1)}, bf16[128,1024]{1,0:T(8,128)(2,1)S(1)}, u32[]{:S(2)}, u32[]{:S(2)}) collective-permute-start(bf16[128,1024]{1,0:T(8,128)(2,1)S(1)} %get-tuple-element.113), channel_id=1, source_target_pairs={{0,16},{4,20},{8,24},{12,28},{16,0},{20,4},{24,8},{28,12},{1,17},{... | collective-permute-start | bytes 786440 | tf_op jit(solution)/shard_map/t9_4/ppermute | solution.py:459
  6.1 14.3 %collective-permute-start.4 = (bf16[128,1024]{1,0:T(8,128)(2,1)S(1)}, bf16[128,1024]{1,0:T(8,128)(2,1)S(1)}, u32[]{:S(2)}, u32[]{:S(2)}) collective-permute-start(bf16[128,1024]{1,0:T(8,128)(2,1)S(1)} %get-tuple-element.111), channel_id=1, source_target_pairs={{0,12},{4,8},{8,4},{12,0},{16,28},{20,24},{24,20},{28,16},{1,13},{... | collective-permute-start | bytes 786440 | tf_op jit(solution)/shard_map/t9_3/ppermute | solution.py:459
  10.9 20.2 %collective-permute-start.6 = (bf16[128,1024]{1,0:T(8,128)(2,1)S(1)}, bf16[128,1024]{1,0:T(8,128)(2,1)S(1)}, u32[]{:S(2)}, u32[]{:S(2)}) collective-permute-start(bf16[128,1024]{1,0:T(8,128)(2,1)S(1)} %enter.5.refs_3_.refs_0_), channel_id=1, source_target_pairs={{0,2},{1,3},{2,0},{3,1},{4,6},{5,7},{6,4},{7,5},{8,10},{9,11},{10,... | collective-permute-start | bytes 786440 | tf_op jit(solution)/shard_map/t10_0/ppermute | solution.py:459
  12.4 18.6 %collective-permute-start.2 = (bf16[128,1024]{1,0:T(8,128)(2,1)S(1)}, bf16[128,1024]{1,0:T(8,128)(2,1)S(1)}, u32[]{:S(2)}, u32[]{:S(2)}) collective-permute-start(bf16[128,1024]{1,0:T(8,128)(2,1)S(1)} %get-tuple-element.107), channel_id=1, source_target_pairs={{0,4},{4,0},{8,12},{12,8},{16,20},{20,16},{24,28},{28,24},{1,5},{5... | collective-permute-start | bytes 786440 | tf_op jit(solution)/shard_map/t9_1/ppermute | solution.py:459
  13.9 17.1 %collective-permute-start.3 = (bf16[128,1024]{1,0:T(8,128)(2,1)S(1)}, bf16[128,1024]{1,0:T(8,128)(2,1)S(1)}, u32[]{:S(2)}, u32[]{:S(2)}) collective-permute-start(bf16[128,1024]{1,0:T(8,128)(2,1)S(1)} %get-tuple-element.109), channel_id=1, source_target_pairs={{0,20},{4,16},{8,28},{12,24},{16,4},{20,0},{24,12},{28,8},{1,21},{... | collective-permute-start | bytes 786440 | tf_op jit(solution)/shard_map/t9_5/ppermute | solution.py:459
  20.7 13.0 %collective-permute-start.8 = (bf16[256,1024]{1,0:T(8,128)(2,1)S(1)}, bf16[256,1024]{1,0:T(8,128)(2,1)S(1)}, u32[]{:S(2)}, u32[]{:S(2)}) collective-permute-start(bf16[256,1024]{1,0:T(8,128)(2,1)S(1)} %enter.6.refs_3_.refs_0_), channel_id=1, source_target_pairs={{0,2},{1,3},{2,0},{3,1},{4,6},{5,7},{6,4},{7,5},{8,10},{9,11},{10,... | collective-permute-start | bytes 1572872 | tf_op jit(solution)/shard_map/t10_3/ppermute | solution.py:459
  31.3 16.8 %collective-permute-start.7 = (bf16[256,1024]{1,0:T(8,128)(2,1)S(1)}, bf16[256,1024]{1,0:T(8,128)(2,1)S(1)}, u32[]{:S(2)}, u32[]{:S(2)}) collective-permute-start(bf16[256,1024]{1,0:T(8,128)(2,1)S(1)} %enter.7.refs_4_.refs_0_), channel_id=1, source_target_pairs={{0,2},{1,3},{2,0},{3,1},{4,6},{5,7},{6,4},{7,5},{8,10},{9,11},{10,... | collective-permute-start | bytes 1572872 | tf_op jit(solution)/shard_map/t10_2/ppermute | solution.py:459
  39.6 25.1 %collective-permute-start.12 = (bf16[256,1024]{1,0:T(8,128)(2,1)S(1)}, bf16[256,1024]{1,0:T(8,128)(2,1)S(1)}, u32[]{:S(2)}, u32[]{:S(2)}) collective-permute-start(bf16[256,1024]{1,0:T(8,128)(2,1)S(1)} %get-tuple-element.124), channel_id=1, source_target_pairs={{0,2},{1,3},{2,0},{3,1},{4,6},{5,7},{6,4},{7,5},{8,10},{9,11},{10,... | collective-permute-start | bytes 1572872 | tf_op jit(solution)/shard_map/t11_2/ppermute | solution.py:459
  41.5 18.4 %collective-permute-start.1 = (bf16[128,1024]{1,0:T(8,128)(2,1)S(1)}, bf16[128,1024]{1,0:T(8,128)(2,1)S(1)}, u32[]{:S(2)}, u32[]{:S(2)}) collective-permute-start(bf16[128,1024]{1,0:T(8,128)(2,1)S(1)} %get-tuple-element.105), channel_id=1, source_target_pairs={{0,24},{4,28},{8,16},{12,20},{16,8},{20,12},{24,0},{28,4},{1,25},{... | collective-permute-start | bytes 786440 | tf_op jit(solution)/shard_map/t9_6/ppermute | solution.py:459
  41.6 18.6 %collective-permute-start.9 = (bf16[128,1024]{1,0:T(8,128)(2,1)S(1)}, bf16[128,1024]{1,0:T(8,128)(2,1)S(1)}, u32[]{:S(2)}, u32[]{:S(2)}) collective-permute-start(bf16[128,1024]{1,0:T(8,128)(2,1)S(1)} %get-tuple-element.117), channel_id=1, source_target_pairs={{0,8},{4,12},{8,0},{12,4},{16,24},{20,28},{24,16},{28,20},{1,9},{5... | collective-permute-start | bytes 786440 | tf_op jit(solution)/shard_map/t9_2/ppermute | solution.py:459
  44.7 19.6 %collective-permute-start.13 = (bf16[128,1024]{1,0:T(8,128)(2,1)S(1)}, bf16[128,1024]{1,0:T(8,128)(2,1)S(1)}, u32[]{:S(2)}, u32[]{:S(2)}) collective-permute-start(bf16[128,1024]{1,0:T(8,128)(2,1)S(1)} %get-tuple-element.126), channel_id=1, source_target_pairs={{0,28},{4,24},{8,20},{12,16},{16,12},{20,8},{24,4},{28,0},{1,29},{... | collective-permute-start | bytes 786440 | tf_op jit(solution)/shard_map/t9_7/ppermute | solution.py:459
  54.2 14.9 %collective-permute-start.11 = (bf16[256,1024]{1,0:T(8,128)(2,1)S(1)}, bf16[256,1024]{1,0:T(8,128)(2,1)S(1)}, u32[]{:S(2)}, u32[]{:S(2)}) collective-permute-start(bf16[256,1024]{1,0:T(8,128)(2,1)S(1)} %get-tuple-element.121), channel_id=1, source_target_pairs={{0,2},{1,3},{2,0},{3,1},{4,6},{5,7},{6,4},{7,5},{8,10},{9,11},{10,... | collective-permute-start | bytes 1572872 | tf_op jit(solution)/shard_map/t11_1/ppermute | solution.py:459
  60.2 14.6 %collective-permute-start.10 = (bf16[128,1024]{1,0:T(8,128)(2,1)S(1)}, bf16[128,1024]{1,0:T(8,128)(2,1)S(1)}, u32[]{:S(2)}, u32[]{:S(2)}) collective-permute-start(bf16[128,1024]{1,0:T(8,128)(2,1)S(1)} %enter.8.refs_3_.refs_1_), channel_id=1, source_target_pairs={{0,2},{1,3},{2,0},{3,1},{4,6},{5,7},{6,4},{7,5},{8,10},{9,11},{10,... | collective-permute-start | bytes 786440 | tf_op jit(solution)/shard_map/t10_1/ppermute | solution.py:459
  65.5 15.2 %collective-permute-start.14 = (bf16[128,1024]{1,0:T(8,128)(2,1)S(1)}, bf16[128,1024]{1,0:T(8,128)(2,1)S(1)}, u32[]{:S(2)}, u32[]{:S(2)}) collective-permute-start(bf16[128,1024]{1,0:T(8,128)(2,1)S(1)} %get-tuple-element.133), channel_id=1, source_target_pairs={{0,16},{4,20},{8,24},{12,28},{16,0},{20,4},{24,8},{28,12},{1,17},{... | collective-permute-start | bytes 786440 | tf_op jit(solution)/shard_map/t12_4/ppermute | solution.py:459
  65.6 20.4 %collective-permute-start.16 = (bf16[256,1024]{1,0:T(8,128)(2,1)S(1)}, bf16[256,1024]{1,0:T(8,128)(2,1)S(1)}, u32[]{:S(2)}, u32[]{:S(2)}) collective-permute-start(bf16[256,1024]{1,0:T(8,128)(2,1)S(1)} %enter.9.refs_5_.refs_0_), channel_id=1, source_target_pairs={{0,2},{1,3},{2,0},{3,1},{4,6},{5,7},{6,4},{7,5},{8,10},{9,11},{10,... | collective-permute-start | bytes 1572872 | tf_op jit(solution)/shard_map/t10_4/ppermute | solution.py:459
  80.7 17.4 %collective-permute-start.15 = (bf16[256,1024]{1,0:T(8,128)(2,1)S(1)}, bf16[256,1024]{1,0:T(8,128)(2,1)S(1)}, u32[]{:S(2)}, u32[]{:S(2)}) collective-permute-start(bf16[256,1024]{1,0:T(8,128)(2,1)S(1)} %get-tuple-element.134), channel_id=1, source_target_pairs={{0,2},{1,3},{2,0},{3,1},{4,6},{5,7},{6,4},{7,5},{8,10},{9,11},{10,... | collective-permute-start | bytes 1572872 | tf_op jit(solution)/shard_map/t11_0/ppermute | solution.py:459
  81.5 16.6 %collective-permute-start.17 = (bf16[128,1024]{1,0:T(8,128)(2,1)S(1)}, bf16[128,1024]{1,0:T(8,128)(2,1)S(1)}, u32[]{:S(2)}, u32[]{:S(2)}) collective-permute-start(bf16[128,1024]{1,0:T(8,128)(2,1)S(1)} %get-tuple-element.153), channel_id=1, source_target_pairs={{0,12},{4,8},{8,4},{12,0},{16,28},{20,24},{24,20},{28,16},{1,13},{... | collective-permute-start | bytes 786440 | tf_op jit(solution)/shard_map/t12_3/ppermute | solution.py:459
  84.5 13.6 %collective-permute-start.18 = (bf16[128,1024]{1,0:T(8,128)(2,1)S(1)}, bf16[128,1024]{1,0:T(8,128)(2,1)S(1)}, u32[]{:S(2)}, u32[]{:S(2)}) collective-permute-start(bf16[128,1024]{1,0:T(8,128)(2,1)S(1)} %get-tuple-element.155), channel_id=1, source_target_pairs={{0,20},{4,16},{8,28},{12,24},{16,4},{20,0},{24,12},{28,8},{1,21},{... | collective-permute-start | bytes 786440 | tf_op jit(solution)/shard_map/t12_5/ppermute | solution.py:459
  92.2 14.8 %collective-permute-start.20 = (bf16[256,1024]{1,0:T(8,128)(2,1)S(1)}, bf16[256,1024]{1,0:T(8,128)(2,1)S(1)}, u32[]{:S(2)}, u32[]{:S(2)}) collective-permute-start(bf16[256,1024]{1,0:T(8,128)(2,1)S(1)} %get-tuple-element.161), channel_id=1, source_target_pairs={{0,2},{1,3},{2,0},{3,1},{4,6},{5,7},{6,4},{7,5},{8,10},{9,11},{10,... | collective-permute-start | bytes 1572872 | tf_op jit(solution)/shard_map/t11_3/ppermute | solution.py:459
  98.1 11.7 %collective-permute-start.23 = (bf16[2048,1024]{1,0:T(8,128)(2,1)S(1)}, bf16[2048,1024]{1,0:T(8,128)(2,1)S(1)}, u32[]{:S(2)}, u32[]{:S(2)}) collective-permute-start(bf16[2048,1024]{1,0:T(8,128)(2,1)S(1)} %sibling_weights.1.refs_6_), channel_id=1, source_target_pairs={{0,1},{1,0},{2,3},{3,2},{4,5},{5,4},{6,7},{7,6},{8,9},{9,8},{10,11... | collective-permute-start | bytes 12582920 | tf_op jit(solution)/shard_map/t14_0/ppermute | solution.py:459
  98.2 8.7 %collective-permute-start.19 = (bf16[128,1024]{1,0:T(8,128)(2,1)S(1)}, bf16[128,1024]{1,0:T(8,128)(2,1)S(1)}, u32[]{:S(2)}, u32[]{:S(2)}) collective-permute-start(bf16[128,1024]{1,0:T(8,128)(2,1)S(1)} %get-tuple-element.158), channel_id=1, source_target_pairs={{0,4},{4,0},{8,12},{12,8},{16,20},{20,16},{24,28},{28,24},{1,5},{5... | collective-permute-start | bytes 786440 | tf_op jit(solution)/shard_map/t12_1/ppermute | solution.py:459
  99.9 14.1 %collective-permute-start.22 = (bf16[128,1024]{1,0:T(8,128)(2,1)S(1)}, bf16[128,1024]{1,0:T(8,128)(2,1)S(1)}, u32[]{:S(2)}, u32[]{:S(2)}) collective-permute-start(bf16[128,1024]{1,0:T(8,128)(2,1)S(1)} %get-tuple-element.167), channel_id=1, source_target_pairs={{0,24},{4,28},{8,16},{12,20},{16,8},{20,12},{24,0},{28,4},{1,25},{... | collective-permute-start | bytes 786440 | tf_op jit(solution)/shard_map/t12_6/ppermute | solution.py:459
  107.9 1.9 %collective-permute-start.24 = (f32[8,1024]{1,0:T(8,128)S(1)}, f32[8,1024]{1,0:T(8,128)S(1)}, u32[]{:S(2)}, u32[]{:S(2)}) collective-permute-start(f32[8,1024]{1,0:T(8,128)S(1)} %get-tuple-element.164.refs_17_), channel_id=1, source_target_pairs={{0,1},{1,0},{2,3},{3,2},{4,5},{5,4},{6,7},{7,6},{8,9},{9,8},{10,11... | collective-permute-start | bytes 98312 | tf_op jit(solution)/shard_map/t15_0/ppermute | solution.py:459
  107.9 14.3 %collective-permute-start.21 = (bf16[128,1024]{1,0:T(8,128)(2,1)S(1)}, bf16[128,1024]{1,0:T(8,128)(2,1)S(1)}, u32[]{:S(2)}, u32[]{:S(2)}) collective-permute-start(bf16[128,1024]{1,0:T(8,128)(2,1)S(1)} %get-tuple-element.165), channel_id=1, source_target_pairs={{0,8},{4,12},{8,0},{12,4},{16,24},{20,28},{24,16},{28,20},{1,9},{5... | collective-permute-start | bytes 786440 | tf_op jit(solution)/shard_map/t12_2/ppermute | solution.py:459
  109.8 11.8 %collective-permute-start.26 = (f32[8,1024]{1,0:T(8,128)S(1)}, f32[8,1024]{1,0:T(8,128)S(1)}, u32[]{:S(2)}, u32[]{:S(2)}) collective-permute-start(f32[8,1024]{1,0:T(8,128)S(1)} %add.9), channel_id=1, source_target_pairs={{0,2},{1,3},{2,0},{3,1},{4,6},{5,7},{6,4},{7,5},{8,10},{9,11},{10,... | collective-permute-start | bytes 98312 | tf_op jit(solution)/shard_map/t16_0/ppermute | solution.py:459
  110.5 15.4 %collective-permute-start.25 = (bf16[128,1024]{1,0:T(8,128)(2,1)S(1)}, bf16[128,1024]{1,0:T(8,128)(2,1)S(1)}, u32[]{:S(2)}, u32[]{:S(2)}) collective-permute-start(bf16[128,1024]{1,0:T(8,128)(2,1)S(1)} %get-tuple-element.170), channel_id=1, source_target_pairs={{0,28},{4,24},{8,20},{12,16},{16,12},{20,8},{24,4},{28,0},{1,29},{... | collective-permute-start | bytes 786440 | tf_op jit(solution)/shard_map/t12_7/ppermute | solution.py:459
